TPU v7x, 32 devices: a whole 2x2x4 slice. The times are simulated.
32 devices in a mesh: dp: 8 (over y, x, core), fsdp: 4 (over z).
Axes of the slice: x: 2, y: 2, z: 4, core: 2. Of those that a mesh axis runs over, the one named last changes fastest.
Arguments:
- tokens_in: bfloat16 [32, 512, 1536], P(('dp', 'fsdp')), may hold values from -6 to 6
- condition: bfloat16 [32, 2, 1536], P(('dp', 'fsdp')), may hold values from -6 to 6
- item_flags: int32 [32, 512], P(('dp', 'fsdp')), may hold values from 0 to 1, as said below
- grad_out: bfloat16 [32, 512, 1536], P(('dp', 'fsdp')), may hold values from -6 to 6
- in_weight: bfloat16 [1536, 6144], P(('dp', 'fsdp')), may hold values from -0.15625 to 0.15625
- out_weight: bfloat16 [3072, 1536], P(('dp', 'fsdp')), may hold values from -0.109375 to 0.109375
- x_projection: bfloat16 [2, 3072, 128], P(None, ('dp', 'fsdp')), may hold values from -0.109375 to 0.109375
- dt_projection: bfloat16 [2, 96, 3072], P(None, None, ('dp', 'fsdp')), may hold values from -0.625 to 0.625
- conv_weight: bfloat16 [2, 4, 3072], P(None, None, ('dp', 'fsdp')), may hold values from -3 to 3
- conv_bias: bfloat16 [2, 3072], P(None, ('dp', 'fsdp')), may hold values from -4 to 4
- dt_bias: bfloat16 [2, 3072], P(None, ('dp', 'fsdp')), may hold values from -6.5 to -2.5
- decay_log: bfloat16 [2, 3072, 16], P(None, ('dp', 'fsdp')), may hold values from -0.69921875 to 2.796875
- skip_gain: bfloat16 [2, 3072], P(None, ('dp', 'fsdp')), may hold values from 0.5 to 1.5
- mod_weight: bfloat16 [1536, 4608], P(('dp', 'fsdp')), may hold values from -0.15625 to 0.15625
- mod_bias: bfloat16 [4608], P(('dp', 'fsdp')), may hold values from -4 to 4
Outputs:
- block_out: bfloat16 [32, 512, 1536], P(('dp', 'fsdp'))
- grad_tokens: float32 [32, 512, 1536], P(('dp', 'fsdp'))
- grad_condition: float32 [32, 2, 1536], P(('dp', 'fsdp'))
- grad_in_weight: float32 [1536, 6144], P(('dp', 'fsdp'))
- grad_out_weight: float32 [3072, 1536], P(('dp', 'fsdp'))
- grad_x_projection: float32 [2, 3072, 128], P(None, ('dp', 'fsdp'))
- grad_dt_projection: float32 [2, 96, 3072], P(None, None, ('dp', 'fsdp'))
- grad_conv_weight: float32 [2, 4, 3072], P(None, None, ('dp', 'fsdp'))
- grad_conv_bias: float32 [2, 3072], P(None, ('dp', 'fsdp'))
- grad_dt_bias: float32 [2, 3072], P(None, ('dp', 'fsdp'))
- grad_decay_log: float32 [2, 3072, 16], P(None, ('dp', 'fsdp'))
- grad_skip_gain: float32 [2, 3072], P(None, ('dp', 'fsdp'))
- grad_mod_weight: float32 [1536, 4608], P(('dp', 'fsdp'))
- grad_mod_bias: float32 [4608], P(('dp', 'fsdp'))
Inputs may be any that keep to these rules, and one draw needn't show every extreme that they name: Each row holds two items: item_flags is 1 at position 0 and at exactly one position p with 128 <= p <= 384, and 0 elsewhere.
All inputs are finite; a program needn't handle non-finite values.
Results may differ from a plain program's by a relative error of at most 0.012.
The roundings to bfloat16 on the way count: a program that leaves them out, or rounds other values in their place, can miss the bound.
Values may be sent and summed in bfloat16 or wider, within the bound.
No kernel may reach another device: no remote copies, remote signals or barrier semaphores. Data moves between devices by JAX's collectives and lax.ppermute only.
A program may use at most 384 MiB of HBM per device.

v0:
```python
import jax
import jax.numpy as jnp
from jax import lax
from jax.sharding import PartitionSpec as P

NST = 16
RDT = 96
KCONV = 4
SCAN_BLOCK = 32


norm_eps = 1e-06


def scan_row(values, deltas, b_matrix, c_matrix, decay_rate, skip_row, starts):
    block_count = values.shape[0] // SCAN_BLOCK

    def block_step(carry_state, pieces_now):
        value_blk, delta_blk, b_blk, c_blk, start_blk = pieces_now
        state = carry_state
        results = []
        for position in range(value_blk.shape[0]):
            decay = jnp.exp(delta_blk[position][:, None] * decay_rate) * (1.0 - start_blk[position])
            state = (
                decay * state
                + (delta_blk[position] * value_blk[position])[:, None] * b_blk[position][None, :]
            )
            results.append(
                jnp.sum(state * c_blk[position][None, :], axis=1) + skip_row * value_blk[position]
            )
        return (state, jnp.stack(results))

    blocks = tuple(
        (
            item.reshape((block_count, SCAN_BLOCK) + item.shape[1:])
            for item in (values, deltas, b_matrix, c_matrix, starts)
        )
    )
    start_state = jnp.zeros((values.shape[1], b_matrix.shape[1]), values.dtype)
    _, results = lax.scan(jax.checkpoint(block_step), start_state, blocks)
    return results.reshape(values.shape)


def run_scans(values, dt_raw, b_and_c, bias_dt, log_rate, skips, both_starts):
    deltas = jax.nn.softplus(dt_raw + bias_dt[:, None, None, :])
    rates = -jnp.exp(log_rate)
    b_matrix = b_and_c[..., :NST]
    c_matrix = b_and_c[..., NST:]
    outputs = []
    for direction in range(2):

        def one_row(row_args, direction=direction):
            return scan_row(
                row_args[0],
                row_args[1],
                row_args[2],
                row_args[3],
                rates[direction],
                skips[direction],
                row_args[4],
            )

        outputs.append(
            lax.map(
                one_row,
                (
                    values[direction],
                    deltas[direction],
                    b_matrix[direction],
                    c_matrix[direction],
                    both_starts[direction],
                ),
            )
        )
    return jnp.stack(outputs)


def conv_silu(values, weights, conv_shift, starts):
    ids_now = jnp.cumsum(starts, axis=1, dtype=jnp.int32)
    length = values.shape[1]
    padded = jnp.pad(values, ((0, 0), (KCONV - 1, 0), (0, 0)))
    padded_ids = jnp.pad(ids_now, ((0, 0), (KCONV - 1, 0)), constant_values=-1)
    summed = values * weights[0] + conv_shift
    for lag_index in range(1, KCONV):
        offset = KCONV - 1 - lag_index
        seen_rows = padded[:, offset : offset + length]
        same_item = (padded_ids[:, offset : offset + length] == ids_now)[:, :, None]
        summed = summed + weights[lag_index] * jnp.where(same_item, seen_rows, 0.0)
    return jax.nn.silu(summed)


def conv_both(both_x, weights, biases, both_starts):
    return jnp.stack(
        [
            conv_silu(
                both_x[direction], weights[direction], biases[direction], both_starts[direction]
            )
            for direction in range(2)
        ]
    )


def reverse_starts(starts):
    flipped = jnp.flip(starts, axis=1)
    first_col = jnp.ones_like(starts[:, :1])
    return jnp.concatenate([first_col, flipped[:, :-1]], axis=1)


def per_token(modulation, ids_now):
    second_item = (ids_now == 1)[:, :, None]
    return jnp.where(second_item, modulation[:, 1][:, None, :], modulation[:, 0][:, None, :])


def normalize(x_now):
    row_mean = jnp.mean(x_now, axis=-1, keepdims=True)
    centered = x_now - row_mean
    variance = jnp.mean(centered * centered, axis=-1, keepdims=True)
    return centered * lax.rsqrt(variance + norm_eps)


def front(x_now, modulation, ids_now):
    model_width = x_now.shape[-1]
    shift_tok = per_token(modulation[..., :model_width], ids_now)
    scale_tok = per_token(modulation[..., model_width : 2 * model_width], ids_now)
    return normalize(x_now) * (1.0 + scale_tok) + shift_tok


def finish(x_now, modulation, branch, ids_now):
    model_width = x_now.shape[-1]
    gate_tok = per_token(modulation[..., 2 * model_width :], ids_now)
    return x_now + gate_tok * branch


def combine_ways(scan_outs, z_part):
    return (scan_outs[0] + jnp.flip(scan_outs[1], axis=1)) * jax.nn.silu(z_part)


def owner_major(grad, shard_dim, owners):
    shape = grad.shape
    pieces = grad.reshape(
        shape[:shard_dim] + (owners, shape[shard_dim] // owners) + shape[shard_dim + 1 :]
    )
    return jnp.moveaxis(pieces, shard_dim, 0).reshape(owners, -1)


def body(
    tokens_in,
    condition,
    item_flags,
    grad_out,
    in_weight,
    out_weight,
    x_projection,
    dt_projection,
    conv_weight,
    conv_bias,
    dt_bias,
    decay_log,
    skip_gain,
    mod_weight,
    mod_bias,
):
    gathered = (
        lax.all_gather(in_weight, ("dp", "fsdp"), axis=0, tiled=True),
        lax.all_gather(out_weight, ("dp", "fsdp"), axis=0, tiled=True),
        lax.all_gather(x_projection, ("dp", "fsdp"), axis=1, tiled=True),
        lax.all_gather(dt_projection, ("dp", "fsdp"), axis=2, tiled=True),
        lax.all_gather(conv_weight, ("dp", "fsdp"), axis=2, tiled=True),
        lax.all_gather(conv_bias, ("dp", "fsdp"), axis=1, tiled=True),
        lax.all_gather(dt_bias, ("dp", "fsdp"), axis=1, tiled=True),
        lax.all_gather(decay_log, ("dp", "fsdp"), axis=1, tiled=True),
        lax.all_gather(skip_gain, ("dp", "fsdp"), axis=1, tiled=True),
        lax.all_gather(mod_weight, ("dp", "fsdp"), axis=0, tiled=True),
        lax.all_gather(mod_bias, ("dp", "fsdp"), axis=0, tiled=True),
    )
    (
        full_in,
        full_out,
        full_xproj,
        full_dtproj,
        full_conv,
        full_convb,
        full_dtbias,
        full_alog,
        full_skip,
        full_mod,
        full_modb,
    ) = gathered
    conv_f = full_conv.astype(jnp.float32)
    convb_f = full_convb.astype(jnp.float32)
    dtbias_f = full_dtbias.astype(jnp.float32)
    alog_f = full_alog.astype(jnp.float32)
    skip_f = full_skip.astype(jnp.float32)
    x_f = tokens_in.astype(jnp.float32)
    ids_now = jnp.cumsum(item_flags, axis=1, dtype=jnp.int32) - 1
    cond_f = condition.astype(jnp.float32)
    cond_act = jax.nn.silu(cond_f).astype(jnp.bfloat16)
    modulation = jnp.einsum(
        "rid,dk->rik", cond_act, full_mod, preferred_element_type=jnp.float32
    ) + full_modb.astype(jnp.float32)
    normed_mod, front_back = jax.vjp(
        lambda x_now, mods_now: front(x_now, mods_now, ids_now), x_f, modulation
    )
    hidden = normed_mod.astype(jnp.bfloat16)
    mixed_rows = jnp.einsum("rtd,dk->rtk", hidden, full_in, preferred_element_type=jnp.float32)
    inner_width = mixed_rows.shape[-1] // 2
    x_part = mixed_rows[..., :inner_width]
    z_part = mixed_rows[..., inner_width:]
    both_starts = jnp.stack([item_flags, reverse_starts(item_flags)])
    both_x = jnp.stack([x_part, jnp.flip(x_part, axis=1)])
    conv_out, conv_back = jax.vjp(
        lambda values, weights, biases: conv_both(values, weights, biases, both_starts),
        both_x,
        conv_f,
        convb_f,
    )
    conv_low = conv_out.astype(jnp.bfloat16)
    projected = jnp.einsum(
        "grte,gek->grtk", conv_low, full_xproj, preferred_element_type=jnp.float32
    )
    dt_low = projected[..., :RDT].astype(jnp.bfloat16)
    dt_raw = jnp.einsum("grtk,gke->grte", dt_low, full_dtproj, preferred_element_type=jnp.float32)
    starts_f = both_starts.astype(jnp.float32)
    scan_outs, scan_back = jax.vjp(
        lambda values, raw_dt, b_and_c, bias_dt, log_rate, skips: run_scans(
            values, raw_dt, b_and_c, bias_dt, log_rate, skips, starts_f
        ),
        conv_low.astype(jnp.float32),
        dt_raw,
        projected[..., RDT:],
        dtbias_f,
        alog_f,
        skip_f,
    )
    gated, gate_back = jax.vjp(combine_ways, scan_outs, z_part)
    gated_low = gated.astype(jnp.bfloat16)
    branch = jnp.einsum("rte,ed->rtd", gated_low, full_out, preferred_element_type=jnp.float32)
    result, finish_back = jax.vjp(
        lambda x_now, mods_now, branch_now: finish(x_now, mods_now, branch_now, ids_now),
        x_f,
        modulation,
        branch,
    )
    out_low = result.astype(jnp.bfloat16)
    tied_shards = lax.optimization_barrier(
        (out_low, in_weight, out_weight, x_projection, dt_projection)
    )
    regathered = (
        lax.all_gather(tied_shards[1], ("dp", "fsdp"), axis=0, tiled=True),
        lax.all_gather(tied_shards[2], ("dp", "fsdp"), axis=0, tiled=True),
        lax.all_gather(tied_shards[3], ("dp", "fsdp"), axis=1, tiled=True),
        lax.all_gather(tied_shards[4], ("dp", "fsdp"), axis=2, tiled=True),
    )
    back_in, back_out, back_xproj, back_dtproj = regathered
    grad_f = grad_out.astype(jnp.float32)
    dx_resid, dmods_gate, d_branch = finish_back(grad_f)
    d_branch_low = d_branch.astype(jnp.bfloat16)
    grad_outw = jnp.einsum(
        "rte,rtd->ed", gated_low, d_branch_low, preferred_element_type=jnp.float32
    )
    d_gated = jnp.einsum("rtd,ed->rte", d_branch_low, back_out, preferred_element_type=jnp.float32)
    d_scans, d_zpart = gate_back(d_gated)
    d_values, d_dtraw, d_bandc, grad_dtbias, grad_alog, grad_skip = scan_back(d_scans)
    d_dtraw_low = d_dtraw.astype(jnp.bfloat16)
    grad_dtproj = jnp.einsum(
        "grtk,grte->gke", dt_low, d_dtraw_low, preferred_element_type=jnp.float32
    )
    d_dtlow = jnp.einsum(
        "grte,gke->grtk", d_dtraw_low, back_dtproj, preferred_element_type=jnp.float32
    )
    d_proj_low = jnp.concatenate([d_dtlow, d_bandc], axis=-1).astype(jnp.bfloat16)
    grad_xproj = jnp.einsum(
        "grte,grtk->gek", conv_low, d_proj_low, preferred_element_type=jnp.float32
    )
    d_convout = d_values + jnp.einsum(
        "grtk,gek->grte", d_proj_low, back_xproj, preferred_element_type=jnp.float32
    )
    d_both_x, grad_conv, grad_convb = conv_back(d_convout)
    d_xpart = d_both_x[0] + jnp.flip(d_both_x[1], axis=1)
    d_mixed_low = jnp.concatenate([d_xpart, d_zpart], axis=-1).astype(jnp.bfloat16)
    grad_inw = jnp.einsum("rtd,rtk->dk", hidden, d_mixed_low, preferred_element_type=jnp.float32)
    d_hidden = jnp.einsum("rtk,dk->rtd", d_mixed_low, back_in, preferred_element_type=jnp.float32)
    dx_front, dmods_front = front_back(d_hidden)
    grad_tokens = dx_resid + dx_front
    d_mods = dmods_gate + dmods_front
    d_mods_low = d_mods.astype(jnp.bfloat16)
    d_act = jnp.einsum("rik,dk->rid", d_mods_low, full_mod, preferred_element_type=jnp.float32)
    sigmoid_c = jax.nn.sigmoid(cond_f)
    grad_condition = d_act * sigmoid_c * (1.0 + cond_f * (1.0 - sigmoid_c))
    owners = lax.axis_size(("dp", "fsdp"))
    local_grads = (
        grad_inw,
        grad_outw,
        grad_xproj,
        grad_dtproj,
        grad_conv,
        grad_convb,
        grad_dtbias,
        grad_alog,
        grad_skip,
    )
    shard_dims = (0, 0, 1, 2, 2, 1, 1, 1, 1)
    flat_terms = jnp.concatenate(
        [owner_major(grad, shard_dim, owners) for grad, shard_dim in zip(local_grads, shard_dims)],
        axis=1,
    )
    received = lax.all_to_all(flat_terms, ("dp", "fsdp"), split_axis=0, concat_axis=0, tiled=True)
    owned_flat = jnp.sum(received, axis=0)
    summed_grads = []
    offset = 0
    for grad, shard_dim in zip(local_grads, shard_dims):
        shard_shape = (
            grad.shape[:shard_dim]
            + (grad.shape[shard_dim] // owners,)
            + grad.shape[shard_dim + 1 :]
        )
        count = grad.size // owners
        summed_grads.append(owned_flat[offset : offset + count].reshape(shard_shape))
        offset = offset + count
    grad_modb = jnp.sum(d_mods, axis=(0, 1))
    grad_modw = jnp.einsum("rid,rik->dk", cond_act, d_mods_low, preferred_element_type=jnp.float32)
    mod_summed = (
        lax.psum_scatter(grad_modw, ("dp", "fsdp"), scatter_dimension=0, tiled=True),
        lax.psum_scatter(grad_modb, ("dp", "fsdp"), scatter_dimension=0, tiled=True),
    )
    own_modw, own_modb = mod_summed
    return (out_low, grad_tokens, grad_condition) + tuple(summed_grads) + (own_modw, own_modb)


def solution(mesh):
    in_specs = (
        P(("dp", "fsdp"), None, None),
        P(("dp", "fsdp"), None, None),
        P(("dp", "fsdp"), None),
        P(("dp", "fsdp"), None, None),
        P(("dp", "fsdp"), None),
        P(("dp", "fsdp"), None),
        P(None, ("dp", "fsdp"), None),
        P(None, None, ("dp", "fsdp")),
        P(None, None, ("dp", "fsdp")),
        P(None, ("dp", "fsdp")),
        P(None, ("dp", "fsdp")),
        P(None, ("dp", "fsdp"), None),
        P(None, ("dp", "fsdp")),
        P(("dp", "fsdp"), None),
        P(("dp", "fsdp")),
    )
    out_specs = (
        P(("dp", "fsdp"), None, None),
        P(("dp", "fsdp"), None, None),
        P(("dp", "fsdp"), None, None),
        P(("dp", "fsdp"), None),
        P(("dp", "fsdp"), None),
        P(None, ("dp", "fsdp"), None),
        P(None, None, ("dp", "fsdp")),
        P(None, None, ("dp", "fsdp")),
        P(None, ("dp", "fsdp")),
        P(None, ("dp", "fsdp")),
        P(None, ("dp", "fsdp"), None),
        P(None, ("dp", "fsdp")),
        P(("dp", "fsdp"), None),
        P(("dp", "fsdp")),
    )
    return jax.shard_map(body, mesh=mesh, in_specs=in_specs, out_specs=out_specs, check_vma=False)
```

profile of v0, /device:TPU:0, one launch (start us, length us, event | category | flops | bytes accessed | tf_op | source)
XLA Modules:
  0.0 6116.8 jit_solution(11726938530918748913)
XLA Ops:
  13.8 43.7 all-reduce.433
  58.9 67.8 %all-gather.1 = bf16[32,96,2]{1,2,0:T(2,128)(2,1)S(1)} all-gather(bf16[1,96,2]{1,2,0:T(2,128)(2,1)} %bitcast.5237), channel_id=1, replica_groups=mesh['dp'=8,'fsdp'=4] {'dp','fsdp'}, dimensions={0}, use_global_device_ids=true | all-gather | bytes 12672 | tf_op jit(solution)/shard_map/all_gather | solution.py:170
  128.6 101.6 %all_gather.48 = bf16[2,4,3072]{1,0,2:T(2,128)(2,1)S(1)} all-gather(bf16[2,4,96]{1,0,2:T(2,128)(2,1)S(1)} %copy.214), channel_id=1, replica_groups=mesh['dp'=8,'fsdp'=4] {'dp','fsdp'}, dimensions={2}, use_global_device_ids=true | all-gather | bytes 50688 | tf_op jit(solution)/shard_map/all_gather | solution.py:168
  231.4 80.4 %slice_reduce_fusion.7 = (f32[3072]{0:T(1024)S(1)}, f32[3072]{0:T(1024)S(1)}, f32[3072]{0:T(1024)S(1)}, f32[3072]{0:T(1024)S(1)}, f32[3072]{0:T(1024)S(1)}, /*in...) fusion(f32[2,4,3072]{1,0,2:T(2,128)S(1)} %convert_element_type.101), kind=kLoop, calls=%fused_computation.1577 | loop fusion | bytes 196608 | tf_op jit(solution)/shard_map/jvp()/slice | solution.py:83
  312.7 66.8 %all-gather = bf16[32,96,2]{1,2,0:T(2,128)(2,1)S(1)} all-gather(bf16[1,96,2]{1,2,0:T(2,128)(2,1)S(1)} %bitcast.5238), channel_id=1, replica_groups=mesh['dp'=8,'fsdp'=4] {'dp','fsdp'}, dimensions={0}, use_global_device_ids=true | all-gather | bytes 12672 | tf_op jit(solution)/shard_map/all_gather | solution.py:169
  380.0 95.0 %all_gather.53 = bf16[2,3072,16]{2,0,1:T(2,128)(2,1)S(1)} all-gather(bf16[2,96,16]{2,0,1:T(2,128)(2,1)S(1)} %copy.219), channel_id=1, replica_groups=mesh['dp'=8,'fsdp'=4] {'dp','fsdp'}, dimensions={1}, use_global_device_ids=true | all-gather | bytes 202752 | tf_op jit(solution)/shard_map/all_gather | solution.py:171
  482.2 65.6 %all-gather.2 = bf16[32,96,2]{1,2,0:T(2,128)(2,1)S(1)} all-gather(bf16[1,96,2]{1,2,0:T(2,128)(2,1)S(1)} %bitcast.5239), channel_id=1, replica_groups=mesh['dp'=8,'fsdp'=4] {'dp','fsdp'}, dimensions={0}, use_global_device_ids=true | all-gather | bytes 12672 | tf_op jit(solution)/shard_map/all_gather | solution.py:172
  557.1 13.8 convolution_bitcast_fusion
  578.5 48.6 rev.17
  627.2 16.5 multiply_convert_fusion.2
  655.9 14.1 compare_select_fusion.2
  706.3 651.6 %while.147 = (s32[]{:T(128)}, f32[3072,16]{0,1:T(8,128)S(1)}, f32[16,32,3072]{2,1,0:T(8,128)}, f32[16,3072,16]{1,2,0:T(8,128)}, f32[16,32,3072]{2,1,0:T(8,128)},...) while((s32[]{:T(128)}, f32[3072,16]{0,1:T(8,128)S(1)}, ...), condition=%wide.region_73.74_spmd.clone, body=%wide.region_40.73_spmd.clone.sunk | while | flops 17006656 | bytes 13606657 | solution.py:40
  1365.1 641.4 %while.146 = (s32[]{:T(128)}, f32[3072,16]{0,1:T(8,128)S(1)}, f32[16,32,3072]{2,1,0:T(8,128)}, f32[16,3072,16]{1,2,0:T(8,128)}, f32[16,32,3072]{2,1,0:T(8,128)},...) while((s32[]{:T(128)}, f32[3072,16]{0,1:T(8,128)S(1)}, ...), condition=%wide.region_39.40_spmd.clone, body=%wide.region_6.39_spmd.clone.sunk | while | flops 17006656 | bytes 13606657 | solution.py:40
  2006.5 48.5 rev.18
  2087.7 21.4 reshape_reshape.7
  2109.1 47.5 all-gather.23.cloned.1.call-done
  2175.0 48.6 rev.19
  2239.5 820.0 %while.149 = (s32[]{:T(128)}, f32[3072,16]{0,1:T(8,128)S(1)}, f32[3072]{0:T(1024)S(1)}, f32[3072,16]{0,1:T(8,128)S(1)}, f32[16,32,3072]{2,1,0:T(8,128)}, /*index...) while((s32[]{:T(128)}, f32[3072,16]{0,1:T(8,128)S(1)}, ...), condition=%wide.region_333.334_spmd.clone, body=%wide.region_204.333_spmd.clone.sunk | while | flops 79463456 | bytes 44261148 | solution.py:40
  3067.8 851.6 %while.148 = (s32[]{:T(128)}, f32[3072,16]{0,1:T(8,128)S(1)}, f32[3072]{0:T(1024)S(1)}, f32[3072,16]{0,1:T(8,128)S(1)}, f32[16,32,3072]{2,1,0:T(8,128)}, /*index...) while((s32[]{:T(128)}, f32[3072,16]{0,1:T(8,128)S(1)}, ...), condition=%wide.region_203.204_spmd.clone, body=%wide.region_74.203_spmd.clone.sunk | while | flops 79463456 | bytes 44246812 | solution.py:40
  3922.8 17.0 fusion.291
  3961.4 31.3 multiply_reduce_fusion.327
  4009.6 17.9 fusion.212
  4035.1 48.5 rev.20
  4090.6 20.5 fusion.225
  4111.1 36.0 reshape_reshape.6
  4147.1 26.9 constant_dynamic-update-slice_fusion.5
  4222.3 12.8 constant_dynamic-update-slice_fusion.4
  4245.3 52.7 all_to_all.6
  4303.9 633.9 %all-gather.29.cloned.1.call-done = bf16[1536,6144]{1,0:T(8,128)(2,1)} async-done(((bf16[48,6144]{1,0:T(8,128)(2,1)}), bf16[1536,6144]{1,0:T(8,128)(2,1)}) %all-gather.29.cloned.1.call-update) | async-done | bytes 18874384 | tf_op jit(solution)/shard_map/all_gather | solution.py:249
  4937.8 16.7 select_reduce_fusion.5
  4968.5 952.6 %all-reduce.434 = f32[4608]{0:T(1024)S(1)} all-reduce(f32[4608]{0:T(1024)S(1)} %fusion.287), channel_id=3, replica_groups=mesh['dp'=8,'fsdp'=4] {'dp','fsdp'}, use_global_device_ids=true, to_apply=%region_356.357.clone | all-reduce | flops 4608 | bytes 36864
  5936.1 164.7 %reduce_sum.5990 = f32[489792]{0:T(1024)S(1)} reduce(f32[32,1,489792]{2,1,0:T(1,128)} %all-to-all-done, f32[]{:T(128)} %constant.448.clone.1), dimensions={0,1}, to_apply=%region_353.354 | reduce | flops 15183552 | bytes 64652548 | tf_op jit(solution)/shard_map/reduce_sum | solution.py:308
  (5322 shorter events, 1974.0 us)
Async XLA Ops:
  7.2 542.7 %all-gather.13.cloned.1.call-start = ((), (), s32[]{:S(2)}) async-start(), calls=%async_computation.2 | async-start | bytes 14598144 | tf_op jit(solution)/shard_map/all_gather | solution.py:173
  7.9 549.1 %all-gather.15.cloned.1.call-start = ((), (), s32[]{:S(2)}) async-start(), calls=%async_computation.3 | async-start | bytes 19464192 | tf_op jit(solution)/shard_map/all_gather | solution.py:164
  8.7 642.5 %all-gather.17.cloned.1.call-start = ((), (), s32[]{:S(2)}) async-start(), calls=%async_computation.4 | async-start | bytes 1622016 | tf_op jit(solution)/shard_map/all_gather | solution.py:166
  9.4 646.5 %all-gather.19.cloned.1.call-start = ((), (), s32[]{:S(2)}) async-start(), calls=%async_computation.5 | async-start | bytes 1622016 | tf_op jit(solution)/shard_map/all_gather | solution.py:167
  11.0 2053.4 %all-gather.21.cloned.1.call-start = ((), (), s32[]{:S(2)}) async-start(), calls=%async_computation.6 | async-start | bytes 9732096 | tf_op jit(solution)/shard_map/all_gather | solution.py:165
  11.6 2145.1 %all-gather.23.cloned.1.call-start = ((), (), s32[]{:S(2)}) async-start(), calls=%async_computation.7 | async-start | bytes 9732096 | tf_op jit(solution)/shard_map/all_gather | solution.py:250
  58.9 2097.7 %copy-start.51 = (pred[512]{0:T(512)(128)(4,1)}, pred[512]{0:T(512)(128)(4,1)S(1)}, u32[]{:S(2)}) copy-start(pred[512]{0:T(512)(128)(4,1)S(1)} %fusion.276) | copy-start | bytes 1540
  126.9 529.1 %copy-start.70 = (f32[3072,2]{0,1:T(2,128)}, f32[3072,2]{0,1:T(2,128)S(1)}, u32[]{:S(2)}) copy-start(f32[3072,2]{0,1:T(2,128)S(1)} %reshape.6859) | copy-start | bytes 73732
  127.8 515.9 %copy-start.79 = (pred[512]{0:T(512)(128)(4,1)}, pred[512]{0:T(512)(128)(4,1)S(1)}, u32[]{:S(2)}) copy-start(pred[512]{0:T(512)(128)(4,1)S(1)} %get-tuple-element.2059) | copy-start | bytes 1540
  127.8 515.9 %copy-start.81 = (pred[512]{0:T(512)(128)(4,1)}, pred[512]{0:T(512)(128)(4,1)S(1)}, u32[]{:S(2)}) copy-start(pred[512]{0:T(512)(128)(4,1)S(1)} %get-tuple-element.2060) | copy-start | bytes 1540
  127.8 515.9 %copy-start.83 = (pred[512]{0:T(512)(128)(4,1)}, pred[512]{0:T(512)(128)(4,1)S(1)}, u32[]{:S(2)}) copy-start(pred[512]{0:T(512)(128)(4,1)S(1)} %get-tuple-element.2061) | copy-start | bytes 1540
  311.7 315.4 %copy-start.54 = (f32[3072]{0:T(1024)}, f32[3072]{0:T(1024)S(1)}, u32[]{:S(2)}) copy-start(f32[3072]{0:T(1024)S(1)} %get-tuple-element.2040) | copy-start | bytes 36868
  311.8 315.4 %copy-start.64 = (f32[3072]{0:T(1024)}, f32[3072]{0:T(1024)S(1)}, u32[]{:S(2)}) copy-start(f32[3072]{0:T(1024)S(1)} %get-tuple-element.2045) | copy-start | bytes 36868
  311.8 315.3 %copy-start.66 = (f32[3072]{0:T(1024)}, f32[3072]{0:T(1024)S(1)}, u32[]{:S(2)}) copy-start(f32[3072]{0:T(1024)S(1)} %get-tuple-element.2046) | copy-start | bytes 36868
  311.8 315.3 %copy-start.68 = (f32[3072]{0:T(1024)}, f32[3072]{0:T(1024)S(1)}, u32[]{:S(2)}) copy-start(f32[3072]{0:T(1024)S(1)} %get-tuple-element.2047) | copy-start | bytes 36868
  311.8 331.9 %copy-start.56 = (f32[3072]{0:T(1024)}, f32[3072]{0:T(1024)S(1)}, u32[]{:S(2)}) copy-start(f32[3072]{0:T(1024)S(1)} %get-tuple-element.2044) | copy-start | bytes 36868
  311.8 331.9 %copy-start.58 = (f32[3072]{0:T(1024)}, f32[3072]{0:T(1024)S(1)}, u32[]{:S(2)}) copy-start(f32[3072]{0:T(1024)S(1)} %get-tuple-element.2041) | copy-start | bytes 36868
  311.8 331.9 %copy-start.60 = (f32[3072]{0:T(1024)}, f32[3072]{0:T(1024)S(1)}, u32[]{:S(2)}) copy-start(f32[3072]{0:T(1024)S(1)} %get-tuple-element.2042) | copy-start | bytes 36868
  311.8 331.9 %copy-start.62 = (f32[3072]{0:T(1024)}, f32[3072]{0:T(1024)S(1)}, u32[]{:S(2)}) copy-start(f32[3072]{0:T(1024)S(1)} %get-tuple-element.2043) | copy-start | bytes 36868
  379.9 247.3 %copy-start.85 = (pred[512]{0:T(512)(128)(4,1)}, pred[512]{0:T(512)(128)(4,1)S(1)}, u32[]{:S(2)}) copy-start(pred[512]{0:T(512)(128)(4,1)S(1)} %get-tuple-element.2056) | copy-start | bytes 1540
  379.9 247.3 %copy-start.87 = (pred[512]{0:T(512)(128)(4,1)}, pred[512]{0:T(512)(128)(4,1)S(1)}, u32[]{:S(2)}) copy-start(pred[512]{0:T(512)(128)(4,1)S(1)} %get-tuple-element.2057) | copy-start | bytes 1540
  2075.3 1864.4 %all-gather.25.cloned.1.call-start = ((), (), s32[]{:S(2)}) async-start(), calls=%async_computation.8 | async-start | bytes 1622016 | tf_op jit(solution)/shard_map/all_gather | solution.py:252
  2076.2 1875.6 %all-gather.27.cloned.1.call-start = ((), (), s32[]{:S(2)}) async-start(), calls=%async_computation.9 | async-start | bytes 1622016 | tf_op jit(solution)/shard_map/all_gather | solution.py:251
  3067.8 855.0 %copy-start.71 = (f32[3072,2]{0,1:T(2,128)S(1)}, f32[3072,2]{0,1:T(2,128)}, u32[]{:S(2)}) copy-start(f32[3072,2]{0,1:T(2,128)} %copy-done.70) | copy-start | bytes 73732
  4297.9 639.8 %copy-start.27 = (bf16[1,512,1536]{2,1,0:T(8,128)(2,1)S(1)}, bf16[1,512,1536]{2,1,0:T(8,128)(2,1)}, u32[]{:S(2)}) copy-start(bf16[1,512,1536]{2,1,0:T(8,128)(2,1)} %param.26) | copy-start | bytes 4718596
  4297.9 639.8 %copy-start.35 = (f32[512]{0:T(512)S(1)}, f32[512]{0:T(512)}, u32[]{:S(2)}) copy-start(f32[512]{0:T(512)} %copy-done.33) | copy-start | bytes 6148
  4297.9 639.8 %copy-start.42 = (f32[512]{0:T(512)S(1)}, f32[512]{0:T(512)}, u32[]{:S(2)}) copy-start(f32[512]{0:T(512)} %copy-done.40) | copy-start | bytes 6148
  4298.0 639.8 %copy-start.53 = (pred[512]{0:T(512)(128)(4,1)S(1)}, pred[512]{0:T(512)(128)(4,1)}, u32[]{:S(2)}) copy-start(pred[512]{0:T(512)(128)(4,1)} %copy-done.51) | copy-start | bytes 1540
  4298.0 1638.1 %all-to-all-start = ((f32[32,1,489792]{2,1,0:T(1,128)}), f32[32,1,489792]{2,1,0:T(1,128)}, u32[]{:S(2)}, u32[]{:S(2)}) async-start(f32[32,1,489792]{2,1,0:T(1,128)} %all_to_all.6), calls=%async_computation | async-start | bytes 125403136 | tf_op jit(solution)/shard_map/all_to_all | solution.py:307
  4303.1 634.7 %all-gather.29.cloned.1.call-start = ((), (), s32[]{:S(2)}) async-start(), calls=%async_computation.10 | async-start | bytes 19464192 | tf_op jit(solution)/shard_map/all_gather | solution.py:249
  4303.8 1805.9 %reduce-scatter.2.cloned.1.call-start = ((), (), s32[]{:S(2)}) async-start(), calls=%async_computation.11 | async-start | bytes 29196288 | tf_op jit(solution)/shard_map/reduce_scatter | solution.py:323
  4968.4 953.3 %copy-start.75 = (f32[512]{0:T(512)S(1)}, f32[512]{0:T(512)}, u32[]{:S(2)}) copy-start(f32[512]{0:T(512)} %copy-done.74) | copy-start | bytes 6148
  (76 other events, 2070.4 us)
Sparse Core Ops, SparseCore 0:
  10.8 106.0 all-gather.12
  119.6 141.7 all-gather.14
  264.3 55.0 all-gather.16
  322.7 53.9 all-gather.18
  379.4 93.0 all-gather.20
  2075.5 81.1 all-gather.22
  2160.1 53.4 all-gather.24
  2216.6 54.0 all-gather.26
  4306.7 631.0 all-gather.28
  4968.6 624.7 reduce-scatter.1
where the time goes:
time: 6180 us; the launch traced here: 6120 us
  blocking collectives  1390 us (22%)
  other arithmetic  1320 us (21%)
  loops' own time  1320 us (21%)
  local copies, waits for them, and re-layouts  1230 us (20%)
  waiting for transfers between devices  685 us (11%)
  matrix products  149 us (2%)
    another operation x4, loops' own time, scan_row(): _, results = lax.scan(jax.checkpoint(block_step), start_state, blocks)  1320 us
    unnamed x2, blocking collectives  996 us
    all_gather x1, waiting for transfers between devices, body(): lax.all_gather(tied_shards[1], ('dp', 'fsdp'), axis=0, tiled=True)  634 us
    reduce_sum x512, other arithmetic, block_step(): delta_blk[position][:, None] * decay_rate  277 us
    dynamic_update_slice x160, other arithmetic, scan_row(): _, results = lax.scan(jax.checkpoint(block_step), start_state, blocks)  204 us
    reduce_sum x1, other arithmetic, body(): owned_flat = jnp.sum(received, axis=0)  165 us
    reduce_sum x288, other arithmetic, block_step(): jnp.sum(state * c_blk[position][None, :], axis=1)  147 us
    slice x128, local copies, waits for them, and re-layouts, block_step(): delta_blk[position][:, None] * decay_rate  140 us

commit v1 on v0

v1 whole, which is shorter than its diff:
```python
import functools

import jax
import jax.numpy as jnp
from jax import lax
from jax.experimental import pallas as pl
from jax.experimental.pallas import tpu as pltpu
from jax.sharding import PartitionSpec as P

NST = 16
SUB = 16
LANES = 128
bf16 = jnp.bfloat16
f32 = jnp.float32


def split_hi_lo(v):
    hi = v.astype(bf16)
    lo = (v - hi.astype(f32)).astype(bf16)
    return jnp.concatenate([hi, lo], axis=0)


def block_diag(tiled):
    rows = lax.broadcasted_iota(jnp.int32, tiled.shape, 0)
    cols = lax.broadcasted_iota(jnp.int32, tiled.shape, 1) // NST
    return jnp.where(rows == cols, tiled, 0.0)


def fwd_kernel(delta_ref, u_ref, sb_ref, bx_ref, ct_ref, a2_ref, skip_ref, y_ref, ck_ref,
               h_scr, dx_scr, du_scr, hs_scr, *, backwards, subs, width):
    first = pl.program_id(1) == 0
    lane0 = pl.multiple_of(pl.program_id(2) * width, width)
    tiles = width // LANES

    @pl.when(first)
    def _():
        h_scr[:, pl.ds(lane0, width)] = jnp.zeros((NST, width), f32)

    order = range(SUB - 1, -1, -1) if backwards else range(SUB)

    def sub_step(step, carry):
        sub = subs - 1 - step if backwards else step
        row0 = pl.multiple_of(sub * SUB, SUB)
        rows = pl.ds(row0, SUB)
        delta = delta_ref[rows, :]
        u = u_ref[rows, :].astype(f32)
        du_scr[...] = delta * u
        sb = sb_ref[rows, :]
        for j in range(tiles):
            lanes = pl.ds(j * LANES, LANES)
            dx_scr[:, lanes] = delta[:, j * LANES:(j + 1) * LANES] + sb
        h = [h_scr[:, pl.ds(lane0 + j * LANES, LANES)] for j in range(tiles)]
        a2 = [a2_ref[:, pl.ds(lane0 + j * LANES, LANES)] for j in range(tiles)]
        for j in range(tiles):
            ck_ref[sub, :, pl.ds(j * LANES, LANES)] = h[j]
        for t in order:
            b = bx_ref[row0 + t]
            for j in range(tiles):
                lanes = pl.ds(j * LANES, LANES)
                dx = dx_scr[pl.ds(t, 1), lanes]
                du = du_scr[pl.ds(t, 1), lanes]
                h[j] = jnp.exp2(dx * a2[j]) * h[j] + du * b
                hs_scr[pl.ds(t * NST, NST), lanes] = h[j].astype(bf16)
        for j in range(tiles):
            h_scr[:, pl.ds(lane0 + j * LANES, LANES)] = h[j]
        c2 = split_hi_lo(block_diag(ct_ref[rows, :]))
        y2 = jnp.dot(c2, hs_scr[...], preferred_element_type=f32)
        y_ref[rows, :] = y2[:SUB] + y2[SUB:] + skip_ref[:, pl.ds(lane0, width)] * u
        return carry

    lax.fori_loop(0, subs, sub_step, 0)


def bwd_kernel(delta_ref, u_ref, sb_ref, bx_ref, cx_ref, bt_ref, ds_ref, ck_ref, a_ref, a2_ref,
               skip_ref, du_out, dr_out, db_out, dc_out, ga_out, gs_out, gb_out,
               g_scr, dx_scr, du_scr, ds_scr, da_scr, hp_scr, hs_scr, lam_scr, r_scr,
               *, backwards, subs, width):
    first = pl.program_id(1) == 0
    start = jnp.logical_and(first, pl.program_id(0) == 0)
    eg = pl.program_id(2)
    lane0 = pl.multiple_of(eg * width, width)
    tiles = width // LANES
    wide = pl.ds(lane0, width)

    @pl.when(first)
    def _():
        g_scr[:, wide] = jnp.zeros((NST, width), f32)

    @pl.when(start)
    def _():
        ga_out[:, wide] = jnp.zeros((NST, width), f32)
        gs_out[:, wide] = jnp.zeros((SUB, width), f32)
        gb_out[:, wide] = jnp.zeros((SUB, width), f32)

    @pl.when(eg == 0)
    def _():
        db_out[...] = jnp.zeros_like(db_out)
        dc_out[...] = jnp.zeros_like(dc_out)

    order = list(range(SUB - 1, -1, -1) if backwards else range(SUB))

    def sub_step(step, carry):
        sub = step if backwards else subs - 1 - step
        row0 = pl.multiple_of(sub * SUB, SUB)
        rows = pl.ds(row0, SUB)
        delta = delta_ref[rows, :]
        u = u_ref[rows, :].astype(f32)
        ds = ds_ref[rows, :]
        du_scr[...] = delta * u
        ds_scr[...] = ds
        sb = sb_ref[rows, :]
        for j in range(tiles):
            dx_scr[:, pl.ds(j * LANES, LANES)] = delta[:, j * LANES:(j + 1) * LANES] + sb
        for j in range(tiles):
            lanes = pl.ds(j * LANES, LANES)
            a2 = a2_ref[:, pl.ds(lane0 + j * LANES, LANES)]
            h = ck_ref[sub, :, lanes]
            for t in order:
                dx = dx_scr[pl.ds(t, 1), lanes]
                du = du_scr[pl.ds(t, 1), lanes]
                hp_scr[t, :, lanes] = h
                da = jnp.exp2(dx * a2)
                da_scr[t, :, lanes] = da
                h = da * h + du * bx_ref[row0 + t]
                hs_scr[pl.ds(t * NST, NST), lanes] = h.astype(bf16)
        for j in range(tiles):
            lanes = pl.ds(j * LANES, LANES)
            glob = pl.ds(lane0 + j * LANES, LANES)
            a = a_ref[:, glob]
            g = g_scr[:, glob]
            ga = ga_out[:, glob]
            for t in reversed(order):
                lam = cx_ref[row0 + t] * ds_scr[pl.ds(t, 1), lanes] + g
                lam_scr[pl.ds(t * NST, NST), lanes] = lam.astype(bf16)
                g = da_scr[t, :, lanes] * lam
                r = g * hp_scr[t, :, lanes] * a
                r_scr[pl.ds(t * NST, NST), lanes] = r.astype(bf16)
                ga = ga + dx_scr[pl.ds(t, 1), lanes] * r
            g_scr[:, glob] = g
            ga_out[:, glob] = ga
        b2 = split_hi_lo(block_diag(bt_ref[rows, :]))
        s2 = jnp.dot(b2, lam_scr[...], preferred_element_type=f32)
        s1 = s2[:SUB] + s2[SUB:]
        ones = block_diag(jnp.ones((SUB, SUB * NST), f32)).astype(bf16)
        dd = jnp.dot(ones, r_scr[...], preferred_element_type=f32) + u * s1
        du_out[rows, :] = skip_ref[:, wide] * ds + delta * s1
        small = delta * (1.0 - delta * (0.5 - delta * (1.0 / 6.0)))
        sig = jnp.where(delta < 0.03, small, 1.0 - jnp.exp(-delta))
        dr = dd * sig
        dr_out[rows, :] = dr.astype(bf16)
        gb_out[:, wide] += dr
        gs_out[:, wide] += ds * u
        nt = (((1,), (1,)), ((), ()))
        d2 = lax.dot_general(split_hi_lo(delta * u), lam_scr[...], nt, preferred_element_type=f32)
        db_out[rows, :] += d2[:SUB] + d2[SUB:]
        e2 = lax.dot_general(split_hi_lo(ds), hs_scr[...], nt, preferred_element_type=f32)
        dc_out[rows, :] += e2[:SUB] + e2[SUB:]
        return carry

    lax.fori_loop(0, subs, sub_step, 0)


def lane_groups(width_all):
    for width in (512, 384, 256, 128):
        if width_all % width == 0:
            return width
    return width_all


def scan_calls(rows, length, inner, backwards, tblock=128, width=None):
    width = width or lane_groups(inner)
    n_t, n_e, subs = length // tblock, inner // width, tblock // SUB
    params = pltpu.CompilerParams(dimension_semantics=("arbitrary",) * 3)

    def specs(flip):
        tb = (lambda i: n_t - 1 - i) if flip else (lambda i: i)
        tok = pl.BlockSpec((None, tblock, width), lambda r, i, e: (r, tb(i), e))
        lane = pl.BlockSpec((None, tblock, LANES), lambda r, i, e: (r, tb(i), 0))
        exp = pl.BlockSpec((None, tblock, NST, LANES), lambda r, i, e: (r, tb(i), 0, 0))
        til = pl.BlockSpec((None, tblock, SUB * NST), lambda r, i, e: (r, tb(i), 0))
        ck = pl.BlockSpec((None, subs, NST, width), lambda r, i, e: (r, tb(i), 0, e))
        full = pl.BlockSpec((NST, inner), lambda r, i, e: (0, 0))
        one = pl.BlockSpec((1, inner), lambda r, i, e: (0, 0))
        return tok, lane, exp, til, ck, full, one

    sds = jax.ShapeDtypeStruct
    work = rows * length * inner * NST
    tok, lane, exp, til, ck, full, one = specs(backwards)
    fwd = pl.pallas_call(
        functools.partial(fwd_kernel, backwards=backwards, subs=subs, width=width),
        grid=(rows, n_t, n_e),
        in_specs=[tok, tok, lane, exp, til, full, one],
        out_specs=[tok, ck],
        out_shape=[sds((rows, length, inner), f32), sds((rows, length // SUB, NST, inner), f32)],
        scratch_shapes=[pltpu.VMEM((NST, inner), f32), pltpu.VMEM((SUB, width), f32),
                        pltpu.VMEM((SUB, width), f32), pltpu.VMEM((SUB * NST, width), bf16)],
        compiler_params=params,
        name="scan_ahead_" + ("b" if backwards else "f"),
    )
    tok, lane, exp, til, ck, full, one = specs(not backwards)
    bwd = pl.pallas_call(
        functools.partial(bwd_kernel, backwards=backwards, subs=subs, width=width),
        grid=(rows, n_t, n_e),
        in_specs=[tok, tok, lane, exp, exp, til, tok, ck, full, full, one],
        out_specs=[tok, tok, til, til, full, full, full],
        out_shape=[sds((rows, length, inner), f32), sds((rows, length, inner), bf16),
                   sds((rows, length, SUB * NST), f32), sds((rows, length, SUB * NST), f32),
                   sds((NST, inner), f32), sds((SUB, inner), f32), sds((SUB, inner), f32)],
        scratch_shapes=[pltpu.VMEM((NST, inner), f32)] + [pltpu.VMEM((SUB, width), f32)] * 3
        + [pltpu.VMEM((SUB, NST, width), f32)] * 2 + [pltpu.VMEM((SUB * NST, width), bf16)] * 3,
        compiler_params=params,
        name="scan_back_" + ("b" if backwards else "f"),
    )
    return fwd, bwd


RDT = 96
KCONV = 4
EPS = 1e-06
AXES = ("dp", "fsdp")
BIG = 1e30
LOG2E = 1.4426950408889634


def shifted(v, by):
    if by == 0:
        return v
    pad = jnp.zeros((abs(by),) + v.shape[1:], v.dtype)
    if by > 0:
        return jnp.concatenate([pad, v[:-by]], axis=0)
    return jnp.concatenate([v[-by:], pad], axis=0)


def same_item(ids, by):
    return (shifted(ids + 1, by) == ids + 1)[:, None]


def conv_pre(x, weights, bias, ids, sign):
    pre = x * weights[0] + bias
    for lag in range(1, KCONV):
        pre = pre + weights[lag] * jnp.where(same_item(ids, sign * lag), shifted(x, sign * lag), 0.0)
    return pre


def mm(a, b, dims):
    return lax.dot_general(a, b, (dims, ((), ())), preferred_element_type=f32)


def body(tokens_in, condition, item_flags, grad_out, in_weight, out_weight, x_projection,
         dt_projection, conv_weight, conv_bias, dt_bias, decay_log, skip_gain, mod_weight, mod_bias):
    length, model = tokens_in.shape[1:]
    owners = lax.axis_size(AXES)
    me = lax.axis_index(AXES)
    inner = in_weight.shape[1] // 2
    own_model = in_weight.shape[0]
    own_inner = out_weight.shape[0]
    gather0 = lambda v: lax.all_gather(v, AXES, axis=0, tiled=True)

    cond = condition[0].astype(f32)
    act = jax.nn.silu(cond).astype(bf16)
    smalls = (act, conv_weight, conv_bias, dt_bias, decay_log, skip_gain, mod_bias)
    flat = jnp.concatenate([v.reshape(-1) for v in smalls])
    flat = jnp.pad(flat, (0, -flat.shape[0] % LANES))
    everyone = lax.all_gather(flat, AXES, axis=0, tiled=False)
    parts, at = [], 0
    for v in smalls:
        parts.append(everyone[:, at:at + v.size].reshape((owners,) + v.shape))
        at += v.size
    act_all = parts[0].reshape(owners * 2, model)
    join = lambda v, dim: jnp.moveaxis(v, 0, dim).reshape(
        v.shape[1:dim + 1] + (owners * v.shape[dim + 1],) + v.shape[dim + 2:]).astype(f32)
    conv_w, conv_b, dt_b = join(parts[1], 2), join(parts[2], 1), join(parts[3], 1)
    log_rate, skip = join(parts[4], 1), join(parts[5], 1)
    modb = parts[6].reshape(-1).astype(f32)

    w_x = gather0(in_weight[:, :inner])
    w_xp = lax.all_gather(x_projection, AXES, axis=1, tiled=True)
    w_dt = lax.all_gather(dt_projection, AXES, axis=2, tiled=True)
    w_z = gather0(in_weight[:, inner:])
    w_o = gather0(out_weight)

    act_own = lax.dynamic_slice(act_all, (0, me * own_model), (owners * 2, own_model))
    partial = mm(act_own, mod_weight, ((1,), (0,))).reshape(owners, 2, -1)
    mods = jnp.sum(lax.all_to_all(partial, AXES, 0, 0, tiled=True), axis=0) + modb
    flags = item_flags[0]
    ids = jnp.cumsum(flags, dtype=jnp.int32) - 1
    second = (ids == 1)[:, None]
    pick = lambda v: jnp.where(second, v[1], v[0])
    shift, scale, gate = (mods[:, i * model:(i + 1) * model] for i in range(3))

    x = tokens_in[0].astype(f32)
    mean = jnp.mean(x, axis=1, keepdims=True)
    centered = x - mean
    inv = lax.rsqrt(jnp.mean(centered * centered, axis=1, keepdims=True) + EPS)
    normed = centered * inv
    hidden = (normed * (1.0 + pick(scale)) + pick(shift)).astype(bf16)
    xs = mm(hidden, w_x, ((1,), (0,)))

    g = grad_out[0].astype(f32)
    d_branch = (g * pick(gate)).astype(bf16)

    starts = flags.astype(f32)
    starts_b = jnp.concatenate([starts[1:], jnp.ones((1,), f32)])
    calls = [scan_calls(1, length, inner, bool(d)) for d in range(2)]
    wide = lambda v: jnp.broadcast_to(v[None, :, :, None], (1, length, NST, LANES))
    tile = lambda v: jnp.tile(v, (1, SUB))[None]
    kept = []
    for d, sign in ((0, 1), (1, -1)):
        u = jax.nn.silu(conv_pre(xs, conv_w[d], conv_b[d], ids, sign)).astype(bf16)
        proj = mm(u, w_xp[d], ((1,), (0,)))
        dt_low = proj[:, :RDT].astype(bf16)
        b_m, c_m = proj[:, RDT:RDT + NST], proj[:, RDT + NST:]
        delta = jax.nn.softplus(mm(dt_low, w_dt[d], ((1,), (0,))) + dt_b[d])
        rate = -jnp.exp(log_rate[d]).T
        rate2 = rate * LOG2E
        sb = jnp.broadcast_to((BIG * (starts_b if d else starts))[None, :, None], (1, length, LANES))
        b_wide = wide(b_m)
        y, ck = calls[d][0](delta[None], u[None], sb, b_wide, tile(c_m), rate2, skip[d][None])
        kept.append((u, dt_low, b_m, c_m, delta, rate, rate2, sb, b_wide, y[0], ck))
    both = kept[0][9] + kept[1][9]
    z = mm(hidden, w_z, ((1,), (0,)))
    sig_z = jax.nn.sigmoid(z)
    silu_z = z * sig_z
    gated = (both * silu_z).astype(bf16)
    branch = mm(gated, w_o, ((1,), (0,)))
    block_out = (x + pick(gate) * branch).astype(bf16)

    d_gate = g * branch
    scatter = lambda v: lax.psum_scatter(v, AXES, scatter_dimension=0, tiled=True)
    grad_out_w = scatter(mm(gated, d_branch, ((0,), (0,))).astype(bf16)).astype(f32)
    d_gated = mm(d_branch, w_o, ((1,), (1,)))
    d_scan = d_gated * silu_z
    d_z = (d_gated * both * sig_z * (1.0 + z * (1.0 - sig_z))).astype(bf16)
    grad_in_z = scatter(mm(hidden, d_z, ((0,), (0,))).astype(bf16)).astype(f32)
    d_xs = 0.0
    per_dir = []
    for d, sign in ((0, 1), (1, -1)):
        u, dt_low, b_m, c_m, delta, rate, rate2, sb, b_wide, _, ck = kept[d]
        du, dr, db, dc, ga, gs, gb = calls[d][1](
            delta[None], u[None], sb, b_wide, wide(c_m), tile(b_m), d_scan[None], ck, rate, rate2,
            skip[d][None])
        own = lambda m: jnp.sum(jnp.where(
            jnp.eye(SUB, dtype=bool)[None, :, :, None],
            m.reshape(length // SUB, SUB, SUB, NST), 0.0), axis=2).reshape(length, NST)
        dr = dr[0]
        g_dt = mm(dt_low, dr, ((0,), (0,)))
        d_low = mm(dr, w_dt[d], ((1,), (1,)))
        d_proj = jnp.concatenate([d_low, own(db), own(dc)], axis=1).astype(bf16)
        g_xp = mm(u, d_proj, ((0,), (0,)))
        d_u = du[0] + mm(d_proj, w_xp[d], ((1,), (1,)))
        pre = conv_pre(xs, conv_w[d], conv_b[d], ids, sign)
        sg = jax.nn.sigmoid(pre)
        d_pre = d_u * sg * (1.0 + pre * (1.0 - sg))
        g_cb = jnp.sum(d_pre, axis=0)
        g_cw = []
        for lag in range(KCONV):
            mine = jnp.where(same_item(ids, sign * lag), shifted(xs, sign * lag), 0.0) if lag else xs
            g_cw.append(jnp.sum(d_pre * mine, axis=0))
            back = (jnp.where(same_item(ids, -sign * lag), shifted(d_pre, -sign * lag), 0.0)
                    if lag else d_pre)
            d_xs = d_xs + conv_w[d, lag] * back
        per_dir.append((g_xp, g_dt, jnp.stack(g_cw), g_cb, jnp.sum(gb, axis=0), ga.T,
                        jnp.sum(gs, axis=0)))
    d_xs = d_xs.astype(bf16)
    grad_in_x = scatter(mm(hidden, d_xs, ((0,), (0,))).astype(bf16)).astype(f32)
    grad_in = jnp.concatenate([grad_in_x, grad_in_z], axis=1)
    d_hidden = mm(d_xs, w_x, ((1,), (1,))) + mm(d_z, w_z, ((1,), (1,)))

    stacked = [jnp.stack(pair) for pair in zip(*per_dir)]
    dims = (1, 2, 2, 1, 1, 1, 1)
    pieces, shapes = [], []
    for v, dim in zip(stacked, dims):
        shape = v.shape[:dim] + (owners, v.shape[dim] // owners) + v.shape[dim + 1:]
        pieces.append(jnp.moveaxis(v.reshape(shape), dim, 0).reshape(owners, -1).astype(bf16))
        shapes.append(v.shape[:dim] + (v.shape[dim] // owners,) + v.shape[dim + 1:])
    packed = jnp.concatenate(pieces, axis=1)
    packed = jnp.pad(packed, ((0, 0), (0, -packed.shape[1] % (16 * LANES))))
    mine = scatter(packed.reshape(-1, LANES)).astype(f32).reshape(-1)
    small_grads, at = [], 0
    for shape in shapes:
        count = 1
        for n in shape:
            count *= n
        small_grads.append(mine[at:at + count].reshape(shape))
        at += count

    scale_tok = 1.0 + pick(scale)
    d_n = d_hidden * scale_tok
    m1 = jnp.mean(d_n, axis=1, keepdims=True)
    m2 = jnp.mean(d_n * normed, axis=1, keepdims=True)
    grad_tokens = g + (d_n - m1 - normed * m2) * inv
    by_item = lambda v: jnp.stack([jnp.sum(jnp.where(second, 0.0, v), axis=0),
                                   jnp.sum(jnp.where(second, v, 0.0), axis=0)])
    d_mods = jnp.concatenate([by_item(d_hidden), by_item(d_hidden * normed), by_item(d_gate)], axis=1)
    d_mods_all = gather0(d_mods.astype(bf16))
    grad_mod_w = mm(act_own, d_mods_all, ((0,), (0,)))
    own_b = mod_bias.shape[0]
    grad_mod_b = jnp.sum(
        lax.dynamic_slice(d_mods_all, (0, me * own_b), (owners * 2, own_b)).astype(f32), axis=0)
    d_act = mm(d_mods_all, mod_weight, ((1,), (1,))).reshape(owners, 2, own_model)
    d_act = lax.all_to_all(d_act, AXES, 0, 0, tiled=True)
    d_act = jnp.moveaxis(d_act, 0, 1).reshape(2, model)
    sc = jax.nn.sigmoid(cond)
    grad_cond = d_act * sc * (1.0 + cond * (1.0 - sc))
    g_xp, g_dt, g_cw, g_cb, g_db, g_al, g_sk = small_grads
    return (block_out[None], grad_tokens[None], grad_cond[None], grad_in, grad_out_w, g_xp, g_dt,
            g_cw, g_cb, g_db, g_al, g_sk, grad_mod_w, grad_mod_b)


def solution(mesh):
    row3, row2, row1 = P(AXES, None, None), P(AXES, None), P(AXES)
    mid3, mid2, last3 = P(None, AXES, None), P(None, AXES), P(None, None, AXES)
    weights = (row2, row2, mid3, last3, last3, mid2, mid2, mid3, mid2, row2, row1)
    return jax.shard_map(
        body, mesh=mesh, in_specs=(row3, row3, row2, row3) + weights,
        out_specs=(row3, row3, row3) + weights, check_vma=False)
```

time: 6180 us -> 1330 us (0.22)
  loops' own time: 1320 us -> 0 us
  other arithmetic: 1320 us -> 79.2 us
  blocking collectives: 1390 us -> 152 us
  local copies, waits for them, and re-layouts: 1230 us -> 177 us
  Pallas kernels: 0 us -> 369 us
  waiting for transfers between devices: 685 us -> 354 us
    another operation x4 -> x0, loops' own time: 1320 us -> none  [scan_row(): _, results = lax.scan(jax.checkpoint(block_step), start_state, blocks)]
    unnamed x2 -> x0, blocking collectives: 996 us -> none
    reduce_sum x1192 -> x9, other arithmetic: 815 us -> 13.2 us  [the longest x1 8.39 us: body(): jnp.sum(jnp.where(jnp.eye(SUB, dtype=bool)[None, :, :, None], m.reshape(l...]
    all_gather x9 -> x5, waiting for transfers between devices: 681 us -> 10.2 us  [the longest x3 10.1 us: body(): gather0 = lambda v: lax.all_gather(v, AXES, axis=0, tiled=True)]
    slice x403 -> x31, local copies, waits for them, and re-layouts: 478 us -> 70.1 us  [the longest x9 47.6 us: shifted(): return jnp.concatenate([v[-by:], pad], axis=0)]
    pallas_call x0 -> x4, Pallas kernels: none -> 369 us  [the longest x2 251 us: body(): calls[d][1]]
    reduce_scatter x1 -> x4, waiting for transfers between devices: 0.01 us -> 342 us  [body(): lax.psum_scatter(v, AXES, scatter_dimension=0, tiled=True)]
    all_gather x5 -> x2, blocking collectives: 397 us -> 152 us  [the longest x1 80 us: body(): everyone = lax.all_gather(flat, AXES, axis=0, tiled=False)]
where the time goes in v1:
time: 1330 us; the launch traced here: 1320 us
  Pallas kernels  369 us (28%)
  waiting for transfers between devices  354 us (27%)
  local copies, waits for them, and re-layouts  177 us (13%)
  matrix products  168 us (13%)
  blocking collectives  152 us (11%)
  other arithmetic  79.2 us (6%)
  between operations  15.6 us (1%)
    reduce_scatter x4, waiting for transfers between devices, body(): lax.psum_scatter(v, AXES, scatter_dimension=0, tiled=True)  342 us
    pallas_call x2, Pallas kernels, body(): calls[d][1]  251 us
    dot_general x24, matrix products, mm(): return lax.dot_general(a, b, (dims, ((), ())), preferred_element_type=f32)  168 us
    pallas_call x2, Pallas kernels, body(): calls[d][0]  118 us
    all_gather x1, blocking collectives, body(): everyone = lax.all_gather(flat, AXES, axis=0, tiled=False)  80 us
    all_gather x1, blocking collectives, body(): gather0 = lambda v: lax.all_gather(v, AXES, axis=0, tiled=True)  71.9 us
    slice x9, local copies, waits for them, and re-layouts, shifted(): return jnp.concatenate([v[-by:], pad], axis=0)  47.6 us
    convert_element_type x2, other arithmetic, body(): u = jax.nn.silu(conv_pre(xs, conv_w[d], conv_b[d], ids, sign)).astype(bf16)  27.9 us
  transfers between devices with their start and end apart: 11, of which 5 were waited for; matrix products, arithmetic and copies ran while one was open for 21% of the time, Pallas kernels for 9%

profile of v1, /device:TPU:0, one launch (start us, length us, event | category | flops | bytes accessed | tf_op | source)
XLA Modules:
  0.0 1320.9 jit_solution(4723346469454282778)
XLA Ops:
  17.6 80.0 %all-gather.1 = bf16[32,1,7680]{2,1,0:T(2,128)(2,1)S(1)} all-gather(bf16[1,1,7680]{2,1,0:T(2,128)(2,1)S(1)} %reshape.508), channel_id=2, replica_groups=mesh['dp'=8,'fsdp'=4] {'dp','fsdp'}, dimensions={0}, use_global_device_ids=true | all-gather | bytes 506880 | tf_op jit(solution)/shard_map/all_gather | solution.py:264
  142.7 6.3 fusion.76
  158.4 10.1 all-gather.9.cloned.1.call-done
  168.5 11.6 fusion.70
  180.1 11.7 fusion.73
  191.8 11.7 fusion.74
  203.5 11.7 fusion.75
  215.2 13.9 %multiply_convert_fusion = (bf16[512,3072]{1,0:T(8,128)(2,1)}, f32[512,3072]{1,0:T(8,128)}) fusion(f32[509,3072]{1,0:T(8,128)} %get-tuple-element.169, pred[512]{0:T(512)(128)(4,1)S(1)} %get-tuple-element.203, f32[3072]{0:T(1024)S(1)} %bitcast.292, f32[510,3072]{1,0:T(8,128)} %get-tuple-element.167, pred[512]{0:T(512)(128)(4,1)S(1)} %get-tuple-element.199, ...), kind=kLoop, calls=%fused_computation.31 | loop fusion | flops 25165824 | bytes 34592256 | tf_op jit(solution)/shard_map/convert_element_type | solution.py:309
  235.3 14.0 %multiply_convert_fusion.1 = (bf16[512,3072]{1,0:T(8,128)(2,1)S(1)}, f32[512,3072]{1,0:T(8,128)}) fusion(f32[509,3072]{1,0:T(8,128)} %get-tuple-element.170, pred[512]{0:T(512)(128)(4,1)S(1)} %copy-done.80, f32[3072]{0:T(1024)S(1)} %bitcast.298, f32[510,3072]{1,0:T(8,128)} %get-tuple-element.168, pred[512]{0:T(512)(128)(4,1)S(1)} %copy-done.83, ...), kind=kLoop, calls=%fused_computation.37 | loop fusion | flops 25165824 | bytes 34592256 | tf_op jit(solution)/shard_map/convert_element_type | solution.py:309
  256.0 6.6 fusion.1.delta_ref
  266.0 58.9 %scan_ahead_b.1 = (f32[1,512,3072]{2,1,0:T(8,128)}, f32[1,32,16,3072]{3,2,1,0:T(8,128)}) custom-call(f32[1,512,3072]{2,1,0:T(8,128)} %fusion.1.delta_ref, bf16[1,512,3072]{2,1,0:T(8,128)(2,1)} %bitcast.261, f32[1,512,128]{2,1,0:T(8,128)} %broadcast_in_dim.339.sb_ref, f32[1,512,16,128]{3,2,1,0:T(8,128)} %broadcast_in_dim.340.bx_ref, ...), custom_call_target="tpu_custom_call" | custom-call | tf_op jit(solution)/shard_map/scan_ahead_b/pallas_call | solution.py:318
  324.9 7.4 fusion.delta_ref
  335.8 59.5 %scan_ahead_f.1 = (f32[1,512,3072]{2,1,0:T(8,128)}, f32[1,32,16,3072]{3,2,1,0:T(8,128)}) custom-call(f32[1,512,3072]{2,1,0:T(8,128)} %fusion.delta_ref, bf16[1,512,3072]{2,1,0:T(8,128)(2,1)} %bitcast.263, f32[1,512,128]{2,1,0:T(8,128)} %broadcast_in_dim.332.sb_ref, f32[1,512,16,128]{3,2,1,0:T(8,128)} %broadcast_in_dim.333.bx_ref, ...), custom_call_target="tpu_custom_call" | custom-call | tf_op jit(solution)/shard_map/scan_ahead_f/pallas_call | solution.py:318
  395.3 11.5 fusion.68
  406.8 16.6 %fusion.9 = (bf16[512,3072]{1,0:T(8,128)(2,1)}, bf16[512,3072]{1,0:T(8,128)(2,1)}, f32[1,512,3072]{2,1,0:T(8,128)}) fusion(f32[512,3072]{1,0:T(8,128)} %fusion.68, f32[1,512,3072]{2,1,0:T(8,128)} %get-tuple-element.32, f32[1,512,3072]{2,1,0:T(8,128)} %get-tuple-element.33, bf16[3072,1536]{1,0:T(8,128)(2,1)} %all-gather.17.cloned.1.call-done, ...), kind=kOutput, calls=%fused_computation.18 | convolution fusion | flops 4858576896 | bytes 42480128 | tf_op jit(solution)/shard_map/dot_general | solution.py:246
  426.0 121.5 %scan_back_f.1 = (f32[1,512,3072]{2,1,0:T(8,128)}, bf16[1,512,3072]{2,1,0:T(8,128)(2,1)}, f32[1,512,256]{2,1,0:T(8,128)}, f32[1,512,256]{2,1,0:T(8,128)}, f32[16...) custom-call(f32[1,512,3072]{2,1,0:T(8,128)} %fusion.delta_ref, bf16[1,512,3072]{2,1,0:T(8,128)(2,1)} %bitcast.264, ...), custom_call_target="tpu_custom_call" | custom-call | tf_op jit(solution)/shard_map/scan_back_f/pallas_call | solution.py:339
  552.3 129.3 %scan_back_b.1 = (f32[1,512,3072]{2,1,0:T(8,128)}, bf16[1,512,3072]{2,1,0:T(8,128)(2,1)}, f32[1,512,256]{2,1,0:T(8,128)}, f32[1,512,256]{2,1,0:T(8,128)}, f32[16...) custom-call(f32[1,512,3072]{2,1,0:T(8,128)} %fusion.1.delta_ref, bf16[1,512,3072]{2,1,0:T(8,128)(2,1)} %bitcast.262, ...), custom_call_target="tpu_custom_call" | custom-call | tf_op jit(solution)/shard_map/scan_back_b/pallas_call | solution.py:339
  700.8 8.4 select_reduce_fusion.3
  721.3 6.1 fusion.3
  727.5 25.0 %fusion.72 = (bf16[3072]{0:T(1024)(128)(2,1)S(1)}, bf16[3072]{0:T(1024)(128)(2,1)S(1)}, bf16[3072]{0:T(1024)(128)(2,1)S(1)}, bf16[3072]{0:T(1024)(128)(2,1)S(1)}...) fusion(f32[509,3072]{1,0:T(8,128)} %get-tuple-element.170, ...), kind=kOutput, calls=%fused_computation.182 | convolution fusion | flops 454920192 | bytes 70040576 | tf_op jit(solution)/shard_map/dot_general | solution.py:246
  762.2 5.0 copy.195
  787.5 9.7 convolution_convert_fusion
  809.3 13.9 %add_convert_fusion = bf16[512,3072]{1,0:T(8,128)(2,1)S(1)} fusion(f32[509,3072]{1,0:T(8,128)S(1)} %bitcast.258, f32[510,3072]{1,0:T(8,128)S(1)} %bitcast.259, f32[511,3072]{1,0:T(8,128)S(1)} %bitcast.260, f32[512,3072]{1,0:T(8,128)S(1)} %bitcast.257, f32[509,3072]{1,0:T(8,128)} %slice.442, f32[510,3072]{1,0:T(8,128)} %slice.441, ...), kind=kLoop, calls=%fused_computation.27 | loop fusion | flops 34603008 | bytes 53431296 | tf_op jit(solution)/shard_map/convert_element_type | solution.py:364
  824.9 8.1 convolution_convert_fusion.2
  834.6 10.0 convolution_convert_fusion.1
  844.7 10.9 fusion.87
  855.6 10.1 convolution_add_fusion
  865.8 11.0 select_reduce_fusion.7
  876.9 71.9 %all-gather.2 = bf16[32,2,4608]{2,1,0:T(2,128)(2,1)S(1)} all-gather(bf16[1,2,4608]{2,1,0:T(2,128)(2,1)S(1)} %maximum_bitcast_fusion.3), channel_id=1, replica_groups=mesh['dp'=8,'fsdp'=4] {'dp','fsdp'}, dimensions={0}, use_global_device_ids=true | all-gather | bytes 608256 | tf_op jit(solution)/shard_map/all_gather | solution.py:257
  968.4 61.5 %reduce-scatter.9.cloned.1.call-done = bf16[96,1536]{1,0:T(8,128)(2,1)} async-done(((bf16[3072,1536]{1,0:T(8,128)(2,1)}), bf16[96,1536]{1,0:T(8,128)(2,1)}) %reduce-scatter.9.cloned.1.call-update) | async-done | bytes 294928 | tf_op jit(solution)/shard_map/reduce_scatter | solution.py:329
  1031.7 139.2 %reduce-scatter.5.cloned.1.call-done = bf16[48,3072]{1,0:T(8,128)(2,1)} async-done(((bf16[1536,3072]{1,0:T(8,128)(2,1)}), bf16[48,3072]{1,0:T(8,128)(2,1)}) %reduce-scatter.5.cloned.1.call-update) | async-done | bytes 294928 | tf_op jit(solution)/shard_map/reduce_scatter | solution.py:329
  1170.9 141.0 %reduce-scatter.7.cloned.1.call-done = bf16[48,3072]{1,0:T(8,128)(2,1)} async-done(((bf16[1536,3072]{1,0:T(8,128)(2,1)}), bf16[48,3072]{1,0:T(8,128)(2,1)}) %reduce-scatter.7.cloned.1.call-update) | async-done | bytes 294928 | tf_op jit(solution)/shard_map/reduce_scatter | solution.py:329
  (437 shorter events, 191.1 us)
Async XLA Ops:
  7.2 92.1 %copy-start = (bf16[48,4608]{1,0:T(8,128)(2,1)S(1)}, bf16[48,4608]{1,0:T(8,128)(2,1)}, u32[]{:S(2)}) copy-start(bf16[48,4608]{1,0:T(8,128)(2,1)} %param.28) | copy-start | bytes 1327108
  7.2 135.5 %all-gather.13.cloned.1.call-start = ((), (), s32[]{:S(2)}) async-start(), calls=%async_computation.8 | async-start | bytes 1622016 | tf_op jit(solution)/shard_map/all_gather | solution.py:278
  8.8 159.7 %all-gather.9.cloned.1.call-start = ((), (), s32[]{:S(2)}) async-start(), calls=%async_computation.6 | async-start | bytes 9732096 | tf_op jit(solution)/shard_map/all_gather | solution.py:257
  10.9 218.3 %all-gather.11.cloned.1.call-start = ((), (), s32[]{:S(2)}) async-start(), calls=%async_computation.7 | async-start | bytes 1622016 | tf_op jit(solution)/shard_map/all_gather | solution.py:277
  11.6 383.7 %all-gather.15.cloned.1.call-start = ((), (), s32[]{:S(2)}) async-start(), calls=%async_computation.9 | async-start | bytes 9732096 | tf_op jit(solution)/shard_map/all_gather | solution.py:257
  101.4 55.9 %all-to-all-start = ((f32[32,2,4608]{2,1,0:T(2,128)}), f32[32,2,4608]{2,1,0:T(2,128)S(1)}, u32[]{:S(2)}, u32[]{:S(2)}) async-start(f32[32,2,4608]{2,1,0:T(2,128)} %reshape.482), calls=%async_computation | async-start | bytes 2359296 | tf_op jit(solution)/shard_map/all_to_all | solution.py:284
  104.1 302.7 %all-gather.17.cloned.1.call-start = ((), (), s32[]{:S(2)}) async-start(), calls=%async_computation.10 | async-start | bytes 9732096 | tf_op jit(solution)/shard_map/all_gather | solution.py:257
  104.7 856.4 %reduce-scatter.11.cloned.1.call-start = ((), (), s32[]{:S(2)}) async-start(), calls=%async_computation.14 | async-start | bytes 3244032 | tf_op jit(solution)/shard_map/reduce_scatter | solution.py:329
  132.3 16.6 %copy-start.15 = (f32[3072,16]{0,1:T(8,128)}, f32[3072,16]{0,1:T(8,128)S(1)}, u32[]{:S(2)}) copy-start(f32[3072,16]{0,1:T(8,128)S(1)} %neg.51) | copy-start | bytes 589828
  140.3 74.9 %copy-start.74 = (pred[512]{0:T(512)(128)(4,1)}, pred[512]{0:T(512)(128)(4,1)S(1)}, u32[]{:S(2)}) copy-start(pred[512]{0:T(512)(128)(4,1)S(1)} %get-tuple-element.198) | copy-start | bytes 1540
  140.3 74.9 %copy-start.77 = (pred[512]{0:T(512)(128)(4,1)}, pred[512]{0:T(512)(128)(4,1)S(1)}, u32[]{:S(2)}) copy-start(pred[512]{0:T(512)(128)(4,1)S(1)} %get-tuple-element.199) | copy-start | bytes 1540
  140.3 74.9 %copy-start.89 = (pred[512]{0:T(512)(128)(4,1)}, pred[512]{0:T(512)(128)(4,1)S(1)}, u32[]{:S(2)}) copy-start(pred[512]{0:T(512)(128)(4,1)S(1)} %get-tuple-element.203) | copy-start | bytes 1540
  148.9 19.6 %copy-start.57 = (f32[512]{0:T(512)S(1)}, f32[512]{0:T(512)}, u32[]{:S(2)}) copy-start(f32[512]{0:T(512)} %copy-done.56) | copy-start | bytes 6148
  148.9 19.6 %copy-start.72 = (f32[512]{0:T(512)S(1)}, f32[512]{0:T(512)}, u32[]{:S(2)}) copy-start(f32[512]{0:T(512)} %add_rsqrt_fusion) | copy-start | bytes 6148
  148.9 19.6 %copy-start.92 = (pred[512]{0:T(512)(128)(4,1)S(1)}, pred[512]{0:T(512)(128)(4,1)}, u32[]{:S(2)}) copy-start(pred[512]{0:T(512)(128)(4,1)} %get-tuple-element.160) | copy-start | bytes 1540
  158.4 21.7 %copy-start.66 = (f32[1536]{0:T(1024)}, f32[1536]{0:T(1024)S(1)}, u32[]{:S(2)}) copy-start(f32[1536]{0:T(1024)S(1)} %get-tuple-element.139) | copy-start | bytes 18436
  158.4 21.7 %copy-start.69 = (f32[1536]{0:T(1024)}, f32[1536]{0:T(1024)S(1)}, u32[]{:S(2)}) copy-start(f32[1536]{0:T(1024)S(1)} %get-tuple-element.140) | copy-start | bytes 18436
  158.4 236.9 %copy-start.48 = (f32[1536]{0:T(1024)}, f32[1536]{0:T(1024)S(1)}, u32[]{:S(2)}) copy-start(f32[1536]{0:T(1024)S(1)} %get-tuple-element.142) | copy-start | bytes 18436
  266.0 58.9 %copy-start.11 = (bf16[1,96,3072]{2,1,0:T(8,128)(2,1)S(1)}, bf16[1,96,3072]{2,1,0:T(8,128)(2,1)}, u32[]{:S(2)}) copy-start(bf16[1,96,3072]{2,1,0:T(8,128)(2,1)} %copy.208) | copy-start | bytes 1769476
  335.8 59.6 %copy-start.67 = (f32[1536]{0:T(1024)S(1)}, f32[1536]{0:T(1024)}, u32[]{:S(2)}) copy-start(f32[1536]{0:T(1024)} %copy-done.66) | copy-start | bytes 18436
  335.8 59.6 %copy-start.70 = (f32[1536]{0:T(1024)S(1)}, f32[1536]{0:T(1024)}, u32[]{:S(2)}) copy-start(f32[1536]{0:T(1024)} %copy-done.69) | copy-start | bytes 18436
  335.8 59.6 %copy-start.93 = (pred[512]{0:T(512)(128)(4,1)S(1)}, pred[512]{0:T(512)(128)(4,1)}, u32[]{:S(2)}) copy-start(pred[512]{0:T(512)(128)(4,1)} %get-tuple-element.160) | copy-start | bytes 1540
  406.8 16.6 %copy-start.23 = (f32[512,16]{1,0:T(8,128)S(1)}, f32[512,16]{1,0:T(8,128)}, u32[]{:S(2)}) copy-start(f32[512,16]{1,0:T(8,128)} %copy.178) | copy-start | bytes 98308
  426.0 123.6 %copy-start.22 = (f32[512,16]{1,0:T(8,128)S(1)}, f32[512,16]{1,0:T(8,128)}, u32[]{:S(2)}) copy-start(f32[512,16]{1,0:T(8,128)} %copy.184) | copy-start | bytes 98308
  552.3 130.6 %copy-start.30 = (f32[16,3072]{1,0:T(8,128)S(1)}, f32[16,3072]{1,0:T(8,128)}, u32[]{:S(2)}) copy-start(f32[16,3072]{1,0:T(8,128)} %get-tuple-element.46) | copy-start | bytes 589828
  727.5 25.1 %copy-start.1 = (f32[512,3072]{1,0:T(8,128)}, f32[512,3072]{1,0:T(8,128)S(1)}, u32[]{:S(2)}) copy-start(f32[512,3072]{1,0:T(8,128)S(1)} %fusion.3) | copy-start | bytes 18874372
  786.2 243.7 %reduce-scatter.9.cloned.1.call-start = ((), (), s32[]{:S(2)}) async-start(), calls=%async_computation.13 | async-start | bytes 9732096 | tf_op jit(solution)/shard_map/reduce_scatter | solution.py:329
  797.2 373.7 %reduce-scatter.5.cloned.1.call-start = ((), (), s32[]{:S(2)}) async-start(), calls=%async_computation.11 | async-start | bytes 9732096 | tf_op jit(solution)/shard_map/reduce_scatter | solution.py:329
  833.1 478.9 %reduce-scatter.7.cloned.1.call-start = ((), (), s32[]{:S(2)}) async-start(), calls=%async_computation.12 | async-start | bytes 9732096 | tf_op jit(solution)/shard_map/reduce_scatter | solution.py:329
  844.7 21.0 %slice-start.6 = ((s8[9437184]{0:T(1024)(128)(4,1)}), s8[4194304]{0:T(1024)(128)(4,1)S(1)}, s32[]{:S(2)}) async-start(s8[9437184]{0:T(1024)(128)(4,1)} %bitcast.310), calls=%async_computation.21 | async-start | bytes 8388608
  844.7 21.0 %slice-start.7 = ((s8[9437184]{0:T(1024)(128)(4,1)}), s8[4194304]{0:T(1024)(128)(4,1)S(1)}, s32[]{:S(2)}) async-start(s8[9437184]{0:T(1024)(128)(4,1)} %bitcast.310), calls=%async_computation.22 | async-start | bytes 8388608
  949.9 10.4 all-to-all-start.1
  (83 other events, 516.0 us)
Sparse Core Ops, SparseCore 0:
  11.5 58.3 all-gather.12
  72.6 95.8 all-gather.8
  171.4 53.6 all-gather.10
  227.8 80.4 all-gather.14
  310.9 80.1 all-gather.16
  786.3 101.1 reduce-scatter.10
  893.4 136.4 reduce-scatter.8
  1035.8 135.0 reduce-scatter.4
  1176.9 135.0 reduce-scatter.6

commit v2 on v1

v2 whole, which is shorter than its diff:
```python
import functools

import jax
import jax.numpy as jnp
from jax import lax
from jax.experimental import pallas as pl
from jax.experimental.pallas import tpu as pltpu
from jax.sharding import PartitionSpec as P

NST = 16
SUB = 16
KCONV = 4
LANES = 128
bf16 = jnp.bfloat16
f32 = jnp.float32


def split_hi_lo(v):
    hi = v.astype(bf16)
    lo = (v - hi.astype(f32)).astype(bf16)
    return jnp.concatenate([hi, lo], axis=0)


def block_diag(tiled):
    rows = lax.broadcasted_iota(jnp.int32, tiled.shape, 0)
    cols = lax.broadcasted_iota(jnp.int32, tiled.shape, 1) // NST
    return jnp.where(rows == cols, tiled, 0.0)


PAIR = 256


def fold(v):
    v = block_diag(v)
    v = v[:, :LANES] + v[:, LANES:]
    for by in (64, 32, 16):
        v = v + pltpu.roll(v, by, 1)
    return v


def fwd_kernel(delta_ref, u_ref, sb_ref, bx_ref, ct_ref, a2_ref, skip_ref, y_ref, ck_ref,
               h_scr, dx_scr, du_scr, *, backwards, subs, width):
    lane0 = pl.multiple_of(pl.program_id(2) * width, width)

    @pl.when(pl.program_id(1) == 0)
    def _():
        h_scr[:, pl.ds(lane0, width)] = jnp.zeros((NST, width), f32)

    order = range(SUB - 1, -1, -1) if backwards else range(SUB)

    def sub_step(step, carry):
        sub = subs - 1 - step if backwards else step
        row0 = pl.multiple_of(sub * SUB, SUB)
        rows = pl.ds(row0, SUB)
        sb = sb_ref[rows, :]
        sb = jnp.concatenate([sb] * (PAIR // LANES), axis=1)
        c2 = split_hi_lo(block_diag(ct_ref[rows, :]))
        for p in range(width // PAIR):
            lanes = pl.ds(p * PAIR, PAIR)
            glob = pl.ds(lane0 + p * PAIR, PAIR)
            delta = delta_ref[rows, lanes]
            u = u_ref[rows, lanes].astype(f32)
            du_scr[:, lanes] = delta * u
            dx_scr[:, lanes] = delta + sb
            h = h_scr[:, glob]
            a2 = a2_ref[:, glob]
            ck_ref[sub, :, lanes] = h
            states = [None] * SUB
            for t in order:
                b = bx_ref[row0 + t]
                b = jnp.concatenate([b] * (PAIR // LANES), axis=1)
                h = jnp.exp2(dx_scr[pl.ds(t, 1), lanes] * a2) * h + du_scr[pl.ds(t, 1), lanes] * b
                states[t] = h.astype(bf16)
            h_scr[:, glob] = h
            y2 = jnp.dot(c2, jnp.concatenate(states, axis=0), preferred_element_type=f32)
            y_ref[rows, lanes] = y2[:SUB] + y2[SUB:] + skip_ref[:, glob] * u
        return carry

    lax.fori_loop(0, subs, sub_step, 0)


def bwd_kernel(delta_ref, u_ref, sb_ref, bx_ref, cx_ref, bt_ref, ds_ref, ck_ref, a_ref, a2_ref,
               skip_ref, du_out, dr_out, db_out, dc_out, ga_out, gs_out, gb_out,
               g_scr, dx_scr, du_scr, *, backwards, subs, width):
    first = pl.program_id(1) == 0
    start = jnp.logical_and(first, pl.program_id(0) == 0)
    eg = pl.program_id(2)
    lane0 = pl.multiple_of(eg * width, width)
    wide = pl.ds(lane0, width)

    @pl.when(first)
    def _():
        g_scr[:, wide] = jnp.zeros((NST, width), f32)

    @pl.when(start)
    def _():
        ga_out[:, wide] = jnp.zeros((NST, width), f32)
        gs_out[:, wide] = jnp.zeros((SUB, width), f32)
        gb_out[:, wide] = jnp.zeros((SUB, width), f32)

    @pl.when(eg == 0)
    def _():
        db_out[...] = jnp.zeros_like(db_out)
        dc_out[...] = jnp.zeros_like(dc_out)

    order = list(range(SUB - 1, -1, -1) if backwards else range(SUB))
    nt = (((1,), (1,)), ((), ()))
    twice = lambda v: jnp.concatenate([v] * (PAIR // LANES), axis=1)

    def sub_step(step, carry):
        sub = step if backwards else subs - 1 - step
        row0 = pl.multiple_of(sub * SUB, SUB)
        rows = pl.ds(row0, SUB)
        sb = twice(sb_ref[rows, :])
        b2 = split_hi_lo(block_diag(bt_ref[rows, :]))
        ones = block_diag(jnp.ones((SUB, SUB * NST), f32)).astype(bf16)
        db, dc = jnp.zeros((SUB, SUB * NST), f32), jnp.zeros((SUB, SUB * NST), f32)
        for p in range(width // PAIR):
            lanes = pl.ds(p * PAIR, PAIR)
            glob = pl.ds(lane0 + p * PAIR, PAIR)
            delta = delta_ref[rows, lanes]
            u = u_ref[rows, lanes].astype(f32)
            ds = ds_ref[rows, lanes]
            d_in = delta * u
            du_scr[:, lanes] = d_in
            dx_scr[:, lanes] = delta + sb
            a2 = a2_ref[:, glob]
            h = ck_ref[sub, :, lanes]
            prev, decay, states = [None] * SUB, [None] * SUB, [None] * SUB
            for t in order:
                prev[t] = h
                decay[t] = jnp.exp2(dx_scr[pl.ds(t, 1), lanes] * a2)
                h = decay[t] * h + du_scr[pl.ds(t, 1), lanes] * twice(bx_ref[row0 + t])
                states[t] = h.astype(bf16)
            e2 = lax.dot_general(split_hi_lo(ds), jnp.concatenate(states, axis=0), nt,
                                 preferred_element_type=f32)
            dc = dc + (e2[:SUB] + e2[SUB:])
            a = a_ref[:, glob]
            g = g_scr[:, glob]
            ga = ga_out[:, glob]
            lams, rs = [None] * SUB, [None] * SUB
            for t in reversed(order):
                lam = twice(cx_ref[row0 + t]) * ds_ref[pl.ds(row0 + t, 1), lanes] + g
                lams[t] = lam.astype(bf16)
                g = decay[t] * lam
                r = g * prev[t] * a
                rs[t] = r.astype(bf16)
                ga = ga + dx_scr[pl.ds(t, 1), lanes] * r
            g_scr[:, glob] = g
            ga_out[:, glob] = ga
            lams = jnp.concatenate(lams, axis=0)
            s2 = jnp.dot(b2, lams, preferred_element_type=f32)
            s1 = s2[:SUB] + s2[SUB:]
            dd = jnp.dot(ones, jnp.concatenate(rs, axis=0), preferred_element_type=f32) + u * s1
            du_out[rows, lanes] = skip_ref[:, glob] * ds + delta * s1
            small = delta * (1.0 - delta * (0.5 - delta * (1.0 / 6.0)))
            sig = jnp.where(delta < 0.03, small, 1.0 - jnp.exp(-delta))
            dr = dd * sig
            dr_out[rows, lanes] = dr.astype(bf16)
            gb_out[:, glob] += dr
            gs_out[:, glob] += ds * u
            d2 = lax.dot_general(split_hi_lo(d_in), lams, nt, preferred_element_type=f32)
            db = db + (d2[:SUB] + d2[SUB:])
        db_out[rows, :] += fold(db)
        dc_out[rows, :] += fold(dc)
        return carry

    lax.fori_loop(0, subs, sub_step, 0)


def lane_groups(width_all, widths):
    for width in widths:
        if width_all % width == 0:
            return width
    return width_all


def scan_calls(rows, length, inner, backwards, tblock=128, width=None):
    width = width or lane_groups(inner, (1536, 1024, 512, 256))
    n_t, n_e, subs = length // tblock, inner // width, tblock // SUB
    params = pltpu.CompilerParams(dimension_semantics=("arbitrary",) * 3)

    def specs(flip):
        tb = (lambda i: n_t - 1 - i) if flip else (lambda i: i)
        tok = pl.BlockSpec((None, tblock, width), lambda r, i, e: (r, tb(i), e))
        lane = pl.BlockSpec((None, tblock, LANES), lambda r, i, e: (r, tb(i), 0))
        exp = pl.BlockSpec((None, tblock, NST, LANES), lambda r, i, e: (r, tb(i), 0, 0))
        til = pl.BlockSpec((None, tblock, SUB * NST), lambda r, i, e: (r, tb(i), 0))
        ck = pl.BlockSpec((None, subs, NST, width), lambda r, i, e: (r, tb(i), 0, e))
        full = pl.BlockSpec((NST, inner), lambda r, i, e: (0, 0))
        one = pl.BlockSpec((1, inner), lambda r, i, e: (0, 0))
        return tok, lane, exp, til, ck, full, one

    sds = jax.ShapeDtypeStruct
    tok, lane, exp, til, ck, full, one = specs(backwards)
    fwd = pl.pallas_call(
        functools.partial(fwd_kernel, backwards=backwards, subs=subs, width=width),
        grid=(rows, n_t, n_e),
        in_specs=[tok, tok, lane, exp, til, full, one],
        out_specs=[tok, ck],
        out_shape=[sds((rows, length, inner), f32), sds((rows, length // SUB, NST, inner), f32)],
        scratch_shapes=[pltpu.VMEM((NST, inner), f32)] + [pltpu.VMEM((SUB, width), f32)] * 2,
        compiler_params=params,
        name="scan_ahead_" + ("b" if backwards else "f"),
    )
    tok, lane, exp, til, ck, full, one = specs(not backwards)
    bwd = pl.pallas_call(
        functools.partial(bwd_kernel, backwards=backwards, subs=subs, width=width),
        grid=(rows, n_t, n_e),
        in_specs=[tok, tok, lane, exp, exp, til, tok, ck, full, full, one],
        out_specs=[tok, tok, lane, lane, full, full, full],
        out_shape=[sds((rows, length, inner), f32), sds((rows, length, inner), bf16),
                   sds((rows, length, LANES), f32), sds((rows, length, LANES), f32),
                   sds((NST, inner), f32), sds((SUB, inner), f32), sds((SUB, inner), f32)],
        scratch_shapes=[pltpu.VMEM((NST, inner), f32)] + [pltpu.VMEM((SUB, width), f32)] * 2,
        compiler_params=params,
        name="scan_back_" + ("b" if backwards else "f"),
    )
    return fwd, bwd


def conv_taps(pad_ref, row0, count, sign, masks_ref, lag):
    if lag == 0:
        return pad_ref[pl.ds(row0 + 8, count), :]
    side = 0 if sign > 0 else KCONV - 1
    return pad_ref[pl.ds(row0 + 8 - sign * lag, count), :] * masks_ref[side + lag - 1, pl.ds(row0, count), :]


def fill_padded(pad_ref, length):
    edge = jnp.zeros((8, LANES), f32)
    pad_ref[pl.ds(0, 8), :] = edge
    pad_ref[pl.ds(8 + length, 8), :] = edge


def conv_kernel(x_ref, masks_ref, w_ref, b_ref, u0_ref, u1_ref, pad_scr, *, length, chunk, tiles):
    for tile in range(tiles):
        lanes = pl.ds(tile * LANES, LANES)
        fill_padded(pad_scr, length)
        pad_scr[pl.ds(8, length), :] = x_ref[:, lanes]
        for row0 in range(0, length, chunk):
            for d, (sign, out) in enumerate(((1, u0_ref), (-1, u1_ref))):
                pre = b_ref[d:d + 1, lanes]
                for lag in range(KCONV):
                    tap = conv_taps(pad_scr, row0, chunk, sign, masks_ref, lag)
                    pre = pre + w_ref[d, lag:lag + 1, lanes] * tap
                out[pl.ds(row0, chunk), lanes] = (pre * jax.nn.sigmoid(pre)).astype(bf16)


def conv_back_kernel(x_ref, du0_ref, du1_ref, masks_ref, w_ref, b_ref, dx_ref, gw_ref, gb_ref,
                     pad_scr, dp0_scr, dp1_scr, *, length, chunk, tiles):
    both = ((1, du0_ref, dp0_scr), (-1, du1_ref, dp1_scr))
    for tile in range(tiles):
        lanes = pl.ds(tile * LANES, LANES)
        for ref in (pad_scr, dp0_scr, dp1_scr):
            fill_padded(ref, length)
        pad_scr[pl.ds(8, length), :] = x_ref[:, lanes]
        for d, (sign, du_ref, dp_scr) in enumerate(both):
            sums = [jnp.zeros((8, LANES), f32) for _ in range(KCONV + 1)]
            for row0 in range(0, length, chunk):
                taps = [conv_taps(pad_scr, row0, chunk, sign, masks_ref, lag) for lag in range(KCONV)]
                pre = b_ref[d:d + 1, lanes]
                for lag in range(KCONV):
                    pre = pre + w_ref[d, lag:lag + 1, lanes] * taps[lag]
                sg = jax.nn.sigmoid(pre)
                d_pre = du_ref[pl.ds(row0, chunk), lanes] * (sg * (1.0 + pre * (1.0 - sg)))
                dp_scr[pl.ds(row0 + 8, chunk), :] = d_pre
                for lag in range(KCONV + 1):
                    term = d_pre * taps[lag] if lag < KCONV else d_pre
                    sums[lag] = sums[lag] + jnp.sum(term.reshape(chunk // 8, 8, LANES), axis=0)
            for lag in range(KCONV):
                gw_ref[d, lag:lag + 1, lanes] = jnp.sum(sums[lag], axis=0, keepdims=True)
            gb_ref[d:d + 1, lanes] = jnp.sum(sums[KCONV], axis=0, keepdims=True)
        for row0 in range(0, length, chunk):
            total = jnp.zeros((chunk, LANES), f32)
            for d, (sign, _, dp_scr) in enumerate(both):
                for lag in range(KCONV):
                    total = total + w_ref[d, lag:lag + 1, lanes] * conv_taps(
                        dp_scr, row0, chunk, -sign, masks_ref, lag)
            dx_ref[pl.ds(row0, chunk), lanes] = total.astype(bf16)


def conv_calls(length, inner, width=256, chunk=64):
    if inner % width:
        width = LANES
    tok = pl.BlockSpec((length, width), lambda e: (0, e))
    masks = pl.BlockSpec((2 * (KCONV - 1), length, LANES), lambda e: (0, 0, 0))
    taps = pl.BlockSpec((2, KCONV, width), lambda e: (0, 0, e))
    bias = pl.BlockSpec((2, width), lambda e: (0, e))
    sds = jax.ShapeDtypeStruct
    pad = pltpu.VMEM((length + 16, LANES), f32)
    sizes = dict(length=length, chunk=chunk, tiles=width // LANES)
    params = pltpu.CompilerParams(dimension_semantics=("arbitrary",))
    ahead = pl.pallas_call(
        functools.partial(conv_kernel, **sizes), grid=(inner // width,),
        in_specs=[tok, masks, taps, bias], out_specs=[tok, tok],
        out_shape=[sds((length, inner), bf16)] * 2, scratch_shapes=[pad],
        compiler_params=params, name="conv_ahead")
    back = pl.pallas_call(
        functools.partial(conv_back_kernel, **sizes), grid=(inner // width,),
        in_specs=[tok, tok, tok, masks, taps, bias], out_specs=[tok, taps, bias],
        out_shape=[sds((length, inner), bf16), sds((2, KCONV, inner), f32), sds((2, inner), f32)],
        scratch_shapes=[pad] * 3, compiler_params=params, name="conv_back")
    return ahead, back


EPS = 1e-06
AXES = ("dp", "fsdp")
BIG = 1e30
LOG2E = 1.4426950408889634


def mm(a, b, dims):
    return lax.dot_general(a, b, (dims, ((), ())), preferred_element_type=f32)


def to_all(v):
    owners = lax.axis_size(AXES)
    return lax.all_to_all(jnp.broadcast_to(v[None], (owners,) + v.shape), AXES, 0, 0, tiled=True)


def gather0(v):
    return lax.all_gather(v, AXES, axis=0, tiled=True)


def scatter0(v):
    return lax.psum_scatter(v, AXES, scatter_dimension=0, tiled=True)


def tied(v, *after):
    return lax.optimization_barrier((v,) + after)[0]


def item_masks(ids):
    length = ids.shape[0]
    pad = jnp.full((KCONV - 1,), -1, ids.dtype)
    long = jnp.concatenate([pad, ids, pad])
    shifts = [-lag for lag in range(1, KCONV)] + list(range(1, KCONV))
    rows = [(long[KCONV - 1 + s:KCONV - 1 + s + length] == ids).astype(f32) for s in shifts]
    return jnp.broadcast_to(jnp.stack(rows)[:, :, None], (len(rows), length, LANES))


def body(tokens_in, condition, item_flags, grad_out, in_weight, out_weight, x_projection,
         dt_projection, conv_weight, conv_bias, dt_bias, decay_log, skip_gain, mod_weight, mod_bias):
    length, model = tokens_in.shape[1:]
    owners = lax.axis_size(AXES)
    me = lax.axis_index(AXES)
    inner = in_weight.shape[1] // 2
    own_model = in_weight.shape[0]
    rank = dt_projection.shape[1]

    own_inner = out_weight.shape[0]
    side = jnp.pad(jnp.swapaxes(dt_projection, 1, 2), ((0, 0), (0, 0), (0, LANES - rank)))
    pair = jnp.stack([x_projection, side])
    first = gather0(jnp.concatenate([in_weight[:, :inner], pair.reshape(-1, inner)], axis=0))
    first = first.reshape(owners, -1, inner)
    w_x = first[:, :own_model].reshape(-1, inner)
    pair = jnp.moveaxis(first[:, own_model:].reshape(owners, 2, 2, own_inner, LANES), 0, 2)
    w_xp, w_dt = pair.reshape(2, 2, inner, LANES)
    w_z = gather0(in_weight[:, inner:])
    w_o = gather0(out_weight)

    cond = condition[0].astype(f32)
    act = jax.nn.silu(cond).astype(bf16)
    smalls = (act, conv_weight, conv_bias, dt_bias, decay_log, skip_gain, mod_bias)
    flat = jnp.concatenate([v.reshape(-1) for v in smalls])
    flat = jnp.pad(flat, (0, -flat.shape[0] % (8 * LANES)))
    everyone = to_all(flat.reshape(-1, LANES)).reshape(owners, -1)
    parts, at = [], 0
    for v in smalls:
        parts.append(everyone[:, at:at + v.size].reshape((owners,) + v.shape))
        at += v.size
    act_all = parts[0].reshape(owners * 2, model)
    join = lambda v, dim: jnp.moveaxis(v, 0, dim).reshape(
        v.shape[1:dim + 1] + (owners * v.shape[dim + 1],) + v.shape[dim + 2:]).astype(f32)
    conv_w, conv_b, dt_b = join(parts[1], 2), join(parts[2], 1), join(parts[3], 1)
    log_rate, skip = join(parts[4], 1), join(parts[5], 1)
    modb = parts[6].reshape(-1).astype(f32)

    act_own = lax.dynamic_slice(act_all, (0, me * own_model), (owners * 2, own_model))
    partial = mm(act_own, mod_weight, ((1,), (0,))).reshape(owners, 2, -1)
    mods = jnp.sum(lax.all_to_all(partial, AXES, 0, 0, tiled=True), axis=0) + modb

    flags = item_flags[0]
    ids = jnp.cumsum(flags, dtype=jnp.int32) - 1
    second = (ids == 1)[:, None]
    pick = lambda v: jnp.where(second, v[1], v[0])
    shift, scale, gate = (mods[:, i * model:(i + 1) * model] for i in range(3))
    masks = item_masks(ids)

    x = tokens_in[0].astype(f32)
    mean = jnp.mean(x, axis=1, keepdims=True)
    centered = x - mean
    inv = lax.rsqrt(jnp.mean(centered * centered, axis=1, keepdims=True) + EPS)
    normed = centered * inv
    hidden = (normed * (1.0 + pick(scale)) + pick(shift)).astype(bf16)
    xs = mm(hidden, w_x, ((1,), (0,)))

    g = grad_out[0].astype(f32)
    d_branch = (g * pick(gate)).astype(bf16)

    starts = flags.astype(f32)
    starts_b = jnp.concatenate([starts[1:], jnp.ones((1,), f32)])
    calls = [scan_calls(1, length, inner, bool(d)) for d in range(2)]
    conv_ahead, conv_back = conv_calls(length, inner)
    wide = lambda v: jnp.broadcast_to(v[None, :, :, None], (1, length, NST, LANES))
    tile = lambda v: jnp.tile(v, (1, SUB))[None]
    us = conv_ahead(xs, masks, conv_w, conv_b)
    kept = []
    for d in range(2):
        u = us[d]
        proj = mm(u, w_xp[d], ((1,), (0,)))
        dt_low = proj.astype(bf16)
        b_m, c_m = proj[:, rank:rank + NST], proj[:, rank + NST:]
        delta = jax.nn.softplus(mm(dt_low, w_dt[d], ((1,), (1,))) + dt_b[d])
        rate = -jnp.exp(log_rate[d]).T
        rate2 = rate * LOG2E
        sb = jnp.broadcast_to((BIG * (starts_b if d else starts))[None, :, None], (1, length, LANES))
        b_wide = wide(b_m)
        y, ck = calls[d][0](delta[None], u[None], sb, b_wide, tile(c_m), rate2, skip[d][None])
        kept.append((u, dt_low, b_m, c_m, delta, rate, rate2, sb, b_wide, y[0], ck))
    both = kept[0][9] + kept[1][9]
    z = mm(tied(hidden, both), w_z, ((1,), (0,)))
    sig_z = jax.nn.sigmoid(z)
    silu_z = z * sig_z
    gated = (both * silu_z).astype(bf16)
    grad_out_w = mm(gated, d_branch, ((0,), (0,))).astype(bf16)

    d_gated = mm(d_branch, w_o, ((1,), (1,)))
    d_scan = d_gated * silu_z
    d_z = (d_gated * both * sig_z * (1.0 + z * (1.0 - sig_z))).astype(bf16)
    grad_in_z = mm(hidden, d_z, ((0,), (0,))).astype(bf16)
    d_scan, grad_out_w, grad_in_z = lax.optimization_barrier((d_scan, grad_out_w, grad_in_z))
    grad_out_w = scatter0(grad_out_w)
    grad_in_z = scatter0(grad_in_z)
    branch = mm(gated, w_o, ((1,), (0,)))
    block_out = (x + pick(gate) * branch).astype(bf16)
    d_gate = g * branch
    lane = lax.broadcasted_iota(jnp.int32, (1, LANES), 1)
    d_us, g_xps, g_dts, g_dbs, g_als, g_sks = [], [], [], [], [], []
    for d in range(2):
        u, dt_low, b_m, c_m, delta, rate, rate2, sb, b_wide, _, ck = kept[d]
        du, dr, db, dc, ga, gs, gb = calls[d][1](
            delta[None], u[None], sb, b_wide, wide(c_m), tile(b_m), d_scan[None], ck, rate, rate2,
            skip[d][None])
        dr = dr[0]
        d_low = mm(dr, w_dt[d], ((1,), (0,)))
        d_proj = jnp.where(lane < rank, d_low, jnp.where(lane < rank + NST, db[0], dc[0])).astype(bf16)
        g_dts.append(mm(dr, dt_low, ((0,), (0,))))
        g_xps.append(mm(u, d_proj, ((0,), (0,))))
        d_us.append(du[0] + mm(d_proj, w_xp[d], ((1,), (1,))))
        g_dbs.append(jnp.sum(gb, axis=0))
        g_als.append(ga.T)
        g_sks.append(jnp.sum(gs, axis=0))
    d_xs, g_cw, g_cb = conv_back(xs, d_us[0], d_us[1], masks, conv_w, conv_b)
    grad_in_x = mm(hidden, d_xs, ((0,), (0,))).astype(bf16)

    wide_rows = [jnp.stack(v).astype(bf16).reshape(2, owners, own_inner, LANES) for v in (g_xps, g_dts)]
    wide_rows = jnp.concatenate([jnp.moveaxis(v, 1, 0).reshape(owners, -1, LANES) for v in wide_rows], axis=1)
    stacked = [g_cw, g_cb, jnp.stack(g_dbs), jnp.stack(g_als), jnp.stack(g_sks)]
    dims = (2, 1, 1, 1, 1)
    pieces, shapes = [], []
    for v, dim in zip(stacked, dims):
        shape = v.shape[:dim] + (owners, v.shape[dim] // owners) + v.shape[dim + 1:]
        pieces.append(jnp.moveaxis(v.reshape(shape), dim, 0).reshape(owners, -1).astype(bf16))
        shapes.append(v.shape[:dim] + (v.shape[dim] // owners,) + v.shape[dim + 1:])
    packed = jnp.concatenate(pieces, axis=1)
    packed = jnp.pad(packed, ((0, 0), (0, -packed.shape[1] % (16 * LANES))))
    packed = jnp.concatenate([wide_rows, packed.reshape(owners, -1, LANES)], axis=1)
    grad_in_x = scatter0(tied(grad_in_x, grad_in_z))
    received = lax.all_to_all(packed, AXES, 0, 0, tiled=True)
    mine = jnp.sum(received.astype(f32), axis=0)
    grad_in = jnp.concatenate([grad_in_x, grad_in_z], axis=1).astype(f32)
    both_rows = mine[:4 * own_inner].reshape(2, 2, own_inner, LANES)
    g_xp = both_rows[0]
    g_dt = jnp.swapaxes(both_rows[1][..., :rank], 1, 2)
    mine = mine[4 * own_inner:].reshape(-1)
    small_grads, at = [], 0
    for shape in shapes:
        count = 1
        for n in shape:
            count *= n
        small_grads.append(mine[at:at + count].reshape(shape))
        at += count

    d_hidden = mm(d_xs, w_x, ((1,), (1,))) + mm(d_z, w_z, ((1,), (1,)))
    scale_tok = 1.0 + pick(scale)
    d_n = d_hidden * scale_tok
    m1 = jnp.mean(d_n, axis=1, keepdims=True)
    m2 = jnp.mean(d_n * normed, axis=1, keepdims=True)
    grad_tokens = g + (d_n - m1 - normed * m2) * inv
    by_item = lambda v: jnp.stack([jnp.sum(jnp.where(second, 0.0, v), axis=0),
                                   jnp.sum(jnp.where(second, v, 0.0), axis=0)])
    d_mods = jnp.concatenate([by_item(d_hidden), by_item(d_hidden * normed), by_item(d_gate)], axis=1)
    d_mods_all = to_all(d_mods.astype(bf16)).reshape(owners * 2, -1)
    grad_mod_w = mm(act_own, d_mods_all, ((0,), (0,)))
    own_b = mod_bias.shape[0]
    grad_mod_b = jnp.sum(
        lax.dynamic_slice(d_mods_all, (0, me * own_b), (owners * 2, own_b)).astype(f32), axis=0)
    d_act = mm(d_mods_all, mod_weight, ((1,), (1,))).reshape(owners, 2, own_model)
    d_act = lax.all_to_all(d_act, AXES, 0, 0, tiled=True)
    d_act = jnp.moveaxis(d_act, 0, 1).reshape(2, model)
    sc = jax.nn.sigmoid(cond)
    grad_cond = d_act * sc * (1.0 + cond * (1.0 - sc))
    g_cw, g_cb, g_db, g_al, g_sk = small_grads
    return (block_out[None], grad_tokens[None], grad_cond[None], grad_in, grad_out_w.astype(f32), g_xp,
            g_dt, g_cw, g_cb, g_db, g_al, g_sk, grad_mod_w, grad_mod_b)


def solution(mesh):
    row3, row2, row1 = P(AXES, None, None), P(AXES, None), P(AXES)
    mid3, mid2, last3 = P(None, AXES, None), P(None, AXES), P(None, None, AXES)
    weights = (row2, row2, mid3, last3, last3, mid2, mid2, mid3, mid2, row2, row1)
    return jax.shard_map(
        body, mesh=mesh, in_specs=(row3, row3, row2, row3) + weights,
        out_specs=(row3, row3, row3) + weights, check_vma=False)
```

time: 1330 us -> 879 us (0.66)
  blocking collectives: 152 us -> 0 us
  Pallas kernels: 369 us -> 282 us
  local copies, waits for them, and re-layouts: 177 us -> 93.2 us
  waiting for transfers between devices: 354 us -> 271 us
  other arithmetic: 79.2 us -> 47 us
  matrix products: 168 us -> 140 us
  starting transfers between devices: 5.59 us -> 24.4 us
    reduce_scatter x4 -> x3, waiting for transfers between devices: 342 us -> 20 us  [scatter0(): return lax.psum_scatter(v, AXES, scatter_dimension=0, tiled=True)]
    all_gather x2 -> x0, blocking collectives: 152 us -> none  [the longest x1 80 us: body(): everyone = lax.all_gather(flat, AXES, axis=0, tiled=False)]
    all_to_all x0 -> x3, waiting for transfers between devices: none -> 119 us  [the longest x1 101 us: body(): received = lax.all_to_all(packed, AXES, 0, 0, tiled=True)]
    all_gather x5 -> x3, waiting for transfers between devices: 10.2 us -> 103 us  [gather0(): return lax.all_gather(v, AXES, axis=0, tiled=True)]
    pallas_call x2, Pallas kernels: 251 us -> 178 us  [body(): calls[d][1]]
    pallas_call x2, Pallas kernels: 118 us -> 68.9 us  [body(): calls[d][0]]
    slice x19 -> x12, local copies, waits for them, and re-layouts: 58.6 us -> 19.9 us  [the longest x1 8.6 us: body(): w_x = first[:, :own_model].reshape(-1, inner)]
    convert_element_type x4 -> x3, other arithmetic: 43.7 us -> 6.74 us  [the longest x1 2.86 us: body(): hidden = (normed * (1.0 + pick(scale)) + pick(shift)).astype(bf16)]
  transfers between devices with their start and end apart: 11 -> 11, of which waited for: 5 -> 8; matrix products, arithmetic and copies ran while one was open for 21% -> 28% of each run, Pallas kernels for 9% -> 32%
where the time goes in v2:
time: 879 us; the launch traced here: 874 us
  Pallas kernels  282 us (32%)
  waiting for transfers between devices  271 us (31%)
  matrix products  140 us (16%)
  local copies, waits for them, and re-layouts  93.2 us (11%)
  other arithmetic  47 us (5%)
  starting transfers between devices  24.4 us (3%)
  between operations  15.6 us (2%)
    pallas_call x2, Pallas kernels, body(): calls[d][1]  178 us
    dot_general x24, matrix products, mm(): return lax.dot_general(a, b, (dims, ((), ())), preferred_element_type=f32)  140 us
    all_gather x3, waiting for transfers between devices, gather0(): return lax.all_gather(v, AXES, axis=0, tiled=True)  103 us
    all_to_all x1, waiting for transfers between devices, body(): received = lax.all_to_all(packed, AXES, 0, 0, tiled=True)  101 us
    pallas_call x2, Pallas kernels, body(): calls[d][0]  68.9 us
    all_to_all x1, waiting for transfers between devices, body(): lax.all_to_all(partial, AXES, 0, 0, tiled=True)  24 us
    pallas_call x1, Pallas kernels, body(): d_xs, g_cw, g_cb = conv_back(xs, d_us[0], d_us[1], masks, conv_w, conv_b)  22.5 us
    reduce_scatter x3, waiting for transfers between devices, scatter0(): return lax.psum_scatter(v, AXES, scatter_dimension=0, tiled=True)  20 us
  transfers between devices with their start and end apart: 11, of which 8 were waited for; matrix products, arithmetic and copies ran while one was open for 28% of the time, Pallas kernels for 32%

profile of v2, /device:TPU:0, one launch (start us, length us, event | category | flops | bytes accessed | tf_op | source)
XLA Modules:
  0.0 873.9 jit_solution(12974621039576947784)
XLA Ops:
  15.0 7.3 all-to-all-start
  25.9 17.5 %all-to-all-done = bf16[32,64,128]{2,1,0:T(8,128)(2,1)S(1)} async-done(((bf16[32,64,128]{2,1,0:T(8,128)(2,1)}), bf16[32,64,128]{2,1,0:T(8,128)(2,1)S(1)}, u32[]{:S(2)}, u32[]{:S(2)}) %all-to-all-start) | async-done | bytes 524320 | tf_op jit(solution)/shard_map/all_to_all | solution.py:318
  72.2 24.0 %all-to-all-done.1 = f32[32,2,4608]{2,1,0:T(2,128)S(1)} async-done(((f32[32,2,4608]{2,1,0:T(2,128)}), f32[32,2,4608]{2,1,0:T(2,128)S(1)}, u32[]{:S(2)}, u32[]{:S(2)}) %all-to-all-start.1) | async-done | bytes 1179680 | tf_op jit(solution)/shard_map/all_to_all | solution.py:381
  99.6 15.3 %all-gather.8.cloned.1.call-done = bf16[3072,1536]{1,0:T(8,128)(2,1)} async-done(((bf16[96,1536]{1,0:T(8,128)(2,1)}), bf16[3072,1536]{1,0:T(8,128)(2,1)}) %all-gather.8.cloned.1.call-update) | async-done | bytes 9437200 | tf_op jit(solution)/shard_map/all_gather | solution.py:322
  114.9 9.9 %fusion.60 = f32[512,3072]{1,0:T(8,128)} fusion(bf16[3072,1536]{1,0:T(8,128)(2,1)} %all-gather.8.cloned.1.call-done, bf16[1,512,1536]{2,1,0:T(8,128)(2,1)} %param.18, f32[1536]{0:T(1024)S(1)} %get-tuple-element.153, f32[1536]{0:T(1024)S(1)} %get-tuple-element.148, pred[512]{0:T(512)(128)(4,1)S(1)} %copy-done.52), kind=kOutput, calls=%fused_computation.86 | convolution fusion | flops 4834983936 | bytes 17314304 | tf_op jit(solution)/shard_map/dot_general | solution.py:313
  124.7 87.3 %all-gather.4.cloned.1.call-done = bf16[2048,3072]{1,0:T(8,128)(2,1)} async-done(((bf16[64,3072]{1,0:T(8,128)(2,1)}), bf16[2048,3072]{1,0:T(8,128)(2,1)}) %all-gather.4.cloned.1.call-update) | async-done | bytes 12582928 | tf_op jit(solution)/shard_map/all_gather | solution.py:322
  212.0 8.6 slice.271
  224.6 5.8 reshape.556
  230.5 11.5 %fusion.31.x_ref = f32[512,3072]{1,0:T(8,128)} fusion(bf16[1536,3072]{1,0:T(8,128)(2,1)} %bitcast.253, bf16[1,512,1536]{2,1,0:T(8,128)(2,1)S(1)} %copy-done.3, f32[1536]{0:T(1024)S(1)} %get-tuple-element.149, f32[1536]{0:T(1024)S(1)} %get-tuple-element.150, f32[1536]{0:T(1024)S(1)} %get-tuple-element.151, f32[1536]{0:T(1024)S(1)} %get-tuple-element.152, ...), kind=kOutput, calls=%fused_computation.61 | convolution fusion | flops 4838916096 | bytes 17330688 | tf_op jit(solution)/shard_map/dot_general | solution.py:313
  243.6 13.3 %conv_ahead.1 = (bf16[512,3072]{1,0:T(8,128)(2,1)}, bf16[512,3072]{1,0:T(8,128)(2,1)}) custom-call(f32[512,3072]{1,0:T(8,128)} %fusion.31.x_ref, f32[6,512,128]{2,1,0:T(8,128)} %broadcast_in_dim.221.masks_ref, f32[2,4,3072]{2,1,0:T(4,128)} %reshape.568.w_ref, f32[2,3072]{1,0:T(2,128)} %reshape.569.b_ref), custom_call_target="tpu_custom_call" | custom-call | tf_op jit(solution)/shard_map/conv_ahead/pallas_call | solution.py:407
  269.7 7.7 fusion.1.delta_ref
  280.8 35.5 %scan_ahead_b.1 = (f32[1,512,3072]{2,1,0:T(8,128)}, f32[1,32,16,3072]{3,2,1,0:T(8,128)}) custom-call(f32[1,512,3072]{2,1,0:T(8,128)} %fusion.1.delta_ref, bf16[1,512,3072]{2,1,0:T(8,128)(2,1)} %bitcast.242, f32[1,512,128]{2,1,0:T(8,128)} %broadcast_in_dim.228.sb_ref, f32[1,512,16,128]{3,2,1,0:T(8,128)} %broadcast_in_dim.229.bx_ref, ...), custom_call_target="tpu_custom_call" | custom-call | tf_op jit(solution)/shard_map/scan_ahead_b/pallas_call | solution.py:419
  316.4 6.2 fusion.delta_ref
  326.2 33.4 %scan_ahead_f.1 = (f32[1,512,3072]{2,1,0:T(8,128)}, f32[1,32,16,3072]{3,2,1,0:T(8,128)}) custom-call(f32[1,512,3072]{2,1,0:T(8,128)} %fusion.delta_ref, bf16[1,512,3072]{2,1,0:T(8,128)(2,1)} %bitcast.240, f32[1,512,128]{2,1,0:T(8,128)} %broadcast_in_dim.224.sb_ref, f32[1,512,16,128]{3,2,1,0:T(8,128)} %broadcast_in_dim.225.bx_ref, ...), custom_call_target="tpu_custom_call" | custom-call | tf_op jit(solution)/shard_map/scan_ahead_f/pallas_call | solution.py:419
  359.5 8.9 %add_bitcast_fusion = f32[512,3072]{1,0:T(8,128)} fusion(f32[1,512,3072]{2,1,0:T(8,128)} %get-tuple-element.43, f32[1,512,3072]{2,1,0:T(8,128)} %get-tuple-element.45), kind=kLoop, calls=%fused_computation.14 | loop fusion | flops 1572864 | bytes 18874368 | tf_op jit(solution)/shard_map/add | solution.py:421
  368.5 15.2 %multiply_convert_fusion = (bf16[512,3072]{1,0:T(8,128)(2,1)S(1)}, f32[512,3072]{1,0:T(8,128)}, bf16[512,3072]{1,0:T(8,128)(2,1)}) fusion(f32[512,3072]{1,0:T(8,128)} %fusion.60, f32[512,3072]{1,0:T(8,128)} %add_bitcast_fusion, bf16[512,1536]{1,0:T(8,128)(2,1)} %fusion.12, bf16[1536,3072]{1,0:T(8,128)(2,1)} %all-gather.6.cloned.1.call-done), kind=kOutput, calls=%fused_computation.10 | convolution fusion | flops 4853858304 | bytes 36175872 | tf_op jit(solution)/shard_map/dot_general | solution.py:313
  385.4 7.5 convolution_convert_fusion.1
  392.9 9.6 %convolution_convert_fusion.2 = bf16[3072,1536]{1,0:T(8,128)(2,1)} fusion(bf16[512,3072]{1,0:T(8,128)(2,1)} %get-tuple-element.164, bf16[1,512,1536]{2,1,0:T(8,128)(2,1)} %param.18, f32[1536]{0:T(1024)S(1)} %get-tuple-element.153, f32[1536]{0:T(1024)S(1)} %get-tuple-element.148, pred[512]{0:T(512)(128)(4,1)S(1)} %copy-done.53), kind=kOutput, calls=%fused_computation.4 | convolution fusion | flops 4839702528 | bytes 14168576 | tf_op jit(solution)/shard_map/dot_general | solution.py:313
  410.7 87.0 %scan_back_b.1 = (f32[1,512,3072]{2,1,0:T(8,128)}, bf16[1,512,3072]{2,1,0:T(8,128)(2,1)}, f32[1,512,128]{2,1,0:T(8,128)}, f32[1,512,128]{2,1,0:T(8,128)}, f32[16...) custom-call(f32[1,512,3072]{2,1,0:T(8,128)} %fusion.1.delta_ref, bf16[1,512,3072]{2,1,0:T(8,128)(2,1)} %bitcast.243, ...), custom_call_target="tpu_custom_call" | custom-call | tf_op jit(solution)/shard_map/scan_back_b/pallas_call | solution.py:442
  497.8 4.7 copy.206
  505.1 90.5 %scan_back_f.1 = (f32[1,512,3072]{2,1,0:T(8,128)}, bf16[1,512,3072]{2,1,0:T(8,128)(2,1)}, f32[1,512,128]{2,1,0:T(8,128)}, f32[1,512,128]{2,1,0:T(8,128)}, f32[16...) custom-call(f32[1,512,3072]{2,1,0:T(8,128)} %fusion.delta_ref, bf16[1,512,3072]{2,1,0:T(8,128)(2,1)} %bitcast.241, ...), custom_call_target="tpu_custom_call" | custom-call | tf_op jit(solution)/shard_map/scan_back_f/pallas_call | solution.py:442
  595.6 4.8 copy.204
  615.8 6.5 bitcast_add_fusion.du1_ref
  625.9 22.5 %conv_back.1 = (bf16[512,3072]{1,0:T(8,128)(2,1)}, f32[2,4,3072]{2,1,0:T(4,128)}, f32[2,3072]{1,0:T(2,128)}) custom-call(f32[512,3072]{1,0:T(8,128)} %fusion.31.x_ref, f32[512,3072]{1,0:T(8,128)} %bitcast_add_fusion.1.du0_ref, f32[512,3072]{1,0:T(8,128)} %bitcast_add_fusion.du1_ref, f32[6,512,128]{2,1,0:T(8,128)} %broadcast_in_dim.221.masks_ref, ...), custom_call_target="tpu_custom_call" | custom-call | tf_op jit(solution)/shard_map/conv_back/pallas_call | solution.py:454
  648.4 11.3 %fusion.92 = f32[512,1536]{1,0:T(8,128)} fusion(bf16[512,3072]{1,0:T(8,128)(2,1)} %get-tuple-element.58, bf16[1536,3072]{1,0:T(8,128)(2,1)} %bitcast.254), kind=kOutput, calls=%fused_computation.174 | convolution fusion | flops 4831838208 | bytes 15728640 | tf_op jit(solution)/shard_map/dot_general | solution.py:313
  659.7 7.6 convolution_convert_fusion
  667.5 10.1 %convolution_add_fusion = f32[512,1536]{1,0:T(8,128)S(1)} fusion(f32[512,1536]{1,0:T(8,128)} %fusion.92, bf16[512,3072]{1,0:T(8,128)(2,1)} %copy-done.64, bf16[1536,3072]{1,0:T(8,128)(2,1)} %all-gather.6.cloned.1.call-done), kind=kOutput, calls=%fused_computation.33 | convolution fusion | flops 4832624640 | bytes 18874368 | tf_op jit(solution)/shard_map/dot_general | solution.py:313
  677.7 12.4 %select_reduce_fusion.3 = (bf16[1536]{0:T(1024)(128)(2,1)S(1)}, bf16[1536]{0:T(1024)(128)(2,1)S(1)}, f32[512]{0:T(512)}, f32[512]{0:T(512)}, bf16[1536]{0:T(1024...) fusion(f32[512,1536]{1,0:T(8,128)S(1)} %convolution_add_fusion,, ...), kind=kOutput, calls=%fused_computation.54 | convolution fusion | flops 4853848064 | bytes 20498944 | tf_op jit(solution)/shard_map/dot_general | solution.py:313
  691.4 4.5 all-to-all-start.2
  712.3 5.0 all-to-all-start.3
  736.4 100.6 %all-to-all-done.4 = bf16[32,432,128]{2,1,0:T(8,128)(2,1)} async-done(((bf16[32,432,128]{2,1,0:T(8,128)(2,1)}), bf16[32,432,128]{2,1,0:T(8,128)(2,1)}, u32[]{:S(2)}, u32[]{:S(2)}) %all-to-all-start.4) | async-done | bytes 3538976 | tf_op jit(solution)/shard_map/all_to_all | solution.py:470
  844.8 20.0 %reduce-scatter.6.cloned.1.call-done = bf16[48,3072]{1,0:T(8,128)(2,1)} async-done(((bf16[1536,3072]{1,0:T(8,128)(2,1)}), bf16[48,3072]{1,0:T(8,128)(2,1)}) %reduce-scatter.6.cloned.1.call-update) | async-done | bytes 294928 | tf_op jit(solution)/shard_map/reduce_scatter | solution.py:326
  (335 shorter events, 146.0 us)
Async XLA Ops:
  7.2 38.2 %copy-start = (bf16[48,4608]{1,0:T(8,128)(2,1)S(1)}, bf16[48,4608]{1,0:T(8,128)(2,1)}, u32[]{:S(2)}) copy-start(bf16[48,4608]{1,0:T(8,128)(2,1)} %param.28) | copy-start | bytes 1327108
  7.3 15.1 %copy-start.40 = (s32[1,512]{1,0:T(1,128)S(1)}, s32[1,512]{1,0:T(1,128)}, u32[]{:S(2)}) copy-start(s32[1,512]{1,0:T(1,128)} %param.17) | copy-start | bytes 6148
  7.3 16.3 %copy-start.3 = (bf16[1,512,1536]{2,1,0:T(8,128)(2,1)S(1)}, bf16[1,512,1536]{2,1,0:T(8,128)(2,1)}, u32[]{:S(2)}) copy-start(bf16[1,512,1536]{2,1,0:T(8,128)(2,1)} %param.15) | copy-start | bytes 4718596
  7.3 107.6 %all-gather.8.cloned.1.call-start = ((), (), s32[]{:S(2)}) async-start(), calls=%async_computation.10 | async-start | bytes 9732096 | tf_op jit(solution)/shard_map/all_gather | solution.py:322
  8.0 204.0 %all-gather.4.cloned.1.call-start = ((), (), s32[]{:S(2)}) async-start(), calls=%async_computation.8 | async-start | bytes 12976128 | tf_op jit(solution)/shard_map/all_gather | solution.py:322
  12.6 355.8 %all-gather.6.cloned.1.call-start = ((), (), s32[]{:S(2)}) async-start(), calls=%async_computation.9 | async-start | bytes 9732096 | tf_op jit(solution)/shard_map/all_gather | solution.py:322
  15.0 28.4 %all-to-all-start = ((bf16[32,64,128]{2,1,0:T(8,128)(2,1)}), bf16[32,64,128]{2,1,0:T(8,128)(2,1)S(1)}, u32[]{:S(2)}, u32[]{:S(2)}) async-start(bf16[32,64,128]{2,1,0:T(8,128)(2,1)} %broadcast_in_dim.209), calls=%async_computation | async-start | bytes 1048576 | tf_op jit(solution)/shard_map/all_to_all | solution.py:318
  25.3 205.1 %copy-start.35 = (f32[512]{0:T(512)}, f32[512]{0:T(512)S(1)}, u32[]{:S(2)}) copy-start(f32[512]{0:T(512)S(1)} %broadcast_multiply_fusion.5) | copy-start | bytes 6148
  25.9 204.6 %copy-start.41 = (f32[512]{0:T(512)}, f32[512]{0:T(512)S(1)}, u32[]{:S(2)}) copy-start(f32[512]{0:T(512)S(1)} %add_rsqrt_fusion) | copy-start | bytes 6148
  47.5 48.7 %all-to-all-start.1 = ((f32[32,2,4608]{2,1,0:T(2,128)}), f32[32,2,4608]{2,1,0:T(2,128)S(1)}, u32[]{:S(2)}, u32[]{:S(2)}) async-start(f32[32,2,4608]{2,1,0:T(2,128)} %reshape.552), calls=%async_computation.1 | async-start | bytes 2359296 | tf_op jit(solution)/shard_map/all_to_all | solution.py:381
  51.0 616.3 %reduce-scatter.4.cloned.1.call-start = ((), (), s32[]{:S(2)}) async-start(), calls=%async_computation.11 | async-start | bytes 9732096 | tf_op jit(solution)/shard_map/reduce_scatter | solution.py:326
  67.0 47.9 %copy-start.52 = (pred[512]{0:T(512)(128)(4,1)S(1)}, pred[512]{0:T(512)(128)(4,1)}, u32[]{:S(2)}) copy-start(pred[512]{0:T(512)(128)(4,1)} %get-tuple-element.160) | copy-start | bytes 1540
  69.8 54.9 %copy-start.9 = (f32[3072,16]{0,1:T(8,128)}, f32[3072,16]{0,1:T(8,128)S(1)}, u32[]{:S(2)}) copy-start(f32[3072,16]{0,1:T(8,128)S(1)} %neg.36) | copy-start | bytes 589828
  96.7 133.8 %copy-start.30 = (f32[1536]{0:T(1024)}, f32[1536]{0:T(1024)S(1)}, u32[]{:S(2)}) copy-start(f32[1536]{0:T(1024)S(1)} %get-tuple-element.151) | copy-start | bytes 18436
  96.7 133.8 %copy-start.32 = (f32[1536]{0:T(1024)}, f32[1536]{0:T(1024)S(1)}, u32[]{:S(2)}) copy-start(f32[1536]{0:T(1024)S(1)} %get-tuple-element.152) | copy-start | bytes 18436
  96.7 296.2 %copy-start.48 = (f32[1536]{0:T(1024)}, f32[1536]{0:T(1024)S(1)}, u32[]{:S(2)}) copy-start(f32[1536]{0:T(1024)S(1)} %get-tuple-element.148) | copy-start | bytes 18436
  96.7 296.2 %copy-start.50 = (f32[1536]{0:T(1024)}, f32[1536]{0:T(1024)S(1)}, u32[]{:S(2)}) copy-start(f32[1536]{0:T(1024)S(1)} %get-tuple-element.153) | copy-start | bytes 18436
  230.5 11.5 %copy-start.34 = (f32[6,512]{1,0:T(8,128)S(1)}, f32[6,512]{1,0:T(8,128)}, u32[]{:S(2)}) copy-start(f32[6,512]{1,0:T(8,128)} %stack.126) | copy-start | bytes 36868
  280.8 35.5 %copy-start.16 = (f32[512,128]{0,1:T(8,128)S(1)}, f32[512,128]{0,1:T(8,128)}, u32[]{:S(2)}) copy-start(f32[512,128]{0,1:T(8,128)} %copy-done.15) | copy-start | bytes 786436
  280.8 35.5 %copy-start.45 = (f32[3072]{0:T(1024)S(1)}, f32[3072]{0:T(1024)}, u32[]{:S(2)}) copy-start(f32[3072]{0:T(1024)} %add.145) | copy-start | bytes 36868
  368.5 16.9 %copy-start.10 = (bf16[512,1536]{1,0:T(8,128)(2,1)S(1)}, bf16[512,1536]{1,0:T(8,128)(2,1)}, u32[]{:S(2)}) copy-start(bf16[512,1536]{1,0:T(8,128)(2,1)} %fusion.12) | copy-start | bytes 4718596
  402.6 440.4 %reduce-scatter.8.cloned.1.call-start = ((), (), s32[]{:S(2)}) async-start(), calls=%async_computation.13 | async-start | bytes 9732096 | tf_op jit(solution)/shard_map/reduce_scatter | solution.py:326
  403.2 461.6 %reduce-scatter.6.cloned.1.call-start = ((), (), s32[]{:S(2)}) async-start(), calls=%async_computation.12 | async-start | bytes 9732096 | tf_op jit(solution)/shard_map/reduce_scatter | solution.py:326
  648.4 11.3 %copy-start.11 = (bf16[512,1536]{1,0:T(8,128)(2,1)S(1)}, bf16[512,1536]{1,0:T(8,128)(2,1)}, u32[]{:S(2)}) copy-start(bf16[512,1536]{1,0:T(8,128)(2,1)} %fusion.12) | copy-start | bytes 4718596
  648.4 11.3 %copy-start.60 = (bf16[512,3072]{1,0:T(8,128)(2,1)S(1)}, bf16[512,3072]{1,0:T(8,128)(2,1)}, u32[]{:S(2)}) copy-start(bf16[512,3072]{1,0:T(8,128)(2,1)} %get-tuple-element.58) | copy-start | bytes 9437188
  677.7 12.4 %copy-start.7 = (f32[512,1536]{1,0:T(8,128)}, f32[512,1536]{1,0:T(8,128)S(1)}, u32[]{:S(2)}) copy-start(f32[512,1536]{1,0:T(8,128)S(1)} %convolution_add_fusion) | copy-start | bytes 9437188
  677.7 18.2 %copy-start.23 = (bf16[1,32,96,16]{2,3,1,0:T(8,128)(2,1)S(1)}, bf16[1,32,96,16]{2,3,1,0:T(8,128)(2,1)}, u32[]{:S(2)}) copy-start(bf16[1,32,96,16]{2,3,1,0:T(8,128)(2,1)} %copy.213) | copy-start | bytes 294916
  677.7 18.2 %copy-start.24 = (bf16[1,32,96,16]{2,3,1,0:T(8,128)(2,1)S(1)}, bf16[1,32,96,16]{2,3,1,0:T(8,128)(2,1)}, u32[]{:S(2)}) copy-start(bf16[1,32,96,16]{2,3,1,0:T(8,128)(2,1)} %copy.212) | copy-start | bytes 294916
  691.4 20.0 %all-to-all-start.2 = ((bf16[32,2,4608]{2,1,0:T(2,128)(2,1)}), bf16[32,2,4608]{2,1,0:T(2,128)(2,1)S(1)}, u32[]{:S(2)}, u32[]{:S(2)}) async-start(bf16[32,2,4608]{2,1,0:T(2,128)(2,1)} %broadcast_in_dim.242), calls=%async_computation.2 | async-start | bytes 1179648 | tf_op jit(solution)/shard_map/all_to_all | solution.py:318
  712.3 12.4 %all-to-all-start.3 = ((f32[32,2,48]{2,1,0:T(2,128)}), f32[32,2,48]{2,1,0:T(2,128)S(1)}, u32[]{:S(2)}, u32[]{:S(2)}) async-start(f32[32,2,48]{2,1,0:T(2,128)} %copy.200), calls=%async_computation.3 | async-start | bytes 65536 | tf_op jit(solution)/shard_map/all_to_all | solution.py:500
  724.7 112.2 %all-to-all-start.4 = ((bf16[32,432,128]{2,1,0:T(8,128)(2,1)}), bf16[32,432,128]{2,1,0:T(8,128)(2,1)}, u32[]{:S(2)}, u32[]{:S(2)}) async-start(bf16[32,432,128]{2,1,0:T(8,128)(2,1)} %pad_maximum_fusion), calls=%async_computation.7 | async-start | bytes 7077888 | tf_op jit(solution)/shard_map/all_to_all | solution.py:470
  735.7 129.1 %copy-start.25 = (bf16[48,3072]{1,0:T(8,128)(2,1)S(1)}, bf16[48,3072]{1,0:T(8,128)(2,1)}, u32[]{:S(2)}) copy-start(bf16[48,3072]{1,0:T(8,128)(2,1)} %reduce-scatter.4.cloned.1.call-done) | copy-start | bytes 884740
  (47 other events, 289.3 us)
Sparse Core Ops, SparseCore 0:
  10.9 103.9 all-gather.7
  118.3 93.6 all-gather.3
  214.8 80.1 all-gather.5
  402.7 135.6 reduce-scatter.3
  544.1 135.2 reduce-scatter.7
  685.1 179.5 reduce-scatter.5

commit v3 on v2

--- a/solution.py
+++ b/solution.py
@@ -232,18 +232,35 @@
     pad_ref[pl.ds(8 + length, 8), :] = edge
 
 
-def conv_kernel(x_ref, masks_ref, w_ref, b_ref, u0_ref, u1_ref, pad_scr, *, length, chunk, tiles):
-    for tile in range(tiles):
+def project_conv_kernel(h_ref, wts_ref, masks_ref, w_ref, b_ref, x_ref, u0_ref, u1_ref, pad_scr,
+                        *, length, chunk, width):
+    for half in range(width // PAIR):
+        cols = pl.ds(half * PAIR, PAIR)
+        wts = wts_ref[:, :, cols].reshape(h_ref.shape[1], PAIR)
+        x_ref[:, cols] = jnp.dot(h_ref[...], wts, preferred_element_type=f32)
+    for tile in range(width // LANES):
         lanes = pl.ds(tile * LANES, LANES)
-        fill_padded(pad_scr, length)
-        pad_scr[pl.ds(8, length), :] = x_ref[:, lanes]
+        pad = pad_scr.at[tile % 2]
+        fill_padded(pad, length)
+        pad[pl.ds(8, length), :] = x_ref[:, lanes]
         for row0 in range(0, length, chunk):
             for d, (sign, out) in enumerate(((1, u0_ref), (-1, u1_ref))):
                 pre = b_ref[d:d + 1, lanes]
                 for lag in range(KCONV):
-                    tap = conv_taps(pad_scr, row0, chunk, sign, masks_ref, lag)
+                    tap = conv_taps(pad, row0, chunk, sign, masks_ref, lag)
                     pre = pre + w_ref[d, lag:lag + 1, lanes] * tap
                 out[pl.ds(row0, chunk), lanes] = (pre * jax.nn.sigmoid(pre)).astype(bf16)
+
+
+def back_project_kernel(dx_ref, dz_ref, wx_ref, wz_ref, out_ref, *, width):
+    @pl.when(pl.program_id(0) == 0)
+    def _():
+        out_ref[...] = jnp.zeros_like(out_ref)
+
+    nt = (((1,), (1,)), ((), ()))
+    wx = wx_ref[...].reshape(out_ref.shape[1], width)
+    out_ref[...] += (lax.dot_general(dx_ref[...], wx, nt, preferred_element_type=f32)
+                     + lax.dot_general(dz_ref[...], wz_ref[...], nt, preferred_element_type=f32))
 
 
 def conv_back_kernel(x_ref, du0_ref, du1_ref, masks_ref, w_ref, b_ref, dx_ref, gw_ref, gb_ref,
@@ -279,7 +296,65 @@
             dx_ref[pl.ds(row0, chunk), lanes] = total.astype(bf16)
 
 
-def conv_calls(length, inner, width=256, chunk=64):
+def gate_kernel(h_ref, g_ref, wz_ref, wo_ref, y0_ref, y1_ref, gated_ref, ds_ref, dz_ref, z_scr, d_scr,
+                *, length, chunk):
+    z_scr[...] = jnp.dot(h_ref[...], wz_ref[...], preferred_element_type=f32)
+    d_scr[...] = lax.dot_general(g_ref[...], wo_ref[...], (((1,), (1,)), ((), ())),
+                                 preferred_element_type=f32)
+    for row0 in range(0, length, chunk):
+        rows = pl.ds(row0, chunk)
+        z, d_gated = z_scr[rows, :], d_scr[rows, :]
+        both = y0_ref[rows, :] + y1_ref[rows, :]
+        sig = jax.nn.sigmoid(z)
+        silu = z * sig
+        gated_ref[rows, :] = (both * silu).astype(bf16)
+        ds_ref[rows, :] = d_gated * silu
+        dz_ref[rows, :] = (d_gated * both * sig * (1.0 + z * (1.0 - sig))).astype(bf16)
+
+
+def gate_call(length, model, inner, width=384, chunk=32):
+    if inner % width:
+        width = PAIR
+    tok = pl.BlockSpec((length, width), lambda e: (0, e))
+    every = pl.BlockSpec((length, model), lambda e: (0, 0))
+    sds = jax.ShapeDtypeStruct
+    return pl.pallas_call(
+        functools.partial(gate_kernel, length=length, chunk=chunk), grid=(inner // width,),
+        in_specs=[every, every, pl.BlockSpec((model, width), lambda e: (0, e)),
+                  pl.BlockSpec((width, model), lambda e: (e, 0)), tok, tok],
+        out_specs=[tok, tok, tok],
+        out_shape=[sds((length, inner), bf16), sds((length, inner), f32), sds((length, inner), bf16)],
+        scratch_shapes=[pltpu.VMEM((length, width), f32)] * 2,
+        compiler_params=pltpu.CompilerParams(dimension_semantics=("arbitrary",)), name="gate")
+
+
+def projection_calls(length, model, inner, blocks, width=512, chunk=64):
+    if inner % width:
+        width = PAIR
+    rows = model // blocks
+    tok = pl.BlockSpec((length, width), lambda e: (0, e))
+    every = pl.BlockSpec((length, model), lambda e: (0, 0))
+    wts = pl.BlockSpec((blocks, rows, width), lambda e: (0, 0, e))
+    flat = pl.BlockSpec((model, width), lambda e: (0, e))
+    masks = pl.BlockSpec((2 * (KCONV - 1), length, LANES), lambda e: (0, 0, 0))
+    taps = pl.BlockSpec((2, KCONV, width), lambda e: (0, 0, e))
+    bias = pl.BlockSpec((2, width), lambda e: (0, e))
+    sds = jax.ShapeDtypeStruct
+    params = pltpu.CompilerParams(dimension_semantics=("arbitrary",))
+    ahead = pl.pallas_call(
+        functools.partial(project_conv_kernel, length=length, chunk=chunk, width=width),
+        grid=(inner // width,), in_specs=[every, wts, masks, taps, bias], out_specs=[tok, tok, tok],
+        out_shape=[sds((length, inner), f32)] + [sds((length, inner), bf16)] * 2,
+        scratch_shapes=[pltpu.VMEM((2, length + 16, LANES), f32)], compiler_params=params,
+        name="project_conv")
+    back = pl.pallas_call(
+        functools.partial(back_project_kernel, width=width), grid=(inner // width,),
+        in_specs=[tok, tok, wts, flat], out_specs=every,
+        out_shape=sds((length, model), f32), compiler_params=params, name="back_project")
+    return ahead, back
+
+
+def conv_back_call(length, inner, width=256, chunk=64):
     if inner % width:
         width = LANES
     tok = pl.BlockSpec((length, width), lambda e: (0, e))
@@ -290,17 +365,12 @@
     pad = pltpu.VMEM((length + 16, LANES), f32)
     sizes = dict(length=length, chunk=chunk, tiles=width // LANES)
     params = pltpu.CompilerParams(dimension_semantics=("arbitrary",))
-    ahead = pl.pallas_call(
-        functools.partial(conv_kernel, **sizes), grid=(inner // width,),
-        in_specs=[tok, masks, taps, bias], out_specs=[tok, tok],
-        out_shape=[sds((length, inner), bf16)] * 2, scratch_shapes=[pad],
-        compiler_params=params, name="conv_ahead")
     back = pl.pallas_call(
         functools.partial(conv_back_kernel, **sizes), grid=(inner // width,),
         in_specs=[tok, tok, tok, masks, taps, bias], out_specs=[tok, taps, bias],
         out_shape=[sds((length, inner), bf16), sds((2, KCONV, inner), f32), sds((2, inner), f32)],
         scratch_shapes=[pad] * 3, compiler_params=params, name="conv_back")
-    return ahead, back
+    return back
 
 
 EPS = 1e-06
@@ -320,10 +390,6 @@
 
 def gather0(v):
     return lax.all_gather(v, AXES, axis=0, tiled=True)
-
-
-def scatter0(v):
-    return lax.psum_scatter(v, AXES, scatter_dimension=0, tiled=True)
 
 
 def tied(v, *after):
@@ -352,12 +418,6 @@
     side = jnp.pad(jnp.swapaxes(dt_projection, 1, 2), ((0, 0), (0, 0), (0, LANES - rank)))
     pair = jnp.stack([x_projection, side])
     first = gather0(jnp.concatenate([in_weight[:, :inner], pair.reshape(-1, inner)], axis=0))
-    first = first.reshape(owners, -1, inner)
-    w_x = first[:, :own_model].reshape(-1, inner)
-    pair = jnp.moveaxis(first[:, own_model:].reshape(owners, 2, 2, own_inner, LANES), 0, 2)
-    w_xp, w_dt = pair.reshape(2, 2, inner, LANES)
-    w_z = gather0(in_weight[:, inner:])
-    w_o = gather0(out_weight)
 
     cond = condition[0].astype(f32)
     act = jax.nn.silu(cond).astype(bf16)
@@ -379,7 +439,6 @@
     act_own = lax.dynamic_slice(act_all, (0, me * own_model), (owners * 2, own_model))
     partial = mm(act_own, mod_weight, ((1,), (0,))).reshape(owners, 2, -1)
     mods = jnp.sum(lax.all_to_all(partial, AXES, 0, 0, tiled=True), axis=0) + modb
-
     flags = item_flags[0]
     ids = jnp.cumsum(flags, dtype=jnp.int32) - 1
     second = (ids == 1)[:, None]
@@ -393,18 +452,23 @@
     inv = lax.rsqrt(jnp.mean(centered * centered, axis=1, keepdims=True) + EPS)
     normed = centered * inv
     hidden = (normed * (1.0 + pick(scale)) + pick(shift)).astype(bf16)
-    xs = mm(hidden, w_x, ((1,), (0,)))
-
+    first, hidden, masks = lax.optimization_barrier((first, hidden, masks))
+    w_z = gather0(tied(in_weight[:, inner:], first))
+    w_o = gather0(tied(out_weight, first))
+    first = first.reshape(owners, -1, inner)
+    w_x = first if own_model % 16 == 0 else first[:, :own_model].reshape(1, -1, inner)
+    pair = jnp.moveaxis(first[:, own_model:].reshape(owners, 2, 2, own_inner, LANES), 0, 2)
+    w_xp, w_dt = pair.reshape(2, 2, inner, LANES)
     g = grad_out[0].astype(f32)
     d_branch = (g * pick(gate)).astype(bf16)
 
     starts = flags.astype(f32)
     starts_b = jnp.concatenate([starts[1:], jnp.ones((1,), f32)])
     calls = [scan_calls(1, length, inner, bool(d)) for d in range(2)]
-    conv_ahead, conv_back = conv_calls(length, inner)
+    project_conv, back_project = projection_calls(length, model, inner, 1 if w_x.shape[0] == 1 else owners)
     wide = lambda v: jnp.broadcast_to(v[None, :, :, None], (1, length, NST, LANES))
     tile = lambda v: jnp.tile(v, (1, SUB))[None]
-    us = conv_ahead(xs, masks, conv_w, conv_b)
+    xs, *us = project_conv(hidden, w_x, masks, conv_w, conv_b)
     kept = []
     for d in range(2):
         u = us[d]
@@ -418,71 +482,79 @@
         b_wide = wide(b_m)
         y, ck = calls[d][0](delta[None], u[None], sb, b_wide, tile(c_m), rate2, skip[d][None])
         kept.append((u, dt_low, b_m, c_m, delta, rate, rate2, sb, b_wide, y[0], ck))
-    both = kept[0][9] + kept[1][9]
-    z = mm(tied(hidden, both), w_z, ((1,), (0,)))
-    sig_z = jax.nn.sigmoid(z)
-    silu_z = z * sig_z
-    gated = (both * silu_z).astype(bf16)
+    gated, d_scan, d_z = gate_call(length, model, inner)(
+        hidden, d_branch, w_z, w_o, kept[0][9], kept[1][9])
     grad_out_w = mm(gated, d_branch, ((0,), (0,))).astype(bf16)
-
-    d_gated = mm(d_branch, w_o, ((1,), (1,)))
-    d_scan = d_gated * silu_z
-    d_z = (d_gated * both * sig_z * (1.0 + z * (1.0 - sig_z))).astype(bf16)
     grad_in_z = mm(hidden, d_z, ((0,), (0,))).astype(bf16)
     d_scan, grad_out_w, grad_in_z = lax.optimization_barrier((d_scan, grad_out_w, grad_in_z))
-    grad_out_w = scatter0(grad_out_w)
-    grad_in_z = scatter0(grad_in_z)
+    over_dp = lambda v: lax.psum_scatter(v, "dp", scatter_dimension=0, tiled=True)
+    over_fsdp = lambda v: lax.psum_scatter(v.reshape(-1, model), "fsdp", scatter_dimension=0, tiled=True)
+    ranks = lax.axis_size("fsdp")
+    halves = lambda v: [h.reshape(ranks, -1, model) for h in jnp.split(v, inner // model, axis=1)]
+    joined = lambda v: jnp.concatenate(jnp.split(v, inner // model, axis=0), axis=1)
+    early_o, early_z = over_dp(grad_out_w), over_dp(grad_in_z)
     branch = mm(gated, w_o, ((1,), (0,)))
     block_out = (x + pick(gate) * branch).astype(bf16)
     d_gate = g * branch
     lane = lax.broadcasted_iota(jnp.int32, (1, LANES), 1)
-    d_us, g_xps, g_dts, g_dbs, g_als, g_sks = [], [], [], [], [], []
+    def by_owner(v, dim):
+        shape = v.shape[:dim] + (owners, v.shape[dim] // owners) + v.shape[dim + 1:]
+        return jnp.moveaxis(v.reshape(shape), dim, 0).astype(bf16)
+
+    def send(values, dims):
+        pieces = [by_owner(v, dim) for v, dim in zip(values, dims)]
+        flat = jnp.concatenate([p.reshape(owners, -1) for p in pieces], axis=1)
+        flat = jnp.pad(flat, ((0, 0), (0, -flat.shape[1] % (8 * LANES)))).reshape(owners, -1, LANES)
+        return flat, [p.shape[1:] for p in pieces]
+
+    def exchange(flat):
+        return jnp.sum(lax.all_to_all(flat, AXES, 0, 0, tiled=True).astype(f32), axis=0).reshape(-1)
+
+    def receive(own, shapes):
+        out, at = [], 0
+        for shape in shapes:
+            count = 1
+            for n in shape:
+                count *= n
+            out.append(own[at:at + count].reshape(shape))
+            at += count
+        return out
+
+    d_us, sent = [], []
+    carried = d_scan
     for d in range(2):
         u, dt_low, b_m, c_m, delta, rate, rate2, sb, b_wide, _, ck = kept[d]
         du, dr, db, dc, ga, gs, gb = calls[d][1](
-            delta[None], u[None], sb, b_wide, wide(c_m), tile(b_m), d_scan[None], ck, rate, rate2,
+            delta[None], u[None], sb, b_wide, wide(c_m), tile(b_m), carried[None], ck, rate, rate2,
             skip[d][None])
         dr = dr[0]
+        if d == 1:
+            dr, early_o, early_z = lax.optimization_barrier((dr, early_o, early_z))
         d_low = mm(dr, w_dt[d], ((1,), (0,)))
         d_proj = jnp.where(lane < rank, d_low, jnp.where(lane < rank + NST, db[0], dc[0])).astype(bf16)
-        g_dts.append(mm(dr, dt_low, ((0,), (0,))))
-        g_xps.append(mm(u, d_proj, ((0,), (0,))))
+        g_dt = mm(dr, dt_low, ((0,), (0,)))
+        g_xp = mm(u, d_proj, ((0,), (0,)))
+        flat, shapes = send((g_xp, g_dt, jnp.sum(gb, axis=0), ga.T, jnp.sum(gs, axis=0)), (0,) * 5)
         d_us.append(du[0] + mm(d_proj, w_xp[d], ((1,), (1,))))
-        g_dbs.append(jnp.sum(gb, axis=0))
-        g_als.append(ga.T)
-        g_sks.append(jnp.sum(gs, axis=0))
-    d_xs, g_cw, g_cb = conv_back(xs, d_us[0], d_us[1], masks, conv_w, conv_b)
+        if d == 0:
+            carried, flat = lax.optimization_barrier((carried, flat))
+        else:
+            d_us[1], flat = lax.optimization_barrier((d_us[1], flat))
+        sent.append((flat, shapes))
+    packed = jnp.concatenate([s[0].reshape(owners, -1) for s in sent], axis=1)
+    span = sent[0][0].size // owners
+    packed = jnp.pad(packed, ((0, 0), (0, -packed.shape[1] % (8 * model)))).reshape(-1, model)
+    early = over_fsdp(jnp.concatenate([early_o.reshape(ranks, -1, model)] + halves(early_z), axis=1))
+    grad_out_w, grad_in_z = early[:own_inner], joined(early[own_inner:])
+    packed = over_dp(packed)
+    d_xs, g_cw, g_cb = conv_back_call(length, inner)(xs, d_us[0], d_us[1], masks, conv_w, conv_b)
     grad_in_x = mm(hidden, d_xs, ((0,), (0,))).astype(bf16)
 
-    wide_rows = [jnp.stack(v).astype(bf16).reshape(2, owners, own_inner, LANES) for v in (g_xps, g_dts)]
-    wide_rows = jnp.concatenate([jnp.moveaxis(v, 1, 0).reshape(owners, -1, LANES) for v in wide_rows], axis=1)
-    stacked = [g_cw, g_cb, jnp.stack(g_dbs), jnp.stack(g_als), jnp.stack(g_sks)]
-    dims = (2, 1, 1, 1, 1)
-    pieces, shapes = [], []
-    for v, dim in zip(stacked, dims):
-        shape = v.shape[:dim] + (owners, v.shape[dim] // owners) + v.shape[dim + 1:]
-        pieces.append(jnp.moveaxis(v.reshape(shape), dim, 0).reshape(owners, -1).astype(bf16))
-        shapes.append(v.shape[:dim] + (v.shape[dim] // owners,) + v.shape[dim + 1:])
-    packed = jnp.concatenate(pieces, axis=1)
-    packed = jnp.pad(packed, ((0, 0), (0, -packed.shape[1] % (16 * LANES))))
-    packed = jnp.concatenate([wide_rows, packed.reshape(owners, -1, LANES)], axis=1)
-    grad_in_x = scatter0(tied(grad_in_x, grad_in_z))
-    received = lax.all_to_all(packed, AXES, 0, 0, tiled=True)
-    mine = jnp.sum(received.astype(f32), axis=0)
-    grad_in = jnp.concatenate([grad_in_x, grad_in_z], axis=1).astype(f32)
-    both_rows = mine[:4 * own_inner].reshape(2, 2, own_inner, LANES)
-    g_xp = both_rows[0]
-    g_dt = jnp.swapaxes(both_rows[1][..., :rank], 1, 2)
-    mine = mine[4 * own_inner:].reshape(-1)
-    small_grads, at = [], 0
-    for shape in shapes:
-        count = 1
-        for n in shape:
-            count *= n
-        small_grads.append(mine[at:at + count].reshape(shape))
-        at += count
-
-    d_hidden = mm(d_xs, w_x, ((1,), (1,))) + mm(d_z, w_z, ((1,), (1,)))
+    grad_in_x = over_dp(tied(grad_in_x, packed, early))
+    flat, shapes = send((g_cw, g_cb), (2, 1))
+    g_cw, g_cb = receive(exchange(flat), shapes)
+
+    d_hidden = back_project(d_xs, d_z, w_x, w_z)
     scale_tok = 1.0 + pick(scale)
     d_n = d_hidden * scale_tok
     m1 = jnp.mean(d_n, axis=1, keepdims=True)
@@ -498,10 +570,17 @@
         lax.dynamic_slice(d_mods_all, (0, me * own_b), (owners * 2, own_b)).astype(f32), axis=0)
     d_act = mm(d_mods_all, mod_weight, ((1,), (1,))).reshape(owners, 2, own_model)
     d_act = lax.all_to_all(d_act, AXES, 0, 0, tiled=True)
+    grad_in_x, d_act, g_cw = lax.optimization_barrier((grad_in_x, d_act, g_cw))
+    late = over_fsdp(jnp.concatenate(halves(grad_in_x) + [packed.reshape(ranks, -1, model)], axis=1))
+    count = own_model * (inner // model)
+    grad_in = jnp.concatenate([joined(late[:count]), grad_in_z], axis=1).astype(f32)
+    packed = late[count:].reshape(-1)[:2 * span].astype(f32).reshape(2, -1)
+    g_xp, g_dt, g_db, g_al, g_sk = [
+        jnp.stack(v) for v in zip(*(receive(packed[d], sent[d][1]) for d in range(2)))]
+    g_dt = jnp.swapaxes(g_dt[..., :rank], 1, 2)
     d_act = jnp.moveaxis(d_act, 0, 1).reshape(2, model)
     sc = jax.nn.sigmoid(cond)
     grad_cond = d_act * sc * (1.0 + cond * (1.0 - sc))
-    g_cw, g_cb, g_db, g_al, g_sk = small_grads
     return (block_out[None], grad_tokens[None], grad_cond[None], grad_in, grad_out_w.astype(f32), g_xp,
             g_dt, g_cw, g_cb, g_db, g_al, g_sk, grad_mod_w, grad_mod_b)
 

time: 879 us -> 840 us (0.956)
  matrix products: 140 us -> 89.2 us
  Pallas kernels: 282 us -> 327 us
  waiting for transfers between devices: 271 us -> 242 us
  other arithmetic: 47 us -> 32.4 us
  local copies, waits for them, and re-layouts: 93.2 us -> 104 us
    all_to_all x1, waiting for transfers between devices: 101 us -> 6.55 us  [exchange(): lax.all_to_all(flat, AXES, 0, 0, tiled=True).astype(f32)]
    reduce_scatter x3 -> x6, waiting for transfers between devices: 20 us -> 90.4 us  [the longest x4 63.1 us: body(): lax.psum_scatter(v, 'dp', scatter_dimension=0, tiled=True)]
    dot_general x24 -> x19, matrix products: 140 us -> 89.2 us  [mm(): return lax.dot_general(a, b, (dims, ((), ())), preferred_element_type=f32)]
    pallas_call x2 -> x4, Pallas kernels: 35.8 us -> 79 us  [the longest x1 22.7 us: body(): conv_back_call(length, inner)(xs, d_us[0], d_us[1], masks, conv_w, conv_b)]
    all_gather x3, waiting for transfers between devices: 103 us -> 62.7 us  [gather0(): return lax.all_gather(v, AXES, axis=0, tiled=True)]
    all_to_all x2, waiting for transfers between devices: 18.3 us -> 35.5 us  [to_all(): lax.all_to_all(jnp.broadcast_to(v[None], (owners,) + v.shape), AXES, 0, 0...]
    all_to_all x1, waiting for transfers between devices: 24 us -> 38.7 us  [body(): lax.all_to_all(partial, AXES, 0, 0, tiled=True)]
    convert_element_type x12 -> x15, local copies, waits for them, and re-layouts: 3.32 us -> 14.2 us  [by_owner(): return jnp.moveaxis(v.reshape(shape), dim, 0).astype(bf16)]
  transfers between devices with their start and end apart: 11 -> 14, of which waited for: 8 -> 10; matrix products, arithmetic and copies ran while one was open for 28% -> 20% of each run, Pallas kernels for 32% -> 36%
where the time goes in v3:
time: 840 us; the launch traced here: 834 us
  Pallas kernels  327 us (39%)
  waiting for transfers between devices  242 us (29%)
  local copies, waits for them, and re-layouts  104 us (12%)
  matrix products  89.2 us (11%)
  other arithmetic  32.4 us (4%)
  starting transfers between devices  25.1 us (3%)
  between operations  15.5 us (2%)
    pallas_call x2, Pallas kernels, body(): calls[d][1]  179 us
    dot_general x19, matrix products, mm(): return lax.dot_general(a, b, (dims, ((), ())), preferred_element_type=f32)  89.2 us
    pallas_call x2, Pallas kernels, body(): calls[d][0]  69 us
    reduce_scatter x4, waiting for transfers between devices, body(): lax.psum_scatter(v, 'dp', scatter_dimension=0, tiled=True)  63.1 us
    all_gather x3, waiting for transfers between devices, gather0(): return lax.all_gather(v, AXES, axis=0, tiled=True)  62.7 us
    all_to_all x1, waiting for transfers between devices, body(): lax.all_to_all(partial, AXES, 0, 0, tiled=True)  38.7 us
    all_to_all x2, waiting for transfers between devices, to_all(): lax.all_to_all(jnp.broadcast_to(v[None], (owners,) + v.shape), AXES, 0, 0...  35.5 us
    reduce_scatter x2, waiting for transfers between devices, body(): lax.psum_scatter(v.reshape(-1, model), 'fsdp', scatter_dimension=0, tiled...  27.2 us
  transfers between devices with their start and end apart: 14, of which 10 were waited for; matrix products, arithmetic and copies ran while one was open for 20% of the time, Pallas kernels for 36%

profile of v3, /device:TPU:0, one launch (start us, length us, event | category | flops | bytes accessed | tf_op | source)
XLA Modules:
  0.0 834.2 jit_solution(18371244758315062269)
XLA Ops:
  13.6 7.3 all-to-all-start
  20.9 21.1 %all-to-all-done = bf16[32,64,128]{2,1,0:T(8,128)(2,1)S(1)} async-done(((bf16[32,64,128]{2,1,0:T(8,128)(2,1)}), bf16[32,64,128]{2,1,0:T(8,128)(2,1)S(1)}, u32[]{:S(2)}, u32[]{:S(2)}) %all-to-all-start) | async-done | bytes 524320 | tf_op jit(solution)/shard_map/all_to_all | solution.py:388
  46.1 5.4 all-to-all-start.1
  54.2 38.7 %all-to-all-done.1 = f32[32,2,4608]{2,1,0:T(2,128)S(1)} async-done(((f32[32,2,4608]{2,1,0:T(2,128)}), f32[32,2,4608]{2,1,0:T(2,128)S(1)}, u32[]{:S(2)}, u32[]{:S(2)}) %all-to-all-start.1) | async-done | bytes 1179680 | tf_op jit(solution)/shard_map/all_to_all | solution.py:441
  97.8 36.0 %all-gather.4.cloned.1.call-done = bf16[2048,3072]{1,0:T(8,128)(2,1)} async-done(((bf16[64,3072]{1,0:T(8,128)(2,1)}), bf16[2048,3072]{1,0:T(8,128)(2,1)}) %all-gather.4.cloned.1.call-update) | async-done | bytes 12582928 | tf_op jit(solution)/shard_map/all_gather | solution.py:392
  149.0 5.9 reshape.406
  154.9 16.8 %project_conv.1 = (f32[512,3072]{1,0:T(8,128)}, bf16[512,3072]{1,0:T(8,128)(2,1)}, bf16[512,3072]{1,0:T(8,128)(2,1)}) custom-call(bf16[512,1536]{1,0:T(8,128)(2,1)} %get-tuple-element.60.h_ref, bf16[32,64,3072]{2,1,0:T(8,128)(2,1)} %bitcast.237, f32[6,512,128]{2,1,0:T(8,128)} %broadcast_in_dim.200.masks_ref, f32[2,4,3072]{2,1,0:T(4,128)} %reshape.433.w_ref, ...), custom_call_target="tpu_custom_call" | custom-call | tf_op jit(solution)/shard_map/project_conv/pallas_call | solution.py:471
  183.1 7.5 fusion.2.delta_ref
  194.0 33.5 %scan_ahead_f.1 = (f32[1,512,3072]{2,1,0:T(8,128)}, f32[1,32,16,3072]{3,2,1,0:T(8,128)}) custom-call(f32[1,512,3072]{2,1,0:T(8,128)} %fusion.2.delta_ref, bf16[1,512,3072]{2,1,0:T(8,128)(2,1)} %bitcast.234, f32[1,512,128]{2,1,0:T(8,128)} %broadcast_in_dim.203.sb_ref, f32[1,512,16,128]{3,2,1,0:T(8,128)} %broadcast_in_dim.204.bx_ref, ...), custom_call_target="tpu_custom_call" | custom-call | tf_op jit(solution)/shard_map/scan_ahead_f/pallas_call | solution.py:483
  227.6 6.3 fusion.3.delta_ref
  237.4 35.5 %scan_ahead_b.1 = (f32[1,512,3072]{2,1,0:T(8,128)}, f32[1,32,16,3072]{3,2,1,0:T(8,128)}) custom-call(f32[1,512,3072]{2,1,0:T(8,128)} %fusion.3.delta_ref, bf16[1,512,3072]{2,1,0:T(8,128)(2,1)} %bitcast.232, f32[1,512,128]{2,1,0:T(8,128)} %broadcast_in_dim.207.sb_ref, f32[1,512,16,128]{3,2,1,0:T(8,128)} %broadcast_in_dim.208.bx_ref, ...), custom_call_target="tpu_custom_call" | custom-call | tf_op jit(solution)/shard_map/scan_ahead_b/pallas_call | solution.py:483
  272.9 26.7 %all-gather.8.cloned.1.call-done.wo_ref = bf16[3072,1536]{1,0:T(8,128)(2,1)} async-done(((bf16[96,1536]{1,0:T(8,128)(2,1)}), bf16[3072,1536]{1,0:T(8,128)(2,1)}) %all-gather.8.cloned.1.call-update) | async-done | bytes 9437200 | tf_op jit(solution)/shard_map/all_gather | solution.py:392
  299.6 22.4 %gate.1 = (bf16[512,3072]{1,0:T(8,128)(2,1)}, f32[512,3072]{1,0:T(8,128)}, bf16[512,3072]{1,0:T(8,128)(2,1)}) custom-call(bf16[512,1536]{1,0:T(8,128)(2,1)} %get-tuple-element.60.h_ref, bf16[512,1536]{1,0:T(8,128)(2,1)} %get-tuple-element.226.g_ref, bf16[1536,3072]{1,0:T(8,128)(2,1)} %all-gather.6.cloned.1.call-done.wz_ref, ...), custom_call_target="tpu_custom_call" | custom-call | tf_op jit(solution)/shard_map/gate/pallas_call | solution.py:485
  322.0 9.4 %convolution_convert_fusion.2 = bf16[3072,1536]{1,0:T(8,128)(2,1)} fusion(bf16[512,3072]{1,0:T(8,128)(2,1)} %get-tuple-element.69, bf16[512,1536]{1,0:T(8,128)(2,1)} %get-tuple-element.226.g_ref), kind=kOutput, calls=%fused_computation.4 | convolution fusion | flops 4836556800 | bytes 14155776 | tf_op jit(solution)/shard_map/dot_general | solution.py:383
  331.5 9.3 %convolution_convert_fusion.1 = bf16[1536,3072]{1,0:T(8,128)(2,1)} fusion(bf16[512,1536]{1,0:T(8,128)(2,1)S(1)} %copy-done.7, bf16[512,3072]{1,0:T(8,128)(2,1)} %get-tuple-element.72.dz_ref), kind=kOutput, calls=%fused_computation.3 | convolution fusion | flops 4836556800 | bytes 14155776 | tf_op jit(solution)/shard_map/dot_general | solution.py:383
  349.3 91.7 %scan_back_f.1 = (f32[1,512,3072]{2,1,0:T(8,128)}, bf16[1,512,3072]{2,1,0:T(8,128)(2,1)}, f32[1,512,128]{2,1,0:T(8,128)}, f32[1,512,128]{2,1,0:T(8,128)}, f32[16...) custom-call(f32[1,512,3072]{2,1,0:T(8,128)} %fusion.2.delta_ref, bf16[1,512,3072]{2,1,0:T(8,128)(2,1)} %bitcast.235, ...), custom_call_target="tpu_custom_call" | custom-call | tf_op jit(solution)/shard_map/scan_back_f/pallas_call | solution.py:527
  448.5 4.7 copy.136
  472.5 86.9 %scan_back_b.1 = (f32[1,512,3072]{2,1,0:T(8,128)}, bf16[1,512,3072]{2,1,0:T(8,128)(2,1)}, f32[1,512,128]{2,1,0:T(8,128)}, f32[1,512,128]{2,1,0:T(8,128)}, f32[16...) custom-call(f32[1,512,3072]{2,1,0:T(8,128)} %fusion.3.delta_ref, bf16[1,512,3072]{2,1,0:T(8,128)(2,1)} %bitcast.233, ...), custom_call_target="tpu_custom_call" | custom-call | tf_op jit(solution)/shard_map/scan_back_b/pallas_call | solution.py:527
  597.7 5.6 reshape.412
  603.3 6.4 bitcast_add_fusion.1.du0_ref
  609.7 22.7 %conv_back.1 = (bf16[512,3072]{1,0:T(8,128)(2,1)}, f32[2,4,3072]{2,1,0:T(4,128)}, f32[2,3072]{1,0:T(2,128)}) custom-call(f32[512,3072]{1,0:T(8,128)} %get-tuple-element.70.x_ref, f32[512,3072]{1,0:T(8,128)} %bitcast_add_fusion.1.du0_ref, f32[512,3072]{1,0:T(8,128)} %bitcast_add_fusion.du1_ref, f32[6,512,128]{2,1,0:T(8,128)} %broadcast_in_dim.200.masks_ref, ...), custom_call_target="tpu_custom_call" | custom-call | tf_op jit(solution)/shard_map/conv_back/pallas_call | solution.py:550
  632.4 9.4 %convolution_convert_fusion = bf16[1536,3072]{1,0:T(8,128)(2,1)} fusion(bf16[512,1536]{1,0:T(8,128)(2,1)S(1)} %copy-done.7, bf16[512,3072]{1,0:T(8,128)(2,1)} %get-tuple-element.95.dx_ref), kind=kOutput, calls=%fused_computation.2 | convolution fusion | flops 4836556800 | bytes 14155776 | tf_op jit(solution)/shard_map/dot_general | solution.py:383
  641.8 51.4 %reduce-scatter.11.cloned.1.call-done = bf16[160,1536]{1,0:T(8,128)(2,1)} async-done(((bf16[1280,1536]{1,0:T(8,128)(2,1)}), bf16[160,1536]{1,0:T(8,128)(2,1)}) %reduce-scatter.11.cloned.1.call-update) | async-done | bytes 491536 | tf_op jit(solution)/shard_map/reduce_scatter | solution.py:490
  693.3 17.1 %back_project.1 = f32[512,1536]{1,0:T(8,128)} custom-call(bf16[512,3072]{1,0:T(8,128)(2,1)} %get-tuple-element.95.dx_ref, bf16[512,3072]{1,0:T(8,128)(2,1)} %get-tuple-element.72.dz_ref, bf16[32,64,3072]{2,1,0:T(8,128)(2,1)} %bitcast.238, bf16[1536,3072]{1,0:T(8,128)(2,1)} %all-gather.6.cloned.1.call-done.wz_ref), custom_call_target="tpu_custom_call" | custom-call | tf_op jit(solution)/shard_map/back_project/pallas_call | solution.py:557
  710.5 15.1 %select_reduce_fusion.3 = (bf16[1536]{0:T(1024)(128)(2,1)S(1)}, bf16[1536]{0:T(1024)(128)(2,1)S(1)}, f32[512]{0:T(512)S(1)}, f32[512]{0:T(512)S(1)}, bf16[1536]{...) fusion(f32[512,1536]{1,0:T(8,128)} %back_project.1, ...), kind=kOutput, calls=%fused_computation.44 | convolution fusion | flops 4853848064 | bytes 20498944 | tf_op jit(solution)/shard_map/dot_general | solution.py:383
  726.9 4.9 all-to-all-start.2
  733.0 14.3 %all-to-all-done.2 = bf16[32,2,4608]{2,1,0:T(2,128)(2,1)S(1)} async-done(((bf16[32,2,4608]{2,1,0:T(2,128)(2,1)}), bf16[32,2,4608]{2,1,0:T(2,128)(2,1)S(1)}, u32[]{:S(2)}, u32[]{:S(2)}) %all-to-all-start.2) | async-done | bytes 589856 | tf_op jit(solution)/shard_map/all_to_all | solution.py:388
  752.6 6.6 all-to-all-done.4
  762.5 6.5 all-to-all-done.3
  769.1 11.7 %reduce-scatter.15.cloned.1.call-done = bf16[192,3072]{1,0:T(8,128)(2,1)} async-done(((bf16[1536,3072]{1,0:T(8,128)(2,1)}), bf16[192,3072]{1,0:T(8,128)(2,1)}) %reduce-scatter.15.cloned.1.call-update) | async-done | bytes 1179664 | tf_op jit(solution)/shard_map/reduce_scatter | solution.py:490
  783.5 4.4 fusion.21
  793.1 27.2 %reduce-scatter.17.cloned.1.call-done = bf16[136,1536]{1,0:T(8,128)(2,1)} async-done(((bf16[544,1536]{1,0:T(8,128)(2,1)}), bf16[136,1536]{1,0:T(8,128)(2,1)}) %reduce-scatter.17.cloned.1.call-update) | async-done | bytes 417808 | tf_op jit(solution)/shard_map/reduce_scatter | solution.py:491
  (329 shorter events, 150.1 us)
Async XLA Ops:
  7.2 36.8 %copy-start = (bf16[48,4608]{1,0:T(8,128)(2,1)S(1)}, bf16[48,4608]{1,0:T(8,128)(2,1)}, u32[]{:S(2)}) copy-start(bf16[48,4608]{1,0:T(8,128)(2,1)} %param.28) | copy-start | bytes 1327108
  7.3 126.5 %all-gather.4.cloned.1.call-start = ((), (), s32[]{:S(2)}) async-start(), calls=%async_computation.11 | async-start | bytes 12976128 | tf_op jit(solution)/shard_map/all_gather | solution.py:392
  13.6 28.5 %all-to-all-start = ((bf16[32,64,128]{2,1,0:T(8,128)(2,1)}), bf16[32,64,128]{2,1,0:T(8,128)(2,1)S(1)}, u32[]{:S(2)}, u32[]{:S(2)}) async-start(bf16[32,64,128]{2,1,0:T(8,128)(2,1)} %broadcast_in_dim.193), calls=%async_computation | async-start | bytes 1048576 | tf_op jit(solution)/shard_map/all_to_all | solution.py:388
  46.1 46.8 %all-to-all-start.1 = ((f32[32,2,4608]{2,1,0:T(2,128)}), f32[32,2,4608]{2,1,0:T(2,128)S(1)}, u32[]{:S(2)}, u32[]{:S(2)}) async-start(f32[32,2,4608]{2,1,0:T(2,128)} %reshape.403), calls=%async_computation.1 | async-start | bytes 2359296 | tf_op jit(solution)/shard_map/all_to_all | solution.py:441
  51.5 221.4 %all-gather.6.cloned.1.call-start = ((), (), s32[]{:S(2)}) async-start(), calls=%async_computation.12 | async-start | bytes 9732096 | tf_op jit(solution)/shard_map/all_gather | solution.py:392
  52.2 45.5 %copy-start.50 = (pred[512]{0:T(512)(128)(4,1)}, pred[512]{0:T(512)(128)(4,1)S(1)}, u32[]{:S(2)}) copy-start(pred[512]{0:T(512)(128)(4,1)S(1)} %get-tuple-element.182) | copy-start | bytes 1540
  52.7 45.0 %copy-start.41 = (f32[512]{0:T(512)}, f32[512]{0:T(512)S(1)}, u32[]{:S(2)}) copy-start(f32[512]{0:T(512)S(1)} %broadcast_multiply_fusion.5) | copy-start | bytes 6148
  53.3 44.5 %copy-start.47 = (f32[512]{0:T(512)}, f32[512]{0:T(512)S(1)}, u32[]{:S(2)}) copy-start(f32[512]{0:T(512)S(1)} %add_rsqrt_fusion) | copy-start | bytes 6148
  97.8 42.7 %copy-start.16 = (f32[32,3072]{1,0:T(8,128)S(1)}, f32[32,3072]{1,0:T(8,128)}, u32[]{:S(2)}) copy-start(f32[32,3072]{1,0:T(8,128)} %get-tuple-element.202) | copy-start | bytes 1179652
  135.4 164.3 %all-gather.8.cloned.1.call-start = ((), (), s32[]{:S(2)}) async-start(), calls=%async_computation.13 | async-start | bytes 9732096 | tf_op jit(solution)/shard_map/all_gather | solution.py:392
  136.1 433.0 %reduce-scatter.7.cloned.1.call-start = ((), (), s32[]{:S(2)}) async-start(), calls=%async_computation.14 | async-start | bytes 10616832 | tf_op jit(solution)/shard_map/reduce_scatter | solution.py:490
  174.9 52.7 %copy-start.11 = (bf16[1,1,32,96,128]{4,3,1,0,2:T(8,128)(2,1)}, bf16[1,1,32,96,128]{4,3,1,0,2:T(8,128)(2,1)S(1)}, u32[]{:S(2)}) copy-start(bf16[1,1,32,96,128]{4,3,1,0,2:T(8,128)(2,1)S(1)} %get-tuple-element.186) | copy-start | bytes 2359300
  181.8 45.7 %copy-start.17 = (f32[512,128]{0,1:T(8,128)}, f32[512,128]{0,1:T(8,128)S(1)}, u32[]{:S(2)}) copy-start(f32[512,128]{0,1:T(8,128)S(1)} %fusion.71) | copy-start | bytes 786436
  340.8 228.3 %reduce-scatter.9.cloned.1.call-start = ((), (), s32[]{:S(2)}) async-start(), calls=%async_computation.15 | async-start | bytes 10616832 | tf_op jit(solution)/shard_map/reduce_scatter | solution.py:490
  341.4 300.4 %reduce-scatter.13.cloned.1.call-start = ((), (), s32[]{:S(2)}) async-start(), calls=%async_computation.17 | async-start | bytes 2949120 | tf_op jit(solution)/shard_map/reduce_scatter | solution.py:491
  594.2 99.0 %reduce-scatter.11.cloned.1.call-start = ((), (), s32[]{:S(2)}) async-start(), calls=%async_computation.16 | async-start | bytes 4423680 | tf_op jit(solution)/shard_map/reduce_scatter | solution.py:490
  603.3 177.5 %reduce-scatter.15.cloned.1.call-start = ((), (), s32[]{:S(2)}) async-start(), calls=%async_computation.18 | async-start | bytes 10616832 | tf_op jit(solution)/shard_map/reduce_scatter | solution.py:490
  693.2 17.2 %copy-start.5 = (bf16[1,512,1536]{2,1,0:T(8,128)(2,1)S(1)}, bf16[1,512,1536]{2,1,0:T(8,128)(2,1)}, u32[]{:S(2)}) copy-start(bf16[1,512,1536]{2,1,0:T(8,128)(2,1)} %param.15) | copy-start | bytes 4718596
  693.2 17.2 %copy-start.34 = (f32[1536]{0:T(1024)S(1)}, f32[1536]{0:T(1024)}, u32[]{:S(2)}) copy-start(f32[1536]{0:T(1024)} %copy-done.33) | copy-start | bytes 18436
  693.2 17.2 %copy-start.36 = (f32[1536]{0:T(1024)S(1)}, f32[1536]{0:T(1024)}, u32[]{:S(2)}) copy-start(f32[1536]{0:T(1024)} %copy-done.35) | copy-start | bytes 18436
  693.2 17.2 %copy-start.38 = (f32[1536]{0:T(1024)S(1)}, f32[1536]{0:T(1024)}, u32[]{:S(2)}) copy-start(f32[1536]{0:T(1024)} %copy-done.37) | copy-start | bytes 18436
  693.2 17.2 %copy-start.40 = (f32[1536]{0:T(1024)S(1)}, f32[1536]{0:T(1024)}, u32[]{:S(2)}) copy-start(f32[1536]{0:T(1024)} %copy-done.39) | copy-start | bytes 18436
  693.3 17.2 %copy-start.42 = (f32[512]{0:T(512)S(1)}, f32[512]{0:T(512)}, u32[]{:S(2)}) copy-start(f32[512]{0:T(512)} %copy-done.41) | copy-start | bytes 6148
  693.3 17.2 %copy-start.48 = (f32[512]{0:T(512)S(1)}, f32[512]{0:T(512)}, u32[]{:S(2)}) copy-start(f32[512]{0:T(512)} %copy-done.47) | copy-start | bytes 6148
  693.3 17.2 %copy-start.51 = (pred[512]{0:T(512)(128)(4,1)S(1)}, pred[512]{0:T(512)(128)(4,1)}, u32[]{:S(2)}) copy-start(pred[512]{0:T(512)(128)(4,1)} %copy-done.50) | copy-start | bytes 1540
  710.5 21.3 %copy-start.43 = (f32[2,3072]{1,0:T(2,128)S(1)}, f32[2,3072]{1,0:T(2,128)}, u32[]{:S(2)}) copy-start(f32[2,3072]{1,0:T(2,128)} %get-tuple-element.102) | copy-start | bytes 73732
  710.5 21.5 %copy-start.32 = (f32[2,4,3072]{2,1,0:T(4,128)S(1)}, f32[2,4,3072]{2,1,0:T(4,128)}, u32[]{:S(2)}) copy-start(f32[2,4,3072]{2,1,0:T(4,128)} %get-tuple-element.101) | copy-start | bytes 294916
  725.8 56.3 %copy-start.27 = (bf16[160,1536]{1,0:T(8,128)(2,1)S(1)}, bf16[160,1536]{1,0:T(8,128)(2,1)}, u32[]{:S(2)}) copy-start(bf16[160,1536]{1,0:T(8,128)(2,1)} %reduce-scatter.11.cloned.1.call-done) | copy-start | bytes 1474564
  726.9 20.4 %all-to-all-start.2 = ((bf16[32,2,4608]{2,1,0:T(2,128)(2,1)}), bf16[32,2,4608]{2,1,0:T(2,128)(2,1)S(1)}, u32[]{:S(2)}, u32[]{:S(2)}) async-start(bf16[32,2,4608]{2,1,0:T(2,128)(2,1)} %broadcast_in_dim.218), calls=%async_computation.7 | async-start | bytes 1179648 | tf_op jit(solution)/shard_map/all_to_all | solution.py:388
  747.3 11.9 %all-to-all-start.4 = ((bf16[32,8,128]{2,1,0:T(8,128)(2,1)}), bf16[32,8,128]{2,1,0:T(8,128)(2,1)S(1)}, u32[]{:S(2)}, u32[]{:S(2)}) async-start(bf16[32,8,128]{2,1,0:T(8,128)(2,1)} %bitcast.94), calls=%async_computation.9 | async-start | bytes 131072 | tf_op jit(solution)/shard_map/all_to_all | solution.py:511
  759.2 9.9 %all-to-all-start.3 = ((f32[32,2,48]{2,1,0:T(2,128)}), f32[32,2,48]{2,1,0:T(2,128)S(1)}, u32[]{:S(2)}, u32[]{:S(2)}) async-start(f32[32,2,48]{2,1,0:T(2,128)} %copy.142), calls=%async_computation.8 | async-start | bytes 65536 | tf_op jit(solution)/shard_map/all_to_all | solution.py:572
  761.8 58.6 %reduce-scatter.17.cloned.1.call-start = ((), (), s32[]{:S(2)}) async-start(), calls=%async_computation.19 | async-start | bytes 2088960 | tf_op jit(solution)/shard_map/reduce_scatter | solution.py:491
  (39 other events, 172.2 us)
Sparse Core Ops, SparseCore 0:
  12.0 121.6 all-gather.3
  136.6 80.0 all-gather.5
  219.5 80.1 all-gather.7
  340.9 75.3 reduce-scatter.6
  419.7 76.8 reduce-scatter.8
  594.3 46.0 reduce-scatter.12
  644.0 49.1 reduce-scatter.10
  696.7 84.0 reduce-scatter.14
  783.6 36.7 reduce-scatter.16

commit v4 on v3

--- a/solution.py
+++ b/solution.py
@@ -22,7 +22,7 @@
 
 
 def block_diag(tiled):
-    rows = lax.broadcasted_iota(jnp.int32, tiled.shape, 0)
+    rows = lax.broadcasted_iota(jnp.int32, tiled.shape, 0) % SUB
     cols = lax.broadcasted_iota(jnp.int32, tiled.shape, 1) // NST
     return jnp.where(rows == cols, tiled, 0.0)
 
@@ -36,6 +36,12 @@
     for by in (64, 32, 16):
         v = v + pltpu.roll(v, by, 1)
     return v
+
+
+def same_state():
+    rows = lax.broadcasted_iota(jnp.int32, (NST, SUB * NST), 0)
+    cols = lax.broadcasted_iota(jnp.int32, (NST, SUB * NST), 1) % NST
+    return jnp.where(rows == cols, 1.0, 0.0).astype(bf16)
 
 
 def fwd_kernel(delta_ref, u_ref, sb_ref, bx_ref, ct_ref, a2_ref, skip_ref, y_ref, ck_ref,
@@ -81,7 +87,7 @@
 
 def bwd_kernel(delta_ref, u_ref, sb_ref, bx_ref, cx_ref, bt_ref, ds_ref, ck_ref, a_ref, a2_ref,
                skip_ref, du_out, dr_out, db_out, dc_out, ga_out, gs_out, gb_out,
-               g_scr, dx_scr, du_scr, *, backwards, subs, width):
+               g_scr, dx_scr, du_scr, db_scr, dc_scr, *, backwards, subs, width):
     first = pl.program_id(1) == 0
     start = jnp.logical_and(first, pl.program_id(0) == 0)
     eg = pl.program_id(2)
@@ -100,8 +106,8 @@
 
     @pl.when(eg == 0)
     def _():
-        db_out[...] = jnp.zeros_like(db_out)
-        dc_out[...] = jnp.zeros_like(dc_out)
+        db_scr[...] = jnp.zeros_like(db_scr)
+        dc_scr[...] = jnp.zeros_like(dc_scr)
 
     order = list(range(SUB - 1, -1, -1) if backwards else range(SUB))
     nt = (((1,), (1,)), ((), ()))
@@ -114,6 +120,7 @@
         sb = twice(sb_ref[rows, :])
         b2 = split_hi_lo(block_diag(bt_ref[rows, :]))
         ones = block_diag(jnp.ones((SUB, SUB * NST), f32)).astype(bf16)
+        pick = same_state()
         db, dc = jnp.zeros((SUB, SUB * NST), f32), jnp.zeros((SUB, SUB * NST), f32)
         for p in range(width // PAIR):
             lanes = pl.ds(p * PAIR, PAIR)
@@ -126,28 +133,27 @@
             dx_scr[:, lanes] = delta + sb
             a2 = a2_ref[:, glob]
             h = ck_ref[sub, :, lanes]
-            prev, decay, states = [None] * SUB, [None] * SUB, [None] * SUB
+            decay, states, before = [None] * SUB, [None] * SUB, h.astype(bf16)
+            prev = [None] * SUB
             for t in order:
-                prev[t] = h
+                prev[t] = before
                 decay[t] = jnp.exp2(dx_scr[pl.ds(t, 1), lanes] * a2)
                 h = decay[t] * h + du_scr[pl.ds(t, 1), lanes] * twice(bx_ref[row0 + t])
-                states[t] = h.astype(bf16)
+                states[t] = before = h.astype(bf16)
             e2 = lax.dot_general(split_hi_lo(ds), jnp.concatenate(states, axis=0), nt,
                                  preferred_element_type=f32)
             dc = dc + (e2[:SUB] + e2[SUB:])
-            a = a_ref[:, glob]
+            a = a_ref[:, glob].astype(bf16)
             g = g_scr[:, glob]
-            ga = ga_out[:, glob]
-            lams, rs = [None] * SUB, [None] * SUB
+            lams, rs, gas = [None] * SUB, [None] * SUB, [None] * SUB
             for t in reversed(order):
                 lam = twice(cx_ref[row0 + t]) * ds_ref[pl.ds(row0 + t, 1), lanes] + g
                 lams[t] = lam.astype(bf16)
                 g = decay[t] * lam
-                r = g * prev[t] * a
-                rs[t] = r.astype(bf16)
-                ga = ga + dx_scr[pl.ds(t, 1), lanes] * r
+                rs[t] = g.astype(bf16) * prev[t] * a
+                gas[t] = rs[t] * jnp.broadcast_to(dx_scr[pl.ds(t, 1), lanes], (NST, PAIR)).astype(bf16)
             g_scr[:, glob] = g
-            ga_out[:, glob] = ga
+            ga_out[:, glob] += jnp.dot(pick, jnp.concatenate(gas, axis=0), preferred_element_type=f32)
             lams = jnp.concatenate(lams, axis=0)
             s2 = jnp.dot(b2, lams, preferred_element_type=f32)
             s1 = s2[:SUB] + s2[SUB:]
@@ -161,11 +167,16 @@
             gs_out[:, glob] += ds * u
             d2 = lax.dot_general(split_hi_lo(d_in), lams, nt, preferred_element_type=f32)
             db = db + (d2[:SUB] + d2[SUB:])
-        db_out[rows, :] += fold(db)
-        dc_out[rows, :] += fold(dc)
+        db_scr[rows, :] += db
+        dc_scr[rows, :] += dc
         return carry
 
     lax.fori_loop(0, subs, sub_step, 0)
+
+    @pl.when(eg == pl.num_programs(2) - 1)
+    def _():
+        db_out[...] = fold(db_scr[...])
+        dc_out[...] = fold(dc_scr[...])
 
 
 def lane_groups(width_all, widths):
@@ -176,7 +187,7 @@
 
 
 def scan_calls(rows, length, inner, backwards, tblock=128, width=None):
-    width = width or lane_groups(inner, (1536, 1024, 512, 256))
+    width = width or lane_groups(inner, (3072, 1536, 1024, 512, 256))
     n_t, n_e, subs = length // tblock, inner // width, tblock // SUB
     params = pltpu.CompilerParams(dimension_semantics=("arbitrary",) * 3)
 
@@ -212,7 +223,8 @@
         out_shape=[sds((rows, length, inner), f32), sds((rows, length, inner), bf16),
                    sds((rows, length, LANES), f32), sds((rows, length, LANES), f32),
                    sds((NST, inner), f32), sds((SUB, inner), f32), sds((SUB, inner), f32)],
-        scratch_shapes=[pltpu.VMEM((NST, inner), f32)] + [pltpu.VMEM((SUB, width), f32)] * 2,
+        scratch_shapes=[pltpu.VMEM((NST, inner), f32)] + [pltpu.VMEM((SUB, width), f32)] * 2
+        + [pltpu.VMEM((tblock, SUB * NST), f32)] * 2,
         compiler_params=params,
         name="scan_back_" + ("b" if backwards else "f"),
     )
@@ -529,7 +541,8 @@
             skip[d][None])
         dr = dr[0]
         if d == 1:
-            dr, early_o, early_z = lax.optimization_barrier((dr, early_o, early_z))
+            early = jnp.concatenate([early_o.reshape(ranks, -1, model)] + halves(early_z), axis=1)
+            dr, early = lax.optimization_barrier((dr, early))
         d_low = mm(dr, w_dt[d], ((1,), (0,)))
         d_proj = jnp.where(lane < rank, d_low, jnp.where(lane < rank + NST, db[0], dc[0])).astype(bf16)
         g_dt = mm(dr, dt_low, ((0,), (0,)))
@@ -544,7 +557,7 @@
     packed = jnp.concatenate([s[0].reshape(owners, -1) for s in sent], axis=1)
     span = sent[0][0].size // owners
     packed = jnp.pad(packed, ((0, 0), (0, -packed.shape[1] % (8 * model)))).reshape(-1, model)
-    early = over_fsdp(jnp.concatenate([early_o.reshape(ranks, -1, model)] + halves(early_z), axis=1))
+    early = over_fsdp(early)
     grad_out_w, grad_in_z = early[:own_inner], joined(early[own_inner:])
     packed = over_dp(packed)
     d_xs, g_cw, g_cb = conv_back_call(length, inner)(xs, d_us[0], d_us[1], masks, conv_w, conv_b)

time: 840 us -> 810 us (0.964)
  Pallas kernels: 327 us -> 282 us
    pallas_call x2, Pallas kernels: 179 us -> 142 us  [body(): calls[d][1]]
    unnamed x126 -> x132, local copies, waits for them, and re-layouts: 16.9 us -> 18.6 us
  transfers between devices with their start and end apart: 14 -> 14, of which waited for: 10 -> 10; matrix products, arithmetic and copies ran while one was open for 20% -> 20% of each run, Pallas kernels for 36% -> 32%
where the time goes in v4:
time: 810 us; the launch traced here: 802 us
  Pallas kernels  282 us (35%)
  waiting for transfers between devices  248 us (31%)
  local copies, waits for them, and re-layouts  108 us (13%)
  matrix products  89.7 us (11%)
  other arithmetic  33.3 us (4%)
  starting transfers between devices  24.9 us (3%)
  between operations  15.5 us (2%)
    pallas_call x2, Pallas kernels, body(): calls[d][1]  142 us
    dot_general x19, matrix products, mm(): return lax.dot_general(a, b, (dims, ((), ())), preferred_element_type=f32)  89.7 us
    all_gather x3, waiting for transfers between devices, gather0(): return lax.all_gather(v, AXES, axis=0, tiled=True)  69.7 us
    reduce_scatter x4, waiting for transfers between devices, body(): lax.psum_scatter(v, 'dp', scatter_dimension=0, tiled=True)  62.6 us
    pallas_call x2, Pallas kernels, body(): calls[d][0]  61.2 us
    all_to_all x1, waiting for transfers between devices, body(): lax.all_to_all(partial, AXES, 0, 0, tiled=True)  38.7 us
    all_to_all x2, waiting for transfers between devices, to_all(): lax.all_to_all(jnp.broadcast_to(v[None], (owners,) + v.shape), AXES, 0, 0...  35.5 us
    reduce_scatter x2, waiting for transfers between devices, body(): lax.psum_scatter(v.reshape(-1, model), 'fsdp', scatter_dimension=0, tiled...  27.2 us
  transfers between devices with their start and end apart: 14, of which 10 were waited for; matrix products, arithmetic and copies ran while one was open for 20% of the time, Pallas kernels for 32%

profile of v4, /device:TPU:0, one launch (start us, length us, event | category | flops | bytes accessed | tf_op | source)
XLA Modules:
  0.0 801.7 jit_solution(6226364558623015627)
XLA Ops:
  13.6 7.3 all-to-all-start
  20.9 21.1 %all-to-all-done = bf16[32,64,128]{2,1,0:T(8,128)(2,1)S(1)} async-done(((bf16[32,64,128]{2,1,0:T(8,128)(2,1)}), bf16[32,64,128]{2,1,0:T(8,128)(2,1)S(1)}, u32[]{:S(2)}, u32[]{:S(2)}) %all-to-all-start) | async-done | bytes 524320 | tf_op jit(solution)/shard_map/all_to_all | solution.py:400
  46.1 5.4 all-to-all-start.1
  54.2 38.7 %all-to-all-done.1 = f32[32,2,4608]{2,1,0:T(2,128)S(1)} async-done(((f32[32,2,4608]{2,1,0:T(2,128)}), f32[32,2,4608]{2,1,0:T(2,128)S(1)}, u32[]{:S(2)}, u32[]{:S(2)}) %all-to-all-start.1) | async-done | bytes 1179680 | tf_op jit(solution)/shard_map/all_to_all | solution.py:453
  97.8 36.0 %all-gather.4.cloned.1.call-done = bf16[2048,3072]{1,0:T(8,128)(2,1)} async-done(((bf16[64,3072]{1,0:T(8,128)(2,1)}), bf16[2048,3072]{1,0:T(8,128)(2,1)}) %all-gather.4.cloned.1.call-update) | async-done | bytes 12582928 | tf_op jit(solution)/shard_map/all_gather | solution.py:404
  148.9 6.1 reshape.406
  154.9 16.8 %project_conv.1 = (f32[512,3072]{1,0:T(8,128)}, bf16[512,3072]{1,0:T(8,128)(2,1)}, bf16[512,3072]{1,0:T(8,128)(2,1)}) custom-call(bf16[512,1536]{1,0:T(8,128)(2,1)} %get-tuple-element.59.h_ref, bf16[32,64,3072]{2,1,0:T(8,128)(2,1)} %bitcast.237, f32[6,512,128]{2,1,0:T(8,128)} %broadcast_in_dim.200.masks_ref, f32[2,4,3072]{2,1,0:T(4,128)} %reshape.433.w_ref, ...), custom_call_target="tpu_custom_call" | custom-call | tf_op jit(solution)/shard_map/project_conv/pallas_call | solution.py:483
  184.1 7.3 fusion.3.delta_ref
  195.0 31.6 %scan_ahead_b.1 = (f32[1,512,3072]{2,1,0:T(8,128)}, f32[1,32,16,3072]{3,2,1,0:T(8,128)}) custom-call(f32[1,512,3072]{2,1,0:T(8,128)} %fusion.3.delta_ref, bf16[1,512,3072]{2,1,0:T(8,128)(2,1)} %bitcast.232, f32[1,512,128]{2,1,0:T(8,128)} %broadcast_in_dim.207.sb_ref, f32[1,512,16,128]{3,2,1,0:T(8,128)} %broadcast_in_dim.208.bx_ref, ...), custom_call_target="tpu_custom_call" | custom-call | tf_op jit(solution)/shard_map/scan_ahead_b/pallas_call | solution.py:495
  226.6 6.3 fusion.2.delta_ref
  236.3 29.6 %scan_ahead_f.1 = (f32[1,512,3072]{2,1,0:T(8,128)}, f32[1,32,16,3072]{3,2,1,0:T(8,128)}) custom-call(f32[1,512,3072]{2,1,0:T(8,128)} %fusion.2.delta_ref, bf16[1,512,3072]{2,1,0:T(8,128)(2,1)} %bitcast.234, f32[1,512,128]{2,1,0:T(8,128)} %broadcast_in_dim.203.sb_ref, f32[1,512,16,128]{3,2,1,0:T(8,128)} %broadcast_in_dim.204.bx_ref, ...), custom_call_target="tpu_custom_call" | custom-call | tf_op jit(solution)/shard_map/scan_ahead_f/pallas_call | solution.py:495
  266.0 33.7 %all-gather.8.cloned.1.call-done.wo_ref = bf16[3072,1536]{1,0:T(8,128)(2,1)} async-done(((bf16[96,1536]{1,0:T(8,128)(2,1)}), bf16[3072,1536]{1,0:T(8,128)(2,1)}) %all-gather.8.cloned.1.call-update) | async-done | bytes 9437200 | tf_op jit(solution)/shard_map/all_gather | solution.py:404
  299.6 22.6 %gate.1 = (bf16[512,3072]{1,0:T(8,128)(2,1)}, f32[512,3072]{1,0:T(8,128)}, bf16[512,3072]{1,0:T(8,128)(2,1)}) custom-call(bf16[512,1536]{1,0:T(8,128)(2,1)} %get-tuple-element.59.h_ref, bf16[512,1536]{1,0:T(8,128)(2,1)} %get-tuple-element.224.g_ref, bf16[1536,3072]{1,0:T(8,128)(2,1)} %all-gather.6.cloned.1.call-done.wz_ref, ...), custom_call_target="tpu_custom_call" | custom-call | tf_op jit(solution)/shard_map/gate/pallas_call | solution.py:497
  322.2 9.3 %convolution_convert_fusion.1 = bf16[1536,3072]{1,0:T(8,128)(2,1)} fusion(bf16[512,1536]{1,0:T(8,128)(2,1)S(1)} %copy-done.7, bf16[512,3072]{1,0:T(8,128)(2,1)} %get-tuple-element.71.dz_ref), kind=kOutput, calls=%fused_computation.3 | convolution fusion | flops 4836556800 | bytes 14155776 | tf_op jit(solution)/shard_map/dot_general | solution.py:395
  331.5 9.3 %convolution_convert_fusion.2 = bf16[3072,1536]{1,0:T(8,128)(2,1)} fusion(bf16[512,3072]{1,0:T(8,128)(2,1)} %get-tuple-element.68, bf16[512,1536]{1,0:T(8,128)(2,1)} %get-tuple-element.224.g_ref), kind=kOutput, calls=%fused_computation.4 | convolution fusion | flops 4836556800 | bytes 14155776 | tf_op jit(solution)/shard_map/dot_general | solution.py:395
  349.5 71.7 %scan_back_f.1 = (f32[1,512,3072]{2,1,0:T(8,128)}, bf16[1,512,3072]{2,1,0:T(8,128)(2,1)}, f32[1,512,128]{2,1,0:T(8,128)}, f32[1,512,128]{2,1,0:T(8,128)}, f32[16...) custom-call(f32[1,512,3072]{2,1,0:T(8,128)} %fusion.2.delta_ref, bf16[1,512,3072]{2,1,0:T(8,128)(2,1)} %bitcast.235, ...), custom_call_target="tpu_custom_call" | custom-call | tf_op jit(solution)/shard_map/scan_back_f/pallas_call | solution.py:539
  421.1 4.7 copy.136
  451.1 70.1 %scan_back_b.1 = (f32[1,512,3072]{2,1,0:T(8,128)}, bf16[1,512,3072]{2,1,0:T(8,128)(2,1)}, f32[1,512,128]{2,1,0:T(8,128)}, f32[1,512,128]{2,1,0:T(8,128)}, f32[16...) custom-call(f32[1,512,3072]{2,1,0:T(8,128)} %fusion.3.delta_ref, bf16[1,512,3072]{2,1,0:T(8,128)(2,1)} %bitcast.233, ...), custom_call_target="tpu_custom_call" | custom-call | tf_op jit(solution)/shard_map/scan_back_b/pallas_call | solution.py:539
  554.0 6.6 bitcast_add_fusion.du1_ref
  565.7 5.6 reshape.415
  571.4 6.4 bitcast_add_fusion.1.du0_ref
  577.8 22.7 %conv_back.1 = (bf16[512,3072]{1,0:T(8,128)(2,1)}, f32[2,4,3072]{2,1,0:T(4,128)}, f32[2,3072]{1,0:T(2,128)}) custom-call(f32[512,3072]{1,0:T(8,128)} %get-tuple-element.69.x_ref, f32[512,3072]{1,0:T(8,128)} %bitcast_add_fusion.1.du0_ref, f32[512,3072]{1,0:T(8,128)} %bitcast_add_fusion.du1_ref, f32[6,512,128]{2,1,0:T(8,128)} %broadcast_in_dim.200.masks_ref, ...), custom_call_target="tpu_custom_call" | custom-call | tf_op jit(solution)/shard_map/conv_back/pallas_call | solution.py:563
  600.5 9.4 %convolution_convert_fusion = bf16[1536,3072]{1,0:T(8,128)(2,1)} fusion(bf16[512,1536]{1,0:T(8,128)(2,1)S(1)} %copy-done.7, bf16[512,3072]{1,0:T(8,128)(2,1)} %get-tuple-element.94.dx_ref), kind=kOutput, calls=%fused_computation.2 | convolution fusion | flops 4836556800 | bytes 14155776 | tf_op jit(solution)/shard_map/dot_general | solution.py:395
  610.0 50.8 %reduce-scatter.11.cloned.1.call-done = bf16[160,1536]{1,0:T(8,128)(2,1)} async-done(((bf16[1280,1536]{1,0:T(8,128)(2,1)}), bf16[160,1536]{1,0:T(8,128)(2,1)}) %reduce-scatter.11.cloned.1.call-update) | async-done | bytes 491536 | tf_op jit(solution)/shard_map/reduce_scatter | solution.py:502
  660.9 17.1 %back_project.1 = f32[512,1536]{1,0:T(8,128)} custom-call(bf16[512,3072]{1,0:T(8,128)(2,1)} %get-tuple-element.94.dx_ref, bf16[512,3072]{1,0:T(8,128)(2,1)} %get-tuple-element.71.dz_ref, bf16[32,64,3072]{2,1,0:T(8,128)(2,1)} %bitcast.238, bf16[1536,3072]{1,0:T(8,128)(2,1)} %all-gather.6.cloned.1.call-done.wz_ref), custom_call_target="tpu_custom_call" | custom-call | tf_op jit(solution)/shard_map/back_project/pallas_call | solution.py:570
  678.1 15.1 %select_reduce_fusion.3 = (bf16[1536]{0:T(1024)(128)(2,1)S(1)}, bf16[1536]{0:T(1024)(128)(2,1)S(1)}, f32[512]{0:T(512)S(1)}, f32[512]{0:T(512)S(1)}, bf16[1536]{...) fusion(f32[512,1536]{1,0:T(8,128)} %back_project.1, ...), kind=kOutput, calls=%fused_computation.44 | convolution fusion | flops 4853848064 | bytes 20498944 | tf_op jit(solution)/shard_map/dot_general | solution.py:395
  694.5 4.9 all-to-all-start.2
  700.5 14.3 %all-to-all-done.2 = bf16[32,2,4608]{2,1,0:T(2,128)(2,1)S(1)} async-done(((bf16[32,2,4608]{2,1,0:T(2,128)(2,1)}), bf16[32,2,4608]{2,1,0:T(2,128)(2,1)S(1)}, u32[]{:S(2)}, u32[]{:S(2)}) %all-to-all-start.2) | async-done | bytes 589856 | tf_op jit(solution)/shard_map/all_to_all | solution.py:400
  720.2 6.6 all-to-all-done.4
  730.1 6.5 all-to-all-done.3
  736.6 11.7 %reduce-scatter.15.cloned.1.call-done = bf16[192,3072]{1,0:T(8,128)(2,1)} async-done(((bf16[1536,3072]{1,0:T(8,128)(2,1)}), bf16[192,3072]{1,0:T(8,128)(2,1)}) %reduce-scatter.15.cloned.1.call-update) | async-done | bytes 1179664 | tf_op jit(solution)/shard_map/reduce_scatter | solution.py:502
  760.7 27.2 %reduce-scatter.17.cloned.1.call-done = bf16[136,1536]{1,0:T(8,128)(2,1)} async-done(((bf16[544,1536]{1,0:T(8,128)(2,1)}), bf16[136,1536]{1,0:T(8,128)(2,1)}) %reduce-scatter.17.cloned.1.call-update) | async-done | bytes 417808 | tf_op jit(solution)/shard_map/reduce_scatter | solution.py:503
  (335 shorter events, 153.6 us)
Async XLA Ops:
  7.2 36.8 %copy-start = (bf16[48,4608]{1,0:T(8,128)(2,1)S(1)}, bf16[48,4608]{1,0:T(8,128)(2,1)}, u32[]{:S(2)}) copy-start(bf16[48,4608]{1,0:T(8,128)(2,1)} %param.28) | copy-start | bytes 1327108
  7.3 126.5 %all-gather.4.cloned.1.call-start = ((), (), s32[]{:S(2)}) async-start(), calls=%async_computation.11 | async-start | bytes 12976128 | tf_op jit(solution)/shard_map/all_gather | solution.py:404
  13.6 28.5 %all-to-all-start = ((bf16[32,64,128]{2,1,0:T(8,128)(2,1)}), bf16[32,64,128]{2,1,0:T(8,128)(2,1)S(1)}, u32[]{:S(2)}, u32[]{:S(2)}) async-start(bf16[32,64,128]{2,1,0:T(8,128)(2,1)} %broadcast_in_dim.193), calls=%async_computation | async-start | bytes 1048576 | tf_op jit(solution)/shard_map/all_to_all | solution.py:400
  46.1 46.8 %all-to-all-start.1 = ((f32[32,2,4608]{2,1,0:T(2,128)}), f32[32,2,4608]{2,1,0:T(2,128)S(1)}, u32[]{:S(2)}, u32[]{:S(2)}) async-start(f32[32,2,4608]{2,1,0:T(2,128)} %reshape.403), calls=%async_computation.1 | async-start | bytes 2359296 | tf_op jit(solution)/shard_map/all_to_all | solution.py:453
  51.5 214.4 %all-gather.6.cloned.1.call-start = ((), (), s32[]{:S(2)}) async-start(), calls=%async_computation.12 | async-start | bytes 9732096 | tf_op jit(solution)/shard_map/all_gather | solution.py:404
  52.2 45.5 %copy-start.53 = (pred[512]{0:T(512)(128)(4,1)}, pred[512]{0:T(512)(128)(4,1)S(1)}, u32[]{:S(2)}) copy-start(pred[512]{0:T(512)(128)(4,1)S(1)} %get-tuple-element.180) | copy-start | bytes 1540
  52.7 45.0 %copy-start.44 = (f32[512]{0:T(512)}, f32[512]{0:T(512)S(1)}, u32[]{:S(2)}) copy-start(f32[512]{0:T(512)S(1)} %broadcast_multiply_fusion.5) | copy-start | bytes 6148
  53.3 44.5 %copy-start.50 = (f32[512]{0:T(512)}, f32[512]{0:T(512)S(1)}, u32[]{:S(2)}) copy-start(f32[512]{0:T(512)S(1)} %add_rsqrt_fusion) | copy-start | bytes 6148
  97.8 43.2 %copy-start.17 = (f32[32,3072]{1,0:T(8,128)S(1)}, f32[32,3072]{1,0:T(8,128)}, u32[]{:S(2)}) copy-start(f32[32,3072]{1,0:T(8,128)} %get-tuple-element.200) | copy-start | bytes 1179652
  135.4 164.2 %all-gather.8.cloned.1.call-start = ((), (), s32[]{:S(2)}) async-start(), calls=%async_computation.13 | async-start | bytes 9732096 | tf_op jit(solution)/shard_map/all_gather | solution.py:404
  136.1 395.4 %reduce-scatter.9.cloned.1.call-start = ((), (), s32[]{:S(2)}) async-start(), calls=%async_computation.15 | async-start | bytes 10616832 | tf_op jit(solution)/shard_map/reduce_scatter | solution.py:502
  174.0 52.6 %copy-start.12 = (bf16[1,1,32,96,128]{4,3,1,0,2:T(8,128)(2,1)}, bf16[1,1,32,96,128]{4,3,1,0,2:T(8,128)(2,1)S(1)}, u32[]{:S(2)}) copy-start(bf16[1,1,32,96,128]{4,3,1,0,2:T(8,128)(2,1)S(1)} %get-tuple-element.185) | copy-start | bytes 2359300
  195.0 31.6 %copy-start.21 = (f32[512,128]{0,1:T(8,128)S(1)}, f32[512,128]{0,1:T(8,128)}, u32[]{:S(2)}) copy-start(f32[512,128]{0,1:T(8,128)} %copy-done.20) | copy-start | bytes 786436
  299.6 22.6 %copy-start.7 = (bf16[512,1536]{1,0:T(8,128)(2,1)S(1)}, bf16[512,1536]{1,0:T(8,128)(2,1)}, u32[]{:S(2)}) copy-start(bf16[512,1536]{1,0:T(8,128)(2,1)} %get-tuple-element.59.h_ref) | copy-start | bytes 4718596
  340.9 192.7 %reduce-scatter.7.cloned.1.call-start = ((), (), s32[]{:S(2)}) async-start(), calls=%async_computation.14 | async-start | bytes 10616832 | tf_op jit(solution)/shard_map/reduce_scatter | solution.py:502
  341.5 268.5 %reduce-scatter.13.cloned.1.call-start = ((), (), s32[]{:S(2)}) async-start(), calls=%async_computation.17 | async-start | bytes 2949120 | tf_op jit(solution)/shard_map/reduce_scatter | solution.py:503
  562.2 98.5 %reduce-scatter.11.cloned.1.call-start = ((), (), s32[]{:S(2)}) async-start(), calls=%async_computation.16 | async-start | bytes 4423680 | tf_op jit(solution)/shard_map/reduce_scatter | solution.py:502
  571.4 177.0 %reduce-scatter.15.cloned.1.call-start = ((), (), s32[]{:S(2)}) async-start(), calls=%async_computation.18 | async-start | bytes 10616832 | tf_op jit(solution)/shard_map/reduce_scatter | solution.py:502
  660.8 17.2 %copy-start.5 = (bf16[1,512,1536]{2,1,0:T(8,128)(2,1)S(1)}, bf16[1,512,1536]{2,1,0:T(8,128)(2,1)}, u32[]{:S(2)}) copy-start(bf16[1,512,1536]{2,1,0:T(8,128)(2,1)} %param.15) | copy-start | bytes 4718596
  660.8 17.2 %copy-start.37 = (f32[1536]{0:T(1024)S(1)}, f32[1536]{0:T(1024)}, u32[]{:S(2)}) copy-start(f32[1536]{0:T(1024)} %copy-done.36) | copy-start | bytes 18436
  660.8 17.2 %copy-start.39 = (f32[1536]{0:T(1024)S(1)}, f32[1536]{0:T(1024)}, u32[]{:S(2)}) copy-start(f32[1536]{0:T(1024)} %copy-done.38) | copy-start | bytes 18436
  660.8 17.2 %copy-start.41 = (f32[1536]{0:T(1024)S(1)}, f32[1536]{0:T(1024)}, u32[]{:S(2)}) copy-start(f32[1536]{0:T(1024)} %copy-done.40) | copy-start | bytes 18436
  660.8 17.2 %copy-start.43 = (f32[1536]{0:T(1024)S(1)}, f32[1536]{0:T(1024)}, u32[]{:S(2)}) copy-start(f32[1536]{0:T(1024)} %copy-done.42) | copy-start | bytes 18436
  660.9 17.2 %copy-start.45 = (f32[512]{0:T(512)S(1)}, f32[512]{0:T(512)}, u32[]{:S(2)}) copy-start(f32[512]{0:T(512)} %copy-done.44) | copy-start | bytes 6148
  660.9 17.2 %copy-start.51 = (f32[512]{0:T(512)S(1)}, f32[512]{0:T(512)}, u32[]{:S(2)}) copy-start(f32[512]{0:T(512)} %copy-done.50) | copy-start | bytes 6148
  678.1 21.3 %copy-start.35 = (f32[2,4,3072]{2,1,0:T(4,128)S(1)}, f32[2,4,3072]{2,1,0:T(4,128)}, u32[]{:S(2)}) copy-start(f32[2,4,3072]{2,1,0:T(4,128)} %get-tuple-element.99) | copy-start | bytes 294916
  678.1 21.5 %copy-start.46 = (f32[2,3072]{1,0:T(2,128)S(1)}, f32[2,3072]{1,0:T(2,128)}, u32[]{:S(2)}) copy-start(f32[2,3072]{1,0:T(2,128)} %get-tuple-element.100) | copy-start | bytes 73732
  693.3 56.4 %copy-start.27 = (bf16[160,1536]{1,0:T(8,128)(2,1)S(1)}, bf16[160,1536]{1,0:T(8,128)(2,1)}, u32[]{:S(2)}) copy-start(bf16[160,1536]{1,0:T(8,128)(2,1)} %reduce-scatter.11.cloned.1.call-done) | copy-start | bytes 1474564
  694.5 20.4 %all-to-all-start.2 = ((bf16[32,2,4608]{2,1,0:T(2,128)(2,1)}), bf16[32,2,4608]{2,1,0:T(2,128)(2,1)S(1)}, u32[]{:S(2)}, u32[]{:S(2)}) async-start(bf16[32,2,4608]{2,1,0:T(2,128)(2,1)} %broadcast_in_dim.218), calls=%async_computation.7 | async-start | bytes 1179648 | tf_op jit(solution)/shard_map/all_to_all | solution.py:400
  714.9 11.9 %all-to-all-start.4 = ((bf16[32,8,128]{2,1,0:T(8,128)(2,1)}), bf16[32,8,128]{2,1,0:T(8,128)(2,1)S(1)}, u32[]{:S(2)}, u32[]{:S(2)}) async-start(bf16[32,8,128]{2,1,0:T(8,128)(2,1)} %bitcast.94), calls=%async_computation.9 | async-start | bytes 131072 | tf_op jit(solution)/shard_map/all_to_all | solution.py:523
  726.8 9.9 %all-to-all-start.3 = ((f32[32,2,48]{2,1,0:T(2,128)}), f32[32,2,48]{2,1,0:T(2,128)S(1)}, u32[]{:S(2)}, u32[]{:S(2)}) async-start(f32[32,2,48]{2,1,0:T(2,128)} %copy.142), calls=%async_computation.8 | async-start | bytes 65536 | tf_op jit(solution)/shard_map/all_to_all | solution.py:585
  729.3 58.6 %reduce-scatter.17.cloned.1.call-start = ((), (), s32[]{:S(2)}) async-start(), calls=%async_computation.19 | async-start | bytes 2088960 | tf_op jit(solution)/shard_map/reduce_scatter | solution.py:503
  (42 other events, 190.0 us)
Sparse Core Ops, SparseCore 0:
  12.0 121.6 all-gather.3
  136.6 80.0 all-gather.5
  219.5 80.0 all-gather.7
  341.0 75.3 reduce-scatter.8
  419.7 76.8 reduce-scatter.6
  562.4 45.6 reduce-scatter.12
  611.5 49.1 reduce-scatter.10
  664.3 84.0 reduce-scatter.14
  751.2 36.7 reduce-scatter.16

commit v5 on v4

--- a/solution.py
+++ b/solution.py
@@ -308,36 +308,46 @@
             dx_ref[pl.ds(row0, chunk), lanes] = total.astype(bf16)
 
 
-def gate_kernel(h_ref, g_ref, wz_ref, wo_ref, y0_ref, y1_ref, gated_ref, ds_ref, dz_ref, z_scr, d_scr,
-                *, length, chunk):
-    z_scr[...] = jnp.dot(h_ref[...], wz_ref[...], preferred_element_type=f32)
-    d_scr[...] = lax.dot_general(g_ref[...], wo_ref[...], (((1,), (1,)), ((), ())),
-                                 preferred_element_type=f32)
+def gate_kernel(h_ref, wz_ref, y0_ref, y1_ref, gated_ref, silu_ref, slope_ref, *, length, chunk):
+    silu_ref[...] = jnp.dot(h_ref[...], wz_ref[...], preferred_element_type=f32)
     for row0 in range(0, length, chunk):
         rows = pl.ds(row0, chunk)
-        z, d_gated = z_scr[rows, :], d_scr[rows, :]
+        z = silu_ref[rows, :]
         both = y0_ref[rows, :] + y1_ref[rows, :]
         sig = jax.nn.sigmoid(z)
         silu = z * sig
         gated_ref[rows, :] = (both * silu).astype(bf16)
-        ds_ref[rows, :] = d_gated * silu
-        dz_ref[rows, :] = (d_gated * both * sig * (1.0 + z * (1.0 - sig))).astype(bf16)
-
-
-def gate_call(length, model, inner, width=384, chunk=32):
+        silu_ref[rows, :] = silu
+        slope_ref[rows, :] = both * sig * (1.0 + z * (1.0 - sig))
+
+
+def gate_back_kernel(g_ref, wo_ref, silu_ref, slope_ref, ds_ref, dz_ref, *, length, chunk):
+    ds_ref[...] = lax.dot_general(g_ref[...], wo_ref[...], (((1,), (1,)), ((), ())),
+                                  preferred_element_type=f32)
+    for row0 in range(0, length, chunk):
+        rows = pl.ds(row0, chunk)
+        d_gated = ds_ref[rows, :]
+        ds_ref[rows, :] = d_gated * silu_ref[rows, :]
+        dz_ref[rows, :] = (d_gated * slope_ref[rows, :]).astype(bf16)
+
+
+def gate_calls(length, model, inner, width=384, chunk=32):
     if inner % width:
         width = PAIR
     tok = pl.BlockSpec((length, width), lambda e: (0, e))
     every = pl.BlockSpec((length, model), lambda e: (0, 0))
-    sds = jax.ShapeDtypeStruct
-    return pl.pallas_call(
+    low = jax.ShapeDtypeStruct((length, inner), bf16)
+    high = jax.ShapeDtypeStruct((length, inner), f32)
+    params = pltpu.CompilerParams(dimension_semantics=("arbitrary",))
+    ahead = pl.pallas_call(
         functools.partial(gate_kernel, length=length, chunk=chunk), grid=(inner // width,),
-        in_specs=[every, every, pl.BlockSpec((model, width), lambda e: (0, e)),
-                  pl.BlockSpec((width, model), lambda e: (e, 0)), tok, tok],
-        out_specs=[tok, tok, tok],
-        out_shape=[sds((length, inner), bf16), sds((length, inner), f32), sds((length, inner), bf16)],
-        scratch_shapes=[pltpu.VMEM((length, width), f32)] * 2,
-        compiler_params=pltpu.CompilerParams(dimension_semantics=("arbitrary",)), name="gate")
+        in_specs=[every, pl.BlockSpec((model, width), lambda e: (0, e)), tok, tok],
+        out_specs=[tok, tok, tok], out_shape=[low, high, high], compiler_params=params, name="gate")
+    back = pl.pallas_call(
+        functools.partial(gate_back_kernel, length=length, chunk=chunk), grid=(inner // width,),
+        in_specs=[every, pl.BlockSpec((width, model), lambda e: (e, 0)), tok, tok],
+        out_specs=[tok, tok], out_shape=[high, low], compiler_params=params, name="gate_back")
+    return ahead, back
 
 
 def projection_calls(length, model, inner, blocks, width=512, chunk=64):
@@ -494,9 +504,11 @@
         b_wide = wide(b_m)
         y, ck = calls[d][0](delta[None], u[None], sb, b_wide, tile(c_m), rate2, skip[d][None])
         kept.append((u, dt_low, b_m, c_m, delta, rate, rate2, sb, b_wide, y[0], ck))
-    gated, d_scan, d_z = gate_call(length, model, inner)(
-        hidden, d_branch, w_z, w_o, kept[0][9], kept[1][9])
+    gate_ahead, gate_back = gate_calls(length, model, inner)
+    gated, silu_z, slope = gate_ahead(hidden, w_z, kept[0][9], kept[1][9])
     grad_out_w = mm(gated, d_branch, ((0,), (0,))).astype(bf16)
+    d_branch, grad_out_w = lax.optimization_barrier((d_branch, grad_out_w))
+    d_scan, d_z = gate_back(d_branch, w_o, silu_z, slope)
     grad_in_z = mm(hidden, d_z, ((0,), (0,))).astype(bf16)
     d_scan, grad_out_w, grad_in_z = lax.optimization_barrier((d_scan, grad_out_w, grad_in_z))
     over_dp = lambda v: lax.psum_scatter(v, "dp", scatter_dimension=0, tiled=True)
@@ -504,7 +516,8 @@
     ranks = lax.axis_size("fsdp")
     halves = lambda v: [h.reshape(ranks, -1, model) for h in jnp.split(v, inner // model, axis=1)]
     joined = lambda v: jnp.concatenate(jnp.split(v, inner // model, axis=0), axis=1)
-    early_o, early_z = over_dp(grad_out_w), over_dp(grad_in_z)
+    grad_out_w = lax.psum_scatter(grad_out_w, AXES, scatter_dimension=0, tiled=True)
+    grad_in_z = over_dp(grad_in_z)
     branch = mm(gated, w_o, ((1,), (0,)))
     block_out = (x + pick(gate) * branch).astype(bf16)
     d_gate = g * branch
@@ -541,8 +554,7 @@
             skip[d][None])
         dr = dr[0]
         if d == 1:
-            early = jnp.concatenate([early_o.reshape(ranks, -1, model)] + halves(early_z), axis=1)
-            dr, early = lax.optimization_barrier((dr, early))
+            dr, grad_in_z = lax.optimization_barrier((dr, grad_in_z))
         d_low = mm(dr, w_dt[d], ((1,), (0,)))
         d_proj = jnp.where(lane < rank, d_low, jnp.where(lane < rank + NST, db[0], dc[0])).astype(bf16)
         g_dt = mm(dr, dt_low, ((0,), (0,)))
@@ -557,13 +569,12 @@
     packed = jnp.concatenate([s[0].reshape(owners, -1) for s in sent], axis=1)
     span = sent[0][0].size // owners
     packed = jnp.pad(packed, ((0, 0), (0, -packed.shape[1] % (8 * model)))).reshape(-1, model)
-    early = over_fsdp(early)
-    grad_out_w, grad_in_z = early[:own_inner], joined(early[own_inner:])
+    d_us[0], d_us[1], grad_out_w, packed = lax.optimization_barrier((d_us[0], d_us[1], grad_out_w, packed))
     packed = over_dp(packed)
     d_xs, g_cw, g_cb = conv_back_call(length, inner)(xs, d_us[0], d_us[1], masks, conv_w, conv_b)
     grad_in_x = mm(hidden, d_xs, ((0,), (0,))).astype(bf16)
 
-    grad_in_x = over_dp(tied(grad_in_x, packed, early))
+    grad_in_x = over_dp(tied(grad_in_x, packed))
     flat, shapes = send((g_cw, g_cb), (2, 1))
     g_cw, g_cb = receive(exchange(flat), shapes)
 
@@ -584,10 +595,11 @@
     d_act = mm(d_mods_all, mod_weight, ((1,), (1,))).reshape(owners, 2, own_model)
     d_act = lax.all_to_all(d_act, AXES, 0, 0, tiled=True)
     grad_in_x, d_act, g_cw = lax.optimization_barrier((grad_in_x, d_act, g_cw))
-    late = over_fsdp(jnp.concatenate(halves(grad_in_x) + [packed.reshape(ranks, -1, model)], axis=1))
+    late = halves(grad_in_x) + halves(grad_in_z) + [packed.reshape(ranks, -1, model)]
+    late = over_fsdp(jnp.concatenate(late, axis=1))
     count = own_model * (inner // model)
-    grad_in = jnp.concatenate([joined(late[:count]), grad_in_z], axis=1).astype(f32)
-    packed = late[count:].reshape(-1)[:2 * span].astype(f32).reshape(2, -1)
+    grad_in = jnp.concatenate([joined(late[:count]), joined(late[count:2 * count])], axis=1).astype(f32)
+    packed = late[2 * count:].reshape(-1)[:2 * span].astype(f32).reshape(2, -1)
     g_xp, g_dt, g_db, g_al, g_sk = [
         jnp.stack(v) for v in zip(*(receive(packed[d], sent[d][1]) for d in range(2)))]
     g_dt = jnp.swapaxes(g_dt[..., :rank], 1, 2)

time: 810 us -> 780 us (0.963)
  waiting for transfers between devices: 248 us -> 198 us
  Pallas kernels: 282 us -> 297 us
    reduce_scatter x4 -> x3, waiting for transfers between devices: 62.6 us -> 27.2 us  [body(): lax.psum_scatter(v, 'dp', scatter_dimension=0, tiled=True)]
    all_gather x3, waiting for transfers between devices: 69.7 us -> 39.1 us  [gather0(): return lax.all_gather(v, AXES, axis=0, tiled=True)]
    reduce_scatter x2 -> x1, waiting for transfers between devices: 27.2 us -> 44.8 us  [body(): lax.psum_scatter(v.reshape(-1, model), 'fsdp', scatter_dimension=0, tiled...]
    pallas_call x1 -> x2, Pallas kernels: 22.6 us -> 37 us  [the longest x1 20.5 us: body(): gated, silu_z, slope = gate_ahead(hidden, w_z, kept[0][9], kept[1][9])]
    unnamed x132 -> x138, local copies, waits for them, and re-layouts: 18.6 us -> 20.7 us
  transfers between devices with their start and end apart: 14 -> 13, of which waited for: 10 -> 10; matrix products, arithmetic and copies ran while one was open for 20% -> 26% of each run, Pallas kernels for 32% -> 36%
where the time goes in v5:
time: 780 us; the launch traced here: 772 us
  Pallas kernels  297 us (38%)
  waiting for transfers between devices  198 us (25%)
  local copies, waits for them, and re-layouts  112 us (14%)
  matrix products  95.1 us (12%)
  other arithmetic  29.6 us (4%)
  starting transfers between devices  25 us (3%)
  between operations  15.7 us (2%)
    pallas_call x2, Pallas kernels, body(): calls[d][1]  142 us
    dot_general x19, matrix products, mm(): return lax.dot_general(a, b, (dims, ((), ())), preferred_element_type=f32)  95.1 us
    pallas_call x2, Pallas kernels, body(): calls[d][0]  61.3 us
    reduce_scatter x1, waiting for transfers between devices, body(): lax.psum_scatter(v.reshape(-1, model), 'fsdp', scatter_dimension=0, tiled...  44.8 us
    all_gather x3, waiting for transfers between devices, gather0(): return lax.all_gather(v, AXES, axis=0, tiled=True)  39.1 us
    all_to_all x1, waiting for transfers between devices, body(): lax.all_to_all(partial, AXES, 0, 0, tiled=True)  38.7 us
    all_to_all x2, waiting for transfers between devices, to_all(): lax.all_to_all(jnp.broadcast_to(v[None], (owners,) + v.shape), AXES, 0, 0...  33.3 us
    reduce_scatter x3, waiting for transfers between devices, body(): lax.psum_scatter(v, 'dp', scatter_dimension=0, tiled=True)  27.2 us
  transfers between devices with their start and end apart: 13, of which 10 were waited for; matrix products, arithmetic and copies ran while one was open for 26% of the time, Pallas kernels for 36%

profile of v5, /device:TPU:0, one launch (start us, length us, event | category | flops | bytes accessed | tf_op | source)
XLA Modules:
  0.0 771.5 jit_solution(2565858018899635374)
XLA Ops:
  13.6 7.3 all-to-all-start
  20.9 21.1 %all-to-all-done = bf16[32,64,128]{2,1,0:T(8,128)(2,1)S(1)} async-done(((bf16[32,64,128]{2,1,0:T(8,128)(2,1)}), bf16[32,64,128]{2,1,0:T(8,128)(2,1)S(1)}, u32[]{:S(2)}, u32[]{:S(2)}) %all-to-all-start) | async-done | bytes 524320 | tf_op jit(solution)/shard_map/all_to_all | solution.py:410
  46.2 5.4 all-to-all-start.1
  54.2 38.7 %all-to-all-done.1 = f32[32,2,4608]{2,1,0:T(2,128)S(1)} async-done(((f32[32,2,4608]{2,1,0:T(2,128)}), f32[32,2,4608]{2,1,0:T(2,128)S(1)}, u32[]{:S(2)}, u32[]{:S(2)}) %all-to-all-start.1) | async-done | bytes 1179680 | tf_op jit(solution)/shard_map/all_to_all | solution.py:463
  97.8 36.0 %all-gather.4.cloned.1.call-done = bf16[2048,3072]{1,0:T(8,128)(2,1)} async-done(((bf16[64,3072]{1,0:T(8,128)(2,1)}), bf16[2048,3072]{1,0:T(8,128)(2,1)}) %all-gather.4.cloned.1.call-update) | async-done | bytes 12582928 | tf_op jit(solution)/shard_map/all_gather | solution.py:414
  148.8 6.1 reshape.400
  154.9 16.8 %project_conv.1 = (f32[512,3072]{1,0:T(8,128)}, bf16[512,3072]{1,0:T(8,128)(2,1)}, bf16[512,3072]{1,0:T(8,128)(2,1)}) custom-call(bf16[512,1536]{1,0:T(8,128)(2,1)} %get-tuple-element.67.h_ref, bf16[32,64,3072]{2,1,0:T(8,128)(2,1)} %bitcast.235, f32[6,512,128]{2,1,0:T(8,128)} %broadcast_in_dim.200.masks_ref, f32[2,4,3072]{2,1,0:T(4,128)} %reshape.424.w_ref, ...), custom_call_target="tpu_custom_call" | custom-call | tf_op jit(solution)/shard_map/project_conv/pallas_call | solution.py:493
  184.1 7.5 fusion.2.delta_ref
  195.0 30.1 %scan_ahead_f.1 = (f32[1,512,3072]{2,1,0:T(8,128)}, f32[1,32,16,3072]{3,2,1,0:T(8,128)}) custom-call(f32[1,512,3072]{2,1,0:T(8,128)} %fusion.2.delta_ref, bf16[1,512,3072]{2,1,0:T(8,128)(2,1)} %bitcast.232, f32[1,512,128]{2,1,0:T(8,128)} %broadcast_in_dim.203.sb_ref, f32[1,512,16,128]{3,2,1,0:T(8,128)} %broadcast_in_dim.204.bx_ref, ...), custom_call_target="tpu_custom_call" | custom-call | tf_op jit(solution)/shard_map/scan_ahead_f/pallas_call | solution.py:505
  225.2 6.2 fusion.3.delta_ref
  234.9 31.2 %scan_ahead_b.1 = (f32[1,512,3072]{2,1,0:T(8,128)}, f32[1,32,16,3072]{3,2,1,0:T(8,128)}) custom-call(f32[1,512,3072]{2,1,0:T(8,128)} %fusion.3.delta_ref, bf16[1,512,3072]{2,1,0:T(8,128)(2,1)} %bitcast.230, f32[1,512,128]{2,1,0:T(8,128)} %broadcast_in_dim.207.sb_ref, f32[1,512,16,128]{3,2,1,0:T(8,128)} %broadcast_in_dim.208.bx_ref, ...), custom_call_target="tpu_custom_call" | custom-call | tf_op jit(solution)/shard_map/scan_ahead_b/pallas_call | solution.py:505
  266.1 20.5 %gate.1 = (bf16[512,3072]{1,0:T(8,128)(2,1)}, f32[512,3072]{1,0:T(8,128)}, f32[512,3072]{1,0:T(8,128)}) custom-call(bf16[512,1536]{1,0:T(8,128)(2,1)} %get-tuple-element.67.h_ref, bf16[1536,3072]{1,0:T(8,128)(2,1)} %all-gather.6.cloned.1.call-done.wz_ref, f32[512,3072]{1,0:T(8,128)} %bitcast.250, f32[512,3072]{1,0:T(8,128)} %bitcast.251), custom_call_target="tpu_custom_call" | custom-call | tf_op jit(solution)/shard_map/gate/pallas_call | solution.py:508
  286.6 9.7 %convolution_convert_fusion.2 = bf16[3072,1536]{1,0:T(8,128)(2,1)} fusion(bf16[512,3072]{1,0:T(8,128)(2,1)} %get-tuple-element.75, bf16[512,1536]{1,0:T(8,128)(2,1)S(1)} %copy-done.10), kind=kOutput, calls=%fused_computation.4 | convolution fusion | flops 4836556800 | bytes 14155776 | tf_op jit(solution)/shard_map/dot_general | solution.py:405
  299.5 16.5 %gate_back.1 = (f32[512,3072]{1,0:T(8,128)}, bf16[512,3072]{1,0:T(8,128)(2,1)}) custom-call(bf16[512,1536]{1,0:T(8,128)(2,1)} %get-tuple-element.78.g_ref, bf16[3072,1536]{1,0:T(8,128)(2,1)} %all-gather.8.cloned.1.call-done.wo_ref, f32[512,3072]{1,0:T(8,128)} %get-tuple-element.79.silu_ref, f32[512,3072]{1,0:T(8,128)} %get-tuple-element.80.slope_ref), custom_call_target="tpu_custom_call" | custom-call | tf_op jit(solution)/shard_map/gate_back/pallas_call | solution.py:511
  316.0 9.3 %convolution_convert_fusion.1 = bf16[1536,3072]{1,0:T(8,128)(2,1)} fusion(bf16[512,1536]{1,0:T(8,128)(2,1)S(1)} %copy-done.6, bf16[512,3072]{1,0:T(8,128)(2,1)} %get-tuple-element.83.dz_ref), kind=kOutput, calls=%fused_computation.3 | convolution fusion | flops 4836556800 | bytes 14155776 | tf_op jit(solution)/shard_map/dot_general | solution.py:405
  334.0 71.7 %scan_back_f.1 = (f32[1,512,3072]{2,1,0:T(8,128)}, bf16[1,512,3072]{2,1,0:T(8,128)(2,1)}, f32[1,512,128]{2,1,0:T(8,128)}, f32[1,512,128]{2,1,0:T(8,128)}, f32[16...) custom-call(f32[1,512,3072]{2,1,0:T(8,128)} %fusion.2.delta_ref, bf16[1,512,3072]{2,1,0:T(8,128)(2,1)} %bitcast.233, ...), custom_call_target="tpu_custom_call" | custom-call | tf_op jit(solution)/shard_map/scan_back_f/pallas_call | solution.py:552
  413.2 4.8 copy.136
  437.5 70.2 %scan_back_b.1 = (f32[1,512,3072]{2,1,0:T(8,128)}, bf16[1,512,3072]{2,1,0:T(8,128)(2,1)}, f32[1,512,128]{2,1,0:T(8,128)}, f32[1,512,128]{2,1,0:T(8,128)}, f32[16...) custom-call(f32[1,512,3072]{2,1,0:T(8,128)} %fusion.3.delta_ref, bf16[1,512,3072]{2,1,0:T(8,128)(2,1)} %bitcast.231, ...), custom_call_target="tpu_custom_call" | custom-call | tf_op jit(solution)/shard_map/scan_back_b/pallas_call | solution.py:552
  518.8 6.5 bitcast_add_fusion.1.du0_ref
  544.4 6.5 bitcast_add_fusion.du1_ref
  554.5 5.5 reshape.406
  560.0 22.7 %conv_back.1 = (bf16[512,3072]{1,0:T(8,128)(2,1)}, f32[2,4,3072]{2,1,0:T(4,128)}, f32[2,3072]{1,0:T(2,128)}) custom-call(f32[512,3072]{1,0:T(8,128)} %get-tuple-element.77.x_ref, f32[512,3072]{1,0:T(8,128)} %bitcast_add_fusion.1.du0_ref, f32[512,3072]{1,0:T(8,128)} %bitcast_add_fusion.du1_ref, f32[6,512,128]{2,1,0:T(8,128)} %broadcast_in_dim.200.masks_ref, ...), custom_call_target="tpu_custom_call" | custom-call | tf_op jit(solution)/shard_map/conv_back/pallas_call | solution.py:574
  582.8 9.4 %convolution_convert_fusion = bf16[1536,3072]{1,0:T(8,128)(2,1)} fusion(bf16[512,1536]{1,0:T(8,128)(2,1)S(1)} %copy-done.6, bf16[512,3072]{1,0:T(8,128)(2,1)} %get-tuple-element.110.dx_ref), kind=kOutput, calls=%fused_computation.2 | convolution fusion | flops 4836556800 | bytes 14155776 | tf_op jit(solution)/shard_map/dot_general | solution.py:405
  592.1 16.0 %reduce-scatter.10.cloned.1.call-done = bf16[160,1536]{1,0:T(8,128)(2,1)} async-done(((bf16[1280,1536]{1,0:T(8,128)(2,1)}), bf16[160,1536]{1,0:T(8,128)(2,1)}) %reduce-scatter.10.cloned.1.call-update) | async-done | bytes 491536 | tf_op jit(solution)/shard_map/reduce_scatter | solution.py:514
  608.2 17.1 %back_project.1 = f32[512,1536]{1,0:T(8,128)} custom-call(bf16[512,3072]{1,0:T(8,128)(2,1)} %get-tuple-element.110.dx_ref, bf16[512,3072]{1,0:T(8,128)(2,1)} %get-tuple-element.83.dz_ref, bf16[32,64,3072]{2,1,0:T(8,128)(2,1)} %bitcast.236, bf16[1536,3072]{1,0:T(8,128)(2,1)} %all-gather.6.cloned.1.call-done.wz_ref), custom_call_target="tpu_custom_call" | custom-call | tf_op jit(solution)/shard_map/back_project/pallas_call | solution.py:581
  625.5 15.7 %select_reduce_fusion.3 = (bf16[1536]{0:T(1024)(128)(2,1)S(1)}, bf16[1536]{0:T(1024)(128)(2,1)S(1)}, f32[512]{0:T(512)}, f32[512]{0:T(512)}, bf16[1536]{0:T(1024...) fusion(f32[512,1536]{1,0:T(8,128)} %back_project.1, ...), kind=kOutput, calls=%fused_computation.44 | convolution fusion | flops 4853848064 | bytes 20498944 | tf_op jit(solution)/shard_map/dot_general | solution.py:405
  642.4 4.9 all-to-all-start.2
  650.6 12.2 %all-to-all-done.2 = bf16[32,2,4608]{2,1,0:T(2,128)(2,1)S(1)} async-done(((bf16[32,2,4608]{2,1,0:T(2,128)(2,1)}), bf16[32,2,4608]{2,1,0:T(2,128)(2,1)S(1)}, u32[]{:S(2)}, u32[]{:S(2)}) %all-to-all-start.2) | async-done | bytes 589856 | tf_op jit(solution)/shard_map/all_to_all | solution.py:410
  668.1 6.6 all-to-all-done.4
  678.0 6.5 all-to-all-done.3
  684.6 11.2 %reduce-scatter.12.cloned.1.call-done = bf16[192,3072]{1,0:T(8,128)(2,1)} async-done(((bf16[1536,3072]{1,0:T(8,128)(2,1)}), bf16[192,3072]{1,0:T(8,128)(2,1)}) %reduce-scatter.12.cloned.1.call-update) | async-done | bytes 1179664 | tf_op jit(solution)/shard_map/reduce_scatter | solution.py:514
  712.5 44.8 %reduce-scatter.14.cloned.1.call-done = bf16[232,1536]{1,0:T(8,128)(2,1)} async-done(((bf16[928,1536]{1,0:T(8,128)(2,1)}), bf16[232,1536]{1,0:T(8,128)(2,1)}) %reduce-scatter.14.cloned.1.call-update) | async-done | bytes 712720 | tf_op jit(solution)/shard_map/reduce_scatter | solution.py:515
  (337 shorter events, 161.1 us)
Async XLA Ops:
  7.2 36.9 %copy-start = (bf16[48,4608]{1,0:T(8,128)(2,1)S(1)}, bf16[48,4608]{1,0:T(8,128)(2,1)}, u32[]{:S(2)}) copy-start(bf16[48,4608]{1,0:T(8,128)(2,1)} %param.28) | copy-start | bytes 1327108
  7.3 126.5 %all-gather.4.cloned.1.call-start = ((), (), s32[]{:S(2)}) async-start(), calls=%async_computation.10 | async-start | bytes 12976128 | tf_op jit(solution)/shard_map/all_gather | solution.py:414
  13.6 28.5 %all-to-all-start = ((bf16[32,64,128]{2,1,0:T(8,128)(2,1)}), bf16[32,64,128]{2,1,0:T(8,128)(2,1)S(1)}, u32[]{:S(2)}, u32[]{:S(2)}) async-start(bf16[32,64,128]{2,1,0:T(8,128)(2,1)} %broadcast_in_dim.193), calls=%async_computation | async-start | bytes 1048576 | tf_op jit(solution)/shard_map/all_to_all | solution.py:410
  46.2 46.8 %all-to-all-start.1 = ((f32[32,2,4608]{2,1,0:T(2,128)}), f32[32,2,4608]{2,1,0:T(2,128)S(1)}, u32[]{:S(2)}, u32[]{:S(2)}) async-start(f32[32,2,4608]{2,1,0:T(2,128)} %reshape.397), calls=%async_computation.1 | async-start | bytes 2359296 | tf_op jit(solution)/shard_map/all_to_all | solution.py:463
  51.5 214.5 %all-gather.6.cloned.1.call-start = ((), (), s32[]{:S(2)}) async-start(), calls=%async_computation.11 | async-start | bytes 9732096 | tf_op jit(solution)/shard_map/all_gather | solution.py:414
  52.2 45.5 %copy-start.54 = (pred[512]{0:T(512)(128)(4,1)}, pred[512]{0:T(512)(128)(4,1)S(1)}, u32[]{:S(2)}) copy-start(pred[512]{0:T(512)(128)(4,1)S(1)} %get-tuple-element.196) | copy-start | bytes 1540
  52.7 45.0 %copy-start.43 = (f32[512]{0:T(512)}, f32[512]{0:T(512)S(1)}, u32[]{:S(2)}) copy-start(f32[512]{0:T(512)S(1)} %broadcast_multiply_fusion.5) | copy-start | bytes 6148
  53.3 44.5 %copy-start.49 = (f32[512]{0:T(512)}, f32[512]{0:T(512)S(1)}, u32[]{:S(2)}) copy-start(f32[512]{0:T(512)S(1)} %add_rsqrt_fusion) | copy-start | bytes 6148
  97.8 42.5 %copy-start.17 = (f32[32,3072]{1,0:T(8,128)S(1)}, f32[32,3072]{1,0:T(8,128)}, u32[]{:S(2)}) copy-start(f32[32,3072]{1,0:T(8,128)} %get-tuple-element.218) | copy-start | bytes 1179652
  135.4 164.1 %all-gather.8.cloned.1.call-start = ((), (), s32[]{:S(2)}) async-start(), calls=%async_computation.12 | async-start | bytes 9732096 | tf_op jit(solution)/shard_map/all_gather | solution.py:414
  136.1 389.2 %reduce-scatter.6.cloned.1.call-start = ((), (), s32[]{:S(2)}) async-start(), calls=%async_computation.13 | async-start | bytes 10616832 | tf_op jit(solution)/shard_map/reduce_scatter | solution.py:514
  174.0 51.1 %copy-start.11 = (bf16[1,1,32,96,128]{4,3,1,0,2:T(8,128)(2,1)}, bf16[1,1,32,96,128]{4,3,1,0,2:T(8,128)(2,1)S(1)}, u32[]{:S(2)}) copy-start(bf16[1,1,32,96,128]{4,3,1,0,2:T(8,128)(2,1)S(1)} %get-tuple-element.200) | copy-start | bytes 2359300
  195.0 30.2 %copy-start.19 = (f32[512,128]{0,1:T(8,128)S(1)}, f32[512,128]{0,1:T(8,128)}, u32[]{:S(2)}) copy-start(f32[512,128]{0,1:T(8,128)} %copy-done.18) | copy-start | bytes 786436
  266.1 20.5 %copy-start.10 = (bf16[512,1536]{1,0:T(8,128)(2,1)S(1)}, bf16[512,1536]{1,0:T(8,128)(2,1)}, u32[]{:S(2)}) copy-start(bf16[512,1536]{1,0:T(8,128)(2,1)} %get-tuple-element.78.g_ref) | copy-start | bytes 4718596
  325.4 234.6 %reduce-scatter.8.cloned.1.call-start = ((), (), s32[]{:S(2)}) async-start(), calls=%async_computation.14 | async-start | bytes 9732096 | tf_op jit(solution)/shard_map/reduce_scatter | solution.py:519
  326.0 282.1 %reduce-scatter.10.cloned.1.call-start = ((), (), s32[]{:S(2)}) async-start(), calls=%async_computation.15 | async-start | bytes 4423680 | tf_op jit(solution)/shard_map/reduce_scatter | solution.py:514
  326.2 79.5 %copy-start.52 = (pred[128]{0:T(512)(128)(4,1)}, pred[128]{0:T(512)(128)(4,1)S(1)}, u32[]{:S(2)}) copy-start(pred[128]{0:T(512)(128)(4,1)S(1)} %get-tuple-element.244) | copy-start | bytes 388
  326.2 79.5 %copy-start.53 = (pred[128]{0:T(512)(128)(4,1)}, pred[128]{0:T(512)(128)(4,1)S(1)}, u32[]{:S(2)}) copy-start(pred[128]{0:T(512)(128)(4,1)S(1)} %get-tuple-element.245) | copy-start | bytes 388
  560.0 135.8 %reduce-scatter.12.cloned.1.call-start = ((), (), s32[]{:S(2)}) async-start(), calls=%async_computation.16 | async-start | bytes 10616832 | tf_op jit(solution)/shard_map/reduce_scatter | solution.py:514
  608.2 17.2 %copy-start.5 = (bf16[1,512,1536]{2,1,0:T(8,128)(2,1)S(1)}, bf16[1,512,1536]{2,1,0:T(8,128)(2,1)}, u32[]{:S(2)}) copy-start(bf16[1,512,1536]{2,1,0:T(8,128)(2,1)} %param.15) | copy-start | bytes 4718596
  608.2 17.2 %copy-start.34 = (f32[1536]{0:T(1024)S(1)}, f32[1536]{0:T(1024)}, u32[]{:S(2)}) copy-start(f32[1536]{0:T(1024)} %copy-done.33) | copy-start | bytes 18436
  608.2 17.2 %copy-start.36 = (f32[1536]{0:T(1024)S(1)}, f32[1536]{0:T(1024)}, u32[]{:S(2)}) copy-start(f32[1536]{0:T(1024)} %copy-done.35) | copy-start | bytes 18436
  608.2 17.2 %copy-start.40 = (f32[1536]{0:T(1024)S(1)}, f32[1536]{0:T(1024)}, u32[]{:S(2)}) copy-start(f32[1536]{0:T(1024)} %copy-done.39) | copy-start | bytes 18436
  608.2 17.2 %copy-start.42 = (f32[1536]{0:T(1024)S(1)}, f32[1536]{0:T(1024)}, u32[]{:S(2)}) copy-start(f32[1536]{0:T(1024)} %copy-done.41) | copy-start | bytes 18436
  608.2 17.2 %copy-start.44 = (f32[512]{0:T(512)S(1)}, f32[512]{0:T(512)}, u32[]{:S(2)}) copy-start(f32[512]{0:T(512)} %copy-done.43) | copy-start | bytes 6148
  608.2 17.2 %copy-start.50 = (f32[512]{0:T(512)S(1)}, f32[512]{0:T(512)}, u32[]{:S(2)}) copy-start(f32[512]{0:T(512)} %copy-done.49) | copy-start | bytes 6148
  625.4 21.8 %copy-start.45 = (f32[2,3072]{1,0:T(2,128)S(1)}, f32[2,3072]{1,0:T(2,128)}, u32[]{:S(2)}) copy-start(f32[2,3072]{1,0:T(2,128)} %get-tuple-element.114) | copy-start | bytes 73732
  625.5 22.0 %copy-start.32 = (f32[2,4,3072]{2,1,0:T(4,128)S(1)}, f32[2,4,3072]{2,1,0:T(4,128)}, u32[]{:S(2)}) copy-start(f32[2,4,3072]{2,1,0:T(4,128)} %get-tuple-element.113) | copy-start | bytes 294916
  642.4 20.4 %all-to-all-start.2 = ((bf16[32,2,4608]{2,1,0:T(2,128)(2,1)}), bf16[32,2,4608]{2,1,0:T(2,128)(2,1)S(1)}, u32[]{:S(2)}, u32[]{:S(2)}) async-start(bf16[32,2,4608]{2,1,0:T(2,128)(2,1)} %broadcast_in_dim.218), calls=%async_computation.6 | async-start | bytes 1179648 | tf_op jit(solution)/shard_map/all_to_all | solution.py:410
  662.8 11.9 %all-to-all-start.4 = ((bf16[32,8,128]{2,1,0:T(8,128)(2,1)}), bf16[32,8,128]{2,1,0:T(8,128)(2,1)S(1)}, u32[]{:S(2)}, u32[]{:S(2)}) async-start(bf16[32,8,128]{2,1,0:T(8,128)(2,1)} %bitcast.92), calls=%async_computation.8 | async-start | bytes 131072 | tf_op jit(solution)/shard_map/all_to_all | solution.py:536
  674.7 9.9 %all-to-all-start.3 = ((f32[32,2,48]{2,1,0:T(2,128)}), f32[32,2,48]{2,1,0:T(2,128)S(1)}, u32[]{:S(2)}, u32[]{:S(2)}) async-start(f32[32,2,48]{2,1,0:T(2,128)} %copy.142), calls=%async_computation.7 | async-start | bytes 65536 | tf_op jit(solution)/shard_map/all_to_all | solution.py:596
  677.3 80.0 %reduce-scatter.14.cloned.1.call-start = ((), (), s32[]{:S(2)}) async-start(), calls=%async_computation.17 | async-start | bytes 3563520 | tf_op jit(solution)/shard_map/reduce_scatter | solution.py:515
  (42 other events, 211.4 us)
Sparse Core Ops, SparseCore 0:
  12.0 121.6 all-gather.3
  136.6 79.8 all-gather.5
  219.3 80.1 all-gather.7
  325.5 75.3 reduce-scatter.5
  406.6 136.2 reduce-scatter.7
  560.1 47.9 reduce-scatter.9
  611.6 84.1 reduce-scatter.11
  701.7 55.5 reduce-scatter.13

commit v6 on v5

--- a/solution.py
+++ b/solution.py
@@ -459,8 +459,8 @@
     modb = parts[6].reshape(-1).astype(f32)
 
     act_own = lax.dynamic_slice(act_all, (0, me * own_model), (owners * 2, own_model))
-    partial = mm(act_own, mod_weight, ((1,), (0,))).reshape(owners, 2, -1)
-    mods = jnp.sum(lax.all_to_all(partial, AXES, 0, 0, tiled=True), axis=0) + modb
+    partial = mm(act_own, mod_weight, ((1,), (0,))).astype(bf16).reshape(owners, 2, -1)
+    mods = jnp.sum(lax.all_to_all(partial, AXES, 0, 0, tiled=True).astype(f32), axis=0) + modb
     flags = item_flags[0]
     ids = jnp.cumsum(flags, dtype=jnp.int32) - 1
     second = (ids == 1)[:, None]
@@ -560,16 +560,15 @@
         g_dt = mm(dr, dt_low, ((0,), (0,)))
         g_xp = mm(u, d_proj, ((0,), (0,)))
         flat, shapes = send((g_xp, g_dt, jnp.sum(gb, axis=0), ga.T, jnp.sum(gs, axis=0)), (0,) * 5)
-        d_us.append(du[0] + mm(d_proj, w_xp[d], ((1,), (1,))))
+        d_us.append((du[0], d_proj))
         if d == 0:
             carried, flat = lax.optimization_barrier((carried, flat))
-        else:
-            d_us[1], flat = lax.optimization_barrier((d_us[1], flat))
         sent.append((flat, shapes))
     packed = jnp.concatenate([s[0].reshape(owners, -1) for s in sent], axis=1)
     span = sent[0][0].size // owners
     packed = jnp.pad(packed, ((0, 0), (0, -packed.shape[1] % (8 * model)))).reshape(-1, model)
-    d_us[0], d_us[1], grad_out_w, packed = lax.optimization_barrier((d_us[0], d_us[1], grad_out_w, packed))
+    d_us, grad_out_w, packed = lax.optimization_barrier((d_us, grad_out_w, packed))
+    d_us = [du + mm(d_proj, w_xp[d], ((1,), (1,))) for d, (du, d_proj) in enumerate(d_us)]
     packed = over_dp(packed)
     d_xs, g_cw, g_cb = conv_back_call(length, inner)(xs, d_us[0], d_us[1], masks, conv_w, conv_b)
     grad_in_x = mm(hidden, d_xs, ((0,), (0,))).astype(bf16)

time: 780 us -> 760 us (0.974)
  waiting for transfers between devices: 198 us -> 182 us
    all_to_all x1, waiting for transfers between devices: 38.7 us -> 26.2 us  [body(): lax.all_to_all(partial, AXES, 0, 0, tiled=True).astype(f32)]
    reduce_scatter x3, waiting for transfers between devices: 27.2 us -> 15.8 us  [body(): lax.psum_scatter(v, 'dp', scatter_dimension=0, tiled=True)]
    all_gather x3, waiting for transfers between devices: 39.1 us -> 48.5 us  [gather0(): return lax.all_gather(v, AXES, axis=0, tiled=True)]
    unnamed x138 -> x115, local copies, waits for them, and re-layouts: 20.7 us -> 15.9 us
  transfers between devices with their start and end apart: 13 -> 13, of which waited for: 10 -> 10; matrix products, arithmetic and copies ran while one was open for 26% -> 27% of each run, Pallas kernels for 36% -> 37%
where the time goes in v6:
time: 760 us; the launch traced here: 752 us
  Pallas kernels  296 us (39%)
  waiting for transfers between devices  182 us (24%)
  local copies, waits for them, and re-layouts  108 us (14%)
  matrix products  96.1 us (13%)
  other arithmetic  29.1 us (4%)
  starting transfers between devices  25.1 us (3%)
  between operations  15.7 us (2%)
    pallas_call x2, Pallas kernels, body(): calls[d][1]  142 us
    dot_general x19, matrix products, mm(): return lax.dot_general(a, b, (dims, ((), ())), preferred_element_type=f32)  96.1 us
    pallas_call x2, Pallas kernels, body(): calls[d][0]  61.2 us
    all_gather x3, waiting for transfers between devices, gather0(): return lax.all_gather(v, AXES, axis=0, tiled=True)  48.5 us
    reduce_scatter x1, waiting for transfers between devices, body(): lax.psum_scatter(v.reshape(-1, model), 'fsdp', scatter_dimension=0, tiled...  44.8 us
    all_to_all x2, waiting for transfers between devices, to_all(): lax.all_to_all(jnp.broadcast_to(v[None], (owners,) + v.shape), AXES, 0, 0...  32.1 us
    all_to_all x1, waiting for transfers between devices, body(): lax.all_to_all(partial, AXES, 0, 0, tiled=True).astype(f32)  26.2 us
    pallas_call x1, Pallas kernels, body(): conv_back_call(length, inner)(xs, d_us[0], d_us[1], masks, conv_w, conv_b)  22.7 us
  transfers between devices with their start and end apart: 13, of which 10 were waited for; matrix products, arithmetic and copies ran while one was open for 27% of the time, Pallas kernels for 37%

profile of v6, /device:TPU:0, one launch (start us, length us, event | category | flops | bytes accessed | tf_op | source)
XLA Modules:
  0.0 752.1 jit_solution(13903877795147564039)
XLA Ops:
  13.6 7.3 all-to-all-start
  22.1 19.9 %all-to-all-done = bf16[32,64,128]{2,1,0:T(8,128)(2,1)S(1)} async-done(((bf16[32,64,128]{2,1,0:T(8,128)(2,1)}), bf16[32,64,128]{2,1,0:T(8,128)(2,1)S(1)}, u32[]{:S(2)}, u32[]{:S(2)}) %all-to-all-start) | async-done | bytes 524320 | tf_op jit(solution)/shard_map/all_to_all | solution.py:410
  45.2 5.5 all-to-all-start.1
  53.8 26.2 %all-to-all-done.1 = bf16[32,2,4608]{2,1,0:T(2,128)(2,1)S(1)} async-done(((bf16[32,2,4608]{2,1,0:T(2,128)(2,1)}), bf16[32,2,4608]{2,1,0:T(2,128)(2,1)S(1)}, u32[]{:S(2)}, u32[]{:S(2)}) %all-to-all-start.1) | async-done | bytes 589856 | tf_op jit(solution)/shard_map/all_to_all | solution.py:463
  85.1 42.1 %all-gather.4.cloned.1.call-done = bf16[2048,3072]{1,0:T(8,128)(2,1)} async-done(((bf16[64,3072]{1,0:T(8,128)(2,1)}), bf16[2048,3072]{1,0:T(8,128)(2,1)}) %all-gather.4.cloned.1.call-update) | async-done | bytes 12582928 | tf_op jit(solution)/shard_map/all_gather | solution.py:414
  140.8 6.0 reshape.394
  146.8 16.9 %project_conv.1 = (f32[512,3072]{1,0:T(8,128)}, bf16[512,3072]{1,0:T(8,128)(2,1)}, bf16[512,3072]{1,0:T(8,128)(2,1)}) custom-call(bf16[512,1536]{1,0:T(8,128)(2,1)} %get-tuple-element.67.h_ref, bf16[32,64,3072]{2,1,0:T(8,128)(2,1)} %bitcast.226, f32[6,512,128]{2,1,0:T(8,128)} %broadcast_in_dim.200.masks_ref, f32[2,4,3072]{2,1,0:T(4,128)} %reshape.416.w_ref, ...), custom_call_target="tpu_custom_call" | custom-call | tf_op jit(solution)/shard_map/project_conv/pallas_call | solution.py:493
  176.0 7.2 fusion.1.delta_ref
  186.7 30.1 %scan_ahead_f.1 = (f32[1,512,3072]{2,1,0:T(8,128)}, f32[1,32,16,3072]{3,2,1,0:T(8,128)}) custom-call(f32[1,512,3072]{2,1,0:T(8,128)} %fusion.1.delta_ref, bf16[1,512,3072]{2,1,0:T(8,128)(2,1)} %bitcast.223, f32[1,512,128]{2,1,0:T(8,128)} %broadcast_in_dim.203.sb_ref, f32[1,512,16,128]{3,2,1,0:T(8,128)} %broadcast_in_dim.204.bx_ref, ...), custom_call_target="tpu_custom_call" | custom-call | tf_op jit(solution)/shard_map/scan_ahead_f/pallas_call | solution.py:505
  216.8 6.3 fusion.2.delta_ref
  226.5 31.1 %scan_ahead_b.1 = (f32[1,512,3072]{2,1,0:T(8,128)}, f32[1,32,16,3072]{3,2,1,0:T(8,128)}) custom-call(f32[1,512,3072]{2,1,0:T(8,128)} %fusion.2.delta_ref, bf16[1,512,3072]{2,1,0:T(8,128)(2,1)} %bitcast.221, f32[1,512,128]{2,1,0:T(8,128)} %broadcast_in_dim.207.sb_ref, f32[1,512,16,128]{3,2,1,0:T(8,128)} %broadcast_in_dim.208.bx_ref, ...), custom_call_target="tpu_custom_call" | custom-call | tf_op jit(solution)/shard_map/scan_ahead_b/pallas_call | solution.py:505
  257.6 19.3 %gate.1 = (bf16[512,3072]{1,0:T(8,128)(2,1)}, f32[512,3072]{1,0:T(8,128)}, f32[512,3072]{1,0:T(8,128)}) custom-call(bf16[512,1536]{1,0:T(8,128)(2,1)} %get-tuple-element.67.h_ref, bf16[1536,3072]{1,0:T(8,128)(2,1)} %all-gather.6.cloned.1.call-done.wz_ref, f32[512,3072]{1,0:T(8,128)} %bitcast.242, f32[512,3072]{1,0:T(8,128)} %bitcast.243), custom_call_target="tpu_custom_call" | custom-call | tf_op jit(solution)/shard_map/gate/pallas_call | solution.py:508
  277.0 9.6 %convolution_convert_fusion.2 = bf16[3072,1536]{1,0:T(8,128)(2,1)} fusion(bf16[512,3072]{1,0:T(8,128)(2,1)} %get-tuple-element.75, bf16[512,1536]{1,0:T(8,128)(2,1)S(1)} %copy-done.8), kind=kOutput, calls=%fused_computation.4 | convolution fusion | flops 4836556800 | bytes 14155776 | tf_op jit(solution)/shard_map/dot_general | solution.py:405
  286.6 6.5 all-gather.8.cloned.1.call-done.wo_ref
  293.0 16.6 %gate_back.1 = (f32[512,3072]{1,0:T(8,128)}, bf16[512,3072]{1,0:T(8,128)(2,1)}) custom-call(bf16[512,1536]{1,0:T(8,128)(2,1)} %get-tuple-element.78.g_ref, bf16[3072,1536]{1,0:T(8,128)(2,1)} %all-gather.8.cloned.1.call-done.wo_ref, f32[512,3072]{1,0:T(8,128)} %get-tuple-element.79.silu_ref, f32[512,3072]{1,0:T(8,128)} %get-tuple-element.80.slope_ref), custom_call_target="tpu_custom_call" | custom-call | tf_op jit(solution)/shard_map/gate_back/pallas_call | solution.py:511
  309.7 9.4 %convolution_convert_fusion.1 = bf16[1536,3072]{1,0:T(8,128)(2,1)} fusion(bf16[512,1536]{1,0:T(8,128)(2,1)S(1)} %copy-done.6, bf16[512,3072]{1,0:T(8,128)(2,1)} %get-tuple-element.83.dz_ref), kind=kOutput, calls=%fused_computation.3 | convolution fusion | flops 4836556800 | bytes 14155776 | tf_op jit(solution)/shard_map/dot_general | solution.py:405
  327.7 71.8 %scan_back_f.1 = (f32[1,512,3072]{2,1,0:T(8,128)}, bf16[1,512,3072]{2,1,0:T(8,128)(2,1)}, f32[1,512,128]{2,1,0:T(8,128)}, f32[1,512,128]{2,1,0:T(8,128)}, f32[16...) custom-call(f32[1,512,3072]{2,1,0:T(8,128)} %fusion.1.delta_ref, bf16[1,512,3072]{2,1,0:T(8,128)(2,1)} %bitcast.224, ...), custom_call_target="tpu_custom_call" | custom-call | tf_op jit(solution)/shard_map/scan_back_f/pallas_call | solution.py:552
  406.9 4.8 copy.136
  431.2 70.2 %scan_back_b.1 = (f32[1,512,3072]{2,1,0:T(8,128)}, bf16[1,512,3072]{2,1,0:T(8,128)(2,1)}, f32[1,512,128]{2,1,0:T(8,128)}, f32[1,512,128]{2,1,0:T(8,128)}, f32[16...) custom-call(f32[1,512,3072]{2,1,0:T(8,128)} %fusion.2.delta_ref, bf16[1,512,3072]{2,1,0:T(8,128)(2,1)} %bitcast.222, ...), custom_call_target="tpu_custom_call" | custom-call | tf_op jit(solution)/shard_map/scan_back_b/pallas_call | solution.py:552
  532.9 5.4 reshape.398
  538.4 6.6 convolution_add_fusion.1.du0_ref
  545.0 7.0 convolution_add_fusion.du1_ref
  552.0 22.7 %conv_back.1 = (bf16[512,3072]{1,0:T(8,128)(2,1)}, f32[2,4,3072]{2,1,0:T(4,128)}, f32[2,3072]{1,0:T(2,128)}) custom-call(f32[512,3072]{1,0:T(8,128)} %get-tuple-element.77.x_ref, f32[512,3072]{1,0:T(8,128)} %convolution_add_fusion.1.du0_ref, f32[512,3072]{1,0:T(8,128)} %convolution_add_fusion.du1_ref, f32[6,512,128]{2,1,0:T(8,128)} %broadcast_in_dim.200.masks_ref, ...), custom_call_target="tpu_custom_call" | custom-call | tf_op jit(solution)/shard_map/conv_back/pallas_call | solution.py:573
  574.8 9.4 %convolution_convert_fusion = bf16[1536,3072]{1,0:T(8,128)(2,1)} fusion(bf16[512,1536]{1,0:T(8,128)(2,1)S(1)} %copy-done.6, bf16[512,3072]{1,0:T(8,128)(2,1)} %get-tuple-element.110.dx_ref), kind=kOutput, calls=%fused_computation.2 | convolution fusion | flops 4836556800 | bytes 14155776 | tf_op jit(solution)/shard_map/dot_general | solution.py:405
  588.9 17.1 %back_project.1 = f32[512,1536]{1,0:T(8,128)} custom-call(bf16[512,3072]{1,0:T(8,128)(2,1)} %get-tuple-element.110.dx_ref, bf16[512,3072]{1,0:T(8,128)(2,1)} %get-tuple-element.83.dz_ref, bf16[32,64,3072]{2,1,0:T(8,128)(2,1)} %bitcast.227, bf16[1536,3072]{1,0:T(8,128)(2,1)} %all-gather.6.cloned.1.call-done.wz_ref), custom_call_target="tpu_custom_call" | custom-call | tf_op jit(solution)/shard_map/back_project/pallas_call | solution.py:580
  606.1 15.7 %select_reduce_fusion.3 = (bf16[1536]{0:T(1024)(128)(2,1)S(1)}, bf16[1536]{0:T(1024)(128)(2,1)S(1)}, f32[512]{0:T(512)}, f32[512]{0:T(512)}, bf16[1536]{0:T(1024...) fusion(f32[512,1536]{1,0:T(8,128)} %back_project.1, ...), kind=kOutput, calls=%fused_computation.44 | convolution fusion | flops 4853848064 | bytes 20498944 | tf_op jit(solution)/shard_map/dot_general | solution.py:405
  623.0 4.9 all-to-all-start.2
  631.2 12.2 %all-to-all-done.2 = bf16[32,2,4608]{2,1,0:T(2,128)(2,1)S(1)} async-done(((bf16[32,2,4608]{2,1,0:T(2,128)(2,1)}), bf16[32,2,4608]{2,1,0:T(2,128)(2,1)S(1)}, u32[]{:S(2)}, u32[]{:S(2)}) %all-to-all-start.2) | async-done | bytes 589856 | tf_op jit(solution)/shard_map/all_to_all | solution.py:410
  648.7 6.6 all-to-all-done.4
  658.6 6.5 all-to-all-done.3
  665.2 11.2 %reduce-scatter.12.cloned.1.call-done = bf16[192,3072]{1,0:T(8,128)(2,1)} async-done(((bf16[1536,3072]{1,0:T(8,128)(2,1)}), bf16[192,3072]{1,0:T(8,128)(2,1)}) %reduce-scatter.12.cloned.1.call-update) | async-done | bytes 1179664 | tf_op jit(solution)/shard_map/reduce_scatter | solution.py:514
  693.0 44.8 %reduce-scatter.14.cloned.1.call-done = bf16[232,1536]{1,0:T(8,128)(2,1)} async-done(((bf16[928,1536]{1,0:T(8,128)(2,1)}), bf16[232,1536]{1,0:T(8,128)(2,1)}) %reduce-scatter.14.cloned.1.call-update) | async-done | bytes 712720 | tf_op jit(solution)/shard_map/reduce_scatter | solution.py:515
  (315 shorter events, 159.7 us)
Async XLA Ops:
  7.2 35.9 %copy-start = (bf16[48,4608]{1,0:T(8,128)(2,1)S(1)}, bf16[48,4608]{1,0:T(8,128)(2,1)}, u32[]{:S(2)}) copy-start(bf16[48,4608]{1,0:T(8,128)(2,1)} %param.28) | copy-start | bytes 1327108
  7.3 13.7 %copy-start.41 = (s32[1,512]{1,0:T(1,128)S(1)}, s32[1,512]{1,0:T(1,128)}, u32[]{:S(2)}) copy-start(s32[1,512]{1,0:T(1,128)} %param.17) | copy-start | bytes 6148
  7.3 119.9 %all-gather.4.cloned.1.call-start = ((), (), s32[]{:S(2)}) async-start(), calls=%async_computation.10 | async-start | bytes 12976128 | tf_op jit(solution)/shard_map/all_gather | solution.py:414
  13.6 28.4 %all-to-all-start = ((bf16[32,64,128]{2,1,0:T(8,128)(2,1)}), bf16[32,64,128]{2,1,0:T(8,128)(2,1)S(1)}, u32[]{:S(2)}, u32[]{:S(2)}) async-start(bf16[32,64,128]{2,1,0:T(8,128)(2,1)} %broadcast_in_dim.193), calls=%async_computation | async-start | bytes 1048576 | tf_op jit(solution)/shard_map/all_to_all | solution.py:410
  20.9 30.6 %copy-start.4 = (bf16[1,512,1536]{2,1,0:T(8,128)(2,1)S(1)}, bf16[1,512,1536]{2,1,0:T(8,128)(2,1)}, u32[]{:S(2)}) copy-start(bf16[1,512,1536]{2,1,0:T(8,128)(2,1)} %param.15) | copy-start | bytes 4718596
  45.2 34.8 %all-to-all-start.1 = ((bf16[32,2,4608]{2,1,0:T(2,128)(2,1)}), bf16[32,2,4608]{2,1,0:T(2,128)(2,1)S(1)}, u32[]{:S(2)}, u32[]{:S(2)}) async-start(bf16[32,2,4608]{2,1,0:T(2,128)(2,1)} %reshape.391), calls=%async_computation.1 | async-start | bytes 1179648 | tf_op jit(solution)/shard_map/all_to_all | solution.py:463
  50.7 206.9 %all-gather.6.cloned.1.call-start = ((), (), s32[]{:S(2)}) async-start(), calls=%async_computation.11 | async-start | bytes 9732096 | tf_op jit(solution)/shard_map/all_gather | solution.py:414
  81.4 45.9 %copy-start.31 = (f32[6,512]{1,0:T(8,128)S(1)}, f32[6,512]{1,0:T(8,128)}, u32[]{:S(2)}) copy-start(f32[6,512]{1,0:T(8,128)} %stack.112) | copy-start | bytes 36868
  81.4 48.3 %copy-start.42 = (s32[1,512]{1,0:T(1,128)S(1)}, s32[1,512]{1,0:T(1,128)}, u32[]{:S(2)}) copy-start(s32[1,512]{1,0:T(1,128)} %param.17) | copy-start | bytes 6148
  128.9 164.1 %all-gather.8.cloned.1.call-start = ((), (), s32[]{:S(2)}) async-start(), calls=%async_computation.12 | async-start | bytes 9732096 | tf_op jit(solution)/shard_map/all_gather | solution.py:414
  129.6 381.7 %reduce-scatter.6.cloned.1.call-start = ((), (), s32[]{:S(2)}) async-start(), calls=%async_computation.13 | async-start | bytes 10616832 | tf_op jit(solution)/shard_map/reduce_scatter | solution.py:514
  166.0 50.8 %copy-start.9 = (bf16[1,1,32,96,128]{4,3,1,0,2:T(8,128)(2,1)}, bf16[1,1,32,96,128]{4,3,1,0,2:T(8,128)(2,1)S(1)}, u32[]{:S(2)}) copy-start(bf16[1,1,32,96,128]{4,3,1,0,2:T(8,128)(2,1)S(1)} %get-tuple-element.200) | copy-start | bytes 2359300
  186.7 30.1 %copy-start.15 = (f32[512,128]{0,1:T(8,128)S(1)}, f32[512,128]{0,1:T(8,128)}, u32[]{:S(2)}) copy-start(f32[512,128]{0,1:T(8,128)} %copy-done.14) | copy-start | bytes 786436
  257.6 19.3 %copy-start.8 = (bf16[512,1536]{1,0:T(8,128)(2,1)S(1)}, bf16[512,1536]{1,0:T(8,128)(2,1)}, u32[]{:S(2)}) copy-start(bf16[512,1536]{1,0:T(8,128)(2,1)} %get-tuple-element.78.g_ref) | copy-start | bytes 4718596
  293.0 16.6 %copy-start.6 = (bf16[512,1536]{1,0:T(8,128)(2,1)S(1)}, bf16[512,1536]{1,0:T(8,128)(2,1)}, u32[]{:S(2)}) copy-start(bf16[512,1536]{1,0:T(8,128)(2,1)} %get-tuple-element.67.h_ref) | copy-start | bytes 4718596
  319.1 219.3 %reduce-scatter.8.cloned.1.call-start = ((), (), s32[]{:S(2)}) async-start(), calls=%async_computation.14 | async-start | bytes 9732096 | tf_op jit(solution)/shard_map/reduce_scatter | solution.py:519
  319.7 269.1 %reduce-scatter.10.cloned.1.call-start = ((), (), s32[]{:S(2)}) async-start(), calls=%async_computation.15 | async-start | bytes 4423680 | tf_op jit(solution)/shard_map/reduce_scatter | solution.py:514
  538.4 138.0 %reduce-scatter.12.cloned.1.call-start = ((), (), s32[]{:S(2)}) async-start(), calls=%async_computation.16 | async-start | bytes 10616832 | tf_op jit(solution)/shard_map/reduce_scatter | solution.py:514
  588.8 17.2 %copy-start.5 = (bf16[1,512,1536]{2,1,0:T(8,128)(2,1)S(1)}, bf16[1,512,1536]{2,1,0:T(8,128)(2,1)}, u32[]{:S(2)}) copy-start(bf16[1,512,1536]{2,1,0:T(8,128)(2,1)} %param.15) | copy-start | bytes 4718596
  588.8 17.2 %copy-start.28 = (f32[1536]{0:T(1024)S(1)}, f32[1536]{0:T(1024)}, u32[]{:S(2)}) copy-start(f32[1536]{0:T(1024)} %copy-done.27) | copy-start | bytes 18436
  588.8 17.2 %copy-start.30 = (f32[1536]{0:T(1024)S(1)}, f32[1536]{0:T(1024)}, u32[]{:S(2)}) copy-start(f32[1536]{0:T(1024)} %copy-done.29) | copy-start | bytes 18436
  588.8 17.2 %copy-start.33 = (f32[1536]{0:T(1024)S(1)}, f32[1536]{0:T(1024)}, u32[]{:S(2)}) copy-start(f32[1536]{0:T(1024)} %copy-done.32) | copy-start | bytes 18436
  588.8 17.2 %copy-start.35 = (f32[1536]{0:T(1024)S(1)}, f32[1536]{0:T(1024)}, u32[]{:S(2)}) copy-start(f32[1536]{0:T(1024)} %copy-done.34) | copy-start | bytes 18436
  588.8 17.2 %copy-start.37 = (f32[512]{0:T(512)S(1)}, f32[512]{0:T(512)}, u32[]{:S(2)}) copy-start(f32[512]{0:T(512)} %copy-done.36) | copy-start | bytes 6148
  588.8 17.2 %copy-start.43 = (f32[512]{0:T(512)S(1)}, f32[512]{0:T(512)}, u32[]{:S(2)}) copy-start(f32[512]{0:T(512)} %add_rsqrt_fusion) | copy-start | bytes 6148
  588.8 17.2 %copy-start.45 = (pred[512]{0:T(512)(128)(4,1)S(1)}, pred[512]{0:T(512)(128)(4,1)}, u32[]{:S(2)}) copy-start(pred[512]{0:T(512)(128)(4,1)} %get-tuple-element.196) | copy-start | bytes 1540
  606.1 21.8 %copy-start.38 = (f32[2,3072]{1,0:T(2,128)S(1)}, f32[2,3072]{1,0:T(2,128)}, u32[]{:S(2)}) copy-start(f32[2,3072]{1,0:T(2,128)} %get-tuple-element.114) | copy-start | bytes 73732
  606.1 22.0 %copy-start.26 = (f32[2,4,3072]{2,1,0:T(4,128)S(1)}, f32[2,4,3072]{2,1,0:T(4,128)}, u32[]{:S(2)}) copy-start(f32[2,4,3072]{2,1,0:T(4,128)} %get-tuple-element.113) | copy-start | bytes 294916
  623.0 20.4 %all-to-all-start.2 = ((bf16[32,2,4608]{2,1,0:T(2,128)(2,1)}), bf16[32,2,4608]{2,1,0:T(2,128)(2,1)S(1)}, u32[]{:S(2)}, u32[]{:S(2)}) async-start(bf16[32,2,4608]{2,1,0:T(2,128)(2,1)} %broadcast_in_dim.218), calls=%async_computation.6 | async-start | bytes 1179648 | tf_op jit(solution)/shard_map/all_to_all | solution.py:410
  643.4 11.9 %all-to-all-start.4 = ((bf16[32,8,128]{2,1,0:T(8,128)(2,1)}), bf16[32,8,128]{2,1,0:T(8,128)(2,1)S(1)}, u32[]{:S(2)}, u32[]{:S(2)}) async-start(bf16[32,8,128]{2,1,0:T(8,128)(2,1)} %bitcast.88), calls=%async_computation.8 | async-start | bytes 131072 | tf_op jit(solution)/shard_map/all_to_all | solution.py:536
  655.3 9.9 %all-to-all-start.3 = ((f32[32,2,48]{2,1,0:T(2,128)}), f32[32,2,48]{2,1,0:T(2,128)S(1)}, u32[]{:S(2)}, u32[]{:S(2)}) async-start(f32[32,2,48]{2,1,0:T(2,128)} %copy.142), calls=%async_computation.7 | async-start | bytes 65536 | tf_op jit(solution)/shard_map/all_to_all | solution.py:595
  657.9 80.0 %reduce-scatter.14.cloned.1.call-start = ((), (), s32[]{:S(2)}) async-start(), calls=%async_computation.17 | async-start | bytes 3563520 | tf_op jit(solution)/shard_map/reduce_scatter | solution.py:515
  (32 other events, 148.6 us)
Sparse Core Ops, SparseCore 0:
  12.0 115.1 all-gather.3
  130.0 80.1 all-gather.5
  213.0 79.9 all-gather.7
  319.2 75.3 reduce-scatter.5
  400.3 136.2 reduce-scatter.7
  540.0 48.7 reduce-scatter.9
  592.2 84.0 reduce-scatter.11
  682.2 55.5 reduce-scatter.13
